TPU v7x, 32 devices: a whole 2x2x4 slice. The times are simulated.
32 devices in a mesh: dp: 16 (over z, y, x), tensor: 2 (over core).
Axes of the slice: x: 2, y: 2, z: 4, core: 2. Of those that a mesh axis runs over, the one named last changes fastest.
Arguments:
- tokens_in: bfloat16 [4096, 2048], P('dp'), may hold values from -6 to 6
- input_proj: bfloat16 [2048, 2048], P('dp'), may hold values from -0.125 to 0.125
- forget_proj: bfloat16 [2048, 2048], P('dp'), may hold values from -0.125 to 0.125
- outgate_proj: bfloat16 [2048, 2048], P('dp'), may hold values from -0.125 to 0.125
- output_proj: bfloat16 [2048, 2048], P('dp'), may hold values from -0.125 to 0.125
- glu_gate: bfloat16 [2048, 5632], P('dp', 'tensor'), may hold values from -0.125 to 0.125
- glu_up: bfloat16 [2048, 5632], P('dp', 'tensor'), may hold values from -0.125 to 0.125
- glu_down: bfloat16 [5632, 2048], P('tensor', 'dp'), may hold values from -0.078125 to 0.078125
- norm_gain: float32 [2048], replicated, may hold values from 0.5 to 1.5
- mixer_gain: float32 [2048], replicated, may hold values from 0.5 to 1.5
- ffn_gain: float32 [2048], replicated, may hold values from 0.5 to 1.5
- bound_table: float32 [24, 2048], replicated, may hold values from -6 to 6
- lengths: int32 [32], P('dp'), may hold values from 0 to 256, as said below
- bucket: int32 [16], P('dp'), may hold values from 0 to 1, as said below
- cotangent: bfloat16 [4096, 2048], P(('dp', 'tensor')), may hold values from -6 to 6
Outputs:
- block_out: bfloat16 [4096, 2048], P(('dp', 'tensor'))
- grad_tokens: float32 [4096, 2048], P('dp')
- grad_input_proj: float32 [2048, 2048], P('dp')
- grad_forget_proj: float32 [2048, 2048], P('dp')
- grad_outgate_proj: float32 [2048, 2048], P('dp')
- grad_output_proj: float32 [2048, 2048], P('dp')
- grad_glu_gate: float32 [2048, 5632], P('dp', 'tensor')
- grad_glu_up: float32 [2048, 5632], P('dp', 'tensor')
- grad_glu_down: float32 [5632, 2048], P('tensor', 'dp')
- grad_norm_gain: float32 [2048], P('dp')
- grad_mixer_gain: float32 [2048], P('dp')
- grad_ffn_gain: float32 [2048], P('dp')
- grad_bound_table: float32 [24, 2048], P(None, 'dp')
Inputs may be any that keep to these rules, and one draw needn't show every extreme that they name: Dp index d holds 2**bucket[d] slots of 256 // 2**bucket[d] rows; index 0 has bucket 0 and index 1 has bucket 1. lengths[d * 2 + j] is the length of slot j of dp index d: 0 for j >= 2**bucket[d]; otherwise between max(128, L // 2 + 1) and L, the slot's length L, and exactly L for j = 0.
All inputs are finite; a program needn't handle non-finite values.
Results may differ from a plain program's by a relative error of at most 0.019.
Values may be sent and summed in bfloat16 or wider, within the bound.
A program may use at most 256 MiB of HBM per device.

v0:
```python
import jax
import jax.numpy as jnp
from jax import lax
from jax.sharding import PartitionSpec as P

LAYER = 12


epsilon = 1e-06


def rms_scale(values):
    return lax.rsqrt(jnp.mean(values * values, axis=-1, keepdims=True) + epsilon)


def norm_back(values, row_scale, gain_row, incoming):
    weighted = incoming * gain_row
    cubed = row_scale * row_scale * row_scale
    return row_scale * weighted - values * cubed * jnp.mean(
        weighted * values, axis=-1, keepdims=True
    )


def silu_slope(values):
    logistic = jax.nn.sigmoid(values)
    return logistic * (1.0 + values * (1.0 - logistic))


def matmul(first_op, second_op):
    return jnp.dot(first_op, second_op, preferred_element_type=jnp.float32)


def cross_rows(first_op, second_op):
    return lax.dot_general(
        first_op, second_op, (((0,), (0,)), ((), ())), preferred_element_type=jnp.float32
    )


def cross_cols(first_op, second_op):
    return lax.dot_general(
        first_op, second_op, (((1,), (1,)), ((), ())), preferred_element_type=jnp.float32
    )


def linear_step(earlier, latter):
    return (earlier[0] * latter[0], latter[0] * earlier[1] + latter[1])


def layout(lengths, bucket, row_count):
    slot_len = row_count // jnp.left_shift(jnp.int32(1), bucket[0])
    position = jnp.arange(row_count, dtype=jnp.int32)
    slot_index = position // slot_len
    offset = position - slot_index * slot_len
    slot_ids = jnp.arange(lengths.shape[0], dtype=jnp.int32)
    chosen = (slot_index[:, None] == slot_ids[None, :]).astype(jnp.int32)
    slot_limit = jnp.sum(chosen * lengths[None, :], axis=1)
    valid_mask = (offset < slot_limit).astype(jnp.float32)[:, None]
    keep_mask = (offset > 0).astype(jnp.float32)[:, None]
    return (valid_mask, keep_mask)


def bound_parts(bound_table):
    shares = jax.nn.softmax(bound_table, axis=0)
    layer_ids = jnp.arange(bound_table.shape[0], dtype=jnp.int32)[:, None]
    picked = ((layer_ids >= 1) & (layer_ids <= LAYER)).astype(jnp.float32)
    return (shares, picked, jnp.sum(shares * picked, axis=0))


def body(
    tokens_in,
    input_proj,
    forget_proj,
    outgate_proj,
    output_proj,
    glu_gate,
    glu_up,
    glu_down,
    norm_gain,
    mixer_gain,
    ffn_gain,
    bound_table,
    lengths,
    bucket,
    cotangent,
):
    row_count = tokens_in.shape[0]
    share_rows = cotangent.shape[0]
    first_row = lax.axis_index("tensor") * share_rows
    valid_mask, keep_mask = layout(lengths, bucket, row_count)
    mixer_full = (
        lax.all_gather(input_proj, "dp", axis=0, tiled=True),
        lax.all_gather(forget_proj, "dp", axis=0, tiled=True),
        lax.all_gather(outgate_proj, "dp", axis=0, tiled=True),
        lax.all_gather(output_proj, "dp", axis=0, tiled=True),
    )
    glu_full = (
        lax.all_gather(glu_gate, "dp", axis=0, tiled=True),
        lax.all_gather(glu_up, "dp", axis=0, tiled=True),
        lax.all_gather(glu_down, "dp", axis=1, tiled=True),
    )
    inputs = tokens_in.astype(jnp.float32)
    scale_one = rms_scale(inputs)
    normed_one = (inputs * scale_one * norm_gain).astype(jnp.bfloat16)
    input_pre = matmul(normed_one, mixer_full[0])
    forget_pre = matmul(normed_one, mixer_full[1])
    outgate_pre = matmul(normed_one, mixer_full[2])
    shares, picked, lower_bound = bound_parts(bound_table)
    forget_sig = jax.nn.sigmoid(forget_pre)
    forget = lower_bound + (1.0 - lower_bound) * forget_sig
    input_act = jax.nn.silu(input_pre)
    inject = input_act * (1.0 - forget) * valid_mask
    decay_rate = forget * keep_mask
    hidden_state = lax.associative_scan(linear_step, (decay_rate, inject), axis=0)[1]
    scale_state = rms_scale(hidden_state)
    normed_state = hidden_state * scale_state
    outgate_act = jax.nn.silu(outgate_pre)
    mix_normed = (normed_state * mixer_gain * outgate_act).astype(jnp.bfloat16)
    residual = inputs + matmul(mix_normed, mixer_full[3])
    scale_two = rms_scale(residual)
    normed_two = (residual * scale_two * ffn_gain).astype(jnp.bfloat16)
    gate_pre = matmul(normed_two, glu_full[0])
    up_pre = matmul(normed_two, glu_full[1])
    hidden = (jax.nn.silu(gate_pre) * up_pre).astype(jnp.bfloat16)
    summed = lax.psum_scatter(
        matmul(hidden, glu_full[2]).astype(jnp.bfloat16), "tensor", scatter_dimension=0, tiled=True
    ).astype(jnp.float32)
    residual_rows = lax.dynamic_slice_in_dim(residual, first_row, share_rows, 0)
    block_out = (residual_rows + summed).astype(jnp.bfloat16)
    valid_rows = lax.dynamic_slice_in_dim(valid_mask, first_row, share_rows, 0)
    grad_out_rows = (cotangent.astype(jnp.float32) * valid_rows).astype(jnp.bfloat16)
    grad_out = lax.all_gather(grad_out_rows, "tensor", axis=0, tiled=True)
    mixer_full = (
        lax.all_gather(input_proj, "dp", axis=0, tiled=True),
        lax.all_gather(forget_proj, "dp", axis=0, tiled=True),
        lax.all_gather(outgate_proj, "dp", axis=0, tiled=True),
        lax.all_gather(output_proj, "dp", axis=0, tiled=True),
    )
    glu_full = (
        lax.all_gather(glu_gate, "dp", axis=0, tiled=True),
        lax.all_gather(glu_up, "dp", axis=0, tiled=True),
        lax.all_gather(glu_down, "dp", axis=1, tiled=True),
    )
    grad_down = cross_rows(hidden, grad_out)
    grad_hidden = cross_cols(grad_out, glu_full[2])
    grad_up = (grad_hidden * jax.nn.silu(gate_pre)).astype(jnp.bfloat16)
    grad_gate = (grad_hidden * up_pre * silu_slope(gate_pre)).astype(jnp.bfloat16)
    grad_w_gate = cross_rows(normed_two, grad_gate)
    grad_w_up = cross_rows(normed_two, grad_up)
    grad_normed_two = cross_cols(grad_gate, glu_full[0]) + cross_cols(grad_up, glu_full[1])
    grad_normed_two = lax.psum(grad_normed_two, "tensor")
    grad_residual = grad_out.astype(jnp.float32) + norm_back(
        residual, scale_two, ffn_gain, grad_normed_two
    )
    grad_ffn_gain = jnp.sum(grad_normed_two * residual * scale_two, axis=0)
    grad_mix = grad_residual.astype(jnp.bfloat16)
    grad_mixed = cross_cols(grad_mix, mixer_full[3])
    grad_mixer_gain = jnp.sum(grad_mixed * normed_state * outgate_act, axis=0)
    grad_state_out = norm_back(hidden_state, scale_state, mixer_gain * outgate_act, grad_mixed)
    grad_outgate = (grad_mixed * normed_state * mixer_gain * silu_slope(outgate_pre)).astype(
        jnp.bfloat16
    )
    decay_next = jnp.concatenate([decay_rate[1:], jnp.zeros_like(decay_rate[:1])], axis=0)
    grad_state = lax.associative_scan(
        linear_step, (decay_next, grad_state_out), reverse=True, axis=0
    )[1]
    state_prev = jnp.concatenate([jnp.zeros_like(hidden_state[:1]), hidden_state[:-1]], axis=0)
    grad_forget = grad_state * (state_prev * keep_mask - input_act * valid_mask)
    grad_input = (grad_state * (1.0 - forget) * valid_mask * silu_slope(input_pre)).astype(
        jnp.bfloat16
    )
    grad_forget_pre = (grad_forget * (1.0 - lower_bound) * forget_sig * (1.0 - forget_sig)).astype(
        jnp.bfloat16
    )
    grad_bound = jnp.sum(grad_forget * (1.0 - forget_sig), axis=0)
    grad_table = shares * (picked - lower_bound[None, :]) * grad_bound[None, :]
    grad_normed_one = (
        cross_cols(grad_input, mixer_full[0])
        + cross_cols(grad_forget_pre, mixer_full[1])
        + cross_cols(grad_outgate, mixer_full[2])
    )
    grad_tokens = grad_residual + norm_back(inputs, scale_one, norm_gain, grad_normed_one)
    grad_norm_gain = jnp.sum(grad_normed_one * inputs * scale_one, axis=0)
    grad_w_input = cross_rows(normed_one, grad_input)
    grad_w_forget = cross_rows(normed_one, grad_forget_pre)
    grad_w_outgate = cross_rows(normed_one, grad_outgate)
    grad_w_out = cross_rows(mix_normed, grad_mix)
    reduced = (
        lax.psum_scatter(
            grad_w_input.astype(jnp.bfloat16), "dp", scatter_dimension=0, tiled=True
        ).astype(jnp.float32),
        lax.psum_scatter(
            grad_w_forget.astype(jnp.bfloat16), "dp", scatter_dimension=0, tiled=True
        ).astype(jnp.float32),
        lax.psum_scatter(
            grad_w_outgate.astype(jnp.bfloat16), "dp", scatter_dimension=0, tiled=True
        ).astype(jnp.float32),
        lax.psum_scatter(
            grad_w_out.astype(jnp.bfloat16), "dp", scatter_dimension=0, tiled=True
        ).astype(jnp.float32),
        lax.psum_scatter(
            grad_w_gate.astype(jnp.bfloat16), "dp", scatter_dimension=0, tiled=True
        ).astype(jnp.float32),
        lax.psum_scatter(
            grad_w_up.astype(jnp.bfloat16), "dp", scatter_dimension=0, tiled=True
        ).astype(jnp.float32),
        lax.psum_scatter(
            grad_down.astype(jnp.bfloat16), "dp", scatter_dimension=1, tiled=True
        ).astype(jnp.float32),
        lax.psum_scatter(
            grad_norm_gain.astype(jnp.bfloat16), "dp", scatter_dimension=0, tiled=True
        ).astype(jnp.float32),
        lax.psum_scatter(
            grad_mixer_gain.astype(jnp.bfloat16), "dp", scatter_dimension=0, tiled=True
        ).astype(jnp.float32),
        lax.psum_scatter(
            grad_ffn_gain.astype(jnp.bfloat16), "dp", scatter_dimension=0, tiled=True
        ).astype(jnp.float32),
        lax.psum_scatter(
            grad_table.astype(jnp.bfloat16), "dp", scatter_dimension=1, tiled=True
        ).astype(jnp.float32),
    )
    mixer_grads = (reduced[0], reduced[1], reduced[2], reduced[3])
    return (
        block_out,
        grad_tokens,
        mixer_grads[0],
        mixer_grads[1],
        mixer_grads[2],
        mixer_grads[3],
        reduced[4],
        reduced[5],
        reduced[6],
        reduced[7],
        reduced[8],
        reduced[9],
        reduced[10],
    )


def solution(mesh):
    return jax.shard_map(
        body,
        mesh=mesh,
        in_specs=(
            P("dp", None),
            P("dp", None),
            P("dp", None),
            P("dp", None),
            P("dp", None),
            P("dp", "tensor"),
            P("dp", "tensor"),
            P("tensor", "dp"),
            P(),
            P(),
            P(),
            P(),
            P("dp"),
            P("dp"),
            P(("dp", "tensor"), None),
        ),
        out_specs=(
            P(("dp", "tensor"), None),
            P("dp", None),
            P("dp", None),
            P("dp", None),
            P("dp", None),
            P("dp", None),
            P("dp", "tensor"),
            P("dp", "tensor"),
            P("tensor", "dp"),
            P("dp"),
            P("dp"),
            P("dp"),
            P(None, "dp"),
        ),
        check_vma=False,
    )
```

profile of v0, /device:TPU:0, one launch (start us, length us, event | category | flops | bytes accessed | tf_op | source)
XLA Modules:
  0.0 2801.7 jit_solution(408120175934849856)
XLA Ops:
  15.7 110.6 %all-gather.9.cloned.1.call-done = bf16[2048,2048]{1,0:T(8,128)(2,1)} async-done(((bf16[128,2048]{1,0:T(8,128)(2,1)}), bf16[2048,2048]{1,0:T(8,128)(2,1)}) %all-gather.9.cloned.1.call-update) | async-done | bytes 8388624 | tf_op jit(solution)/shard_map/all_gather | solution.py:91
  133.5 106.7 %all-gather.11.cloned.1.call-done = bf16[2048,2048]{1,0:T(8,128)(2,1)} async-done(((bf16[128,2048]{1,0:T(8,128)(2,1)}), bf16[2048,2048]{1,0:T(8,128)(2,1)}) %all-gather.11.cloned.1.call-update) | async-done | bytes 8388624 | tf_op jit(solution)/shard_map/all_gather | solution.py:92
  309.5 44.5 %all-gather.13.cloned.1.call-done = bf16[2048,2048]{1,0:T(8,128)(2,1)} async-done(((bf16[128,2048]{1,0:T(8,128)(2,1)}), bf16[2048,2048]{1,0:T(8,128)(2,1)}) %all-gather.13.cloned.1.call-update) | async-done | bytes 8388624 | tf_op jit(solution)/shard_map/all_gather | solution.py:93
  362.3 105.3 %all-gather.15.cloned.1.call-done = bf16[2048,2048]{1,0:T(8,128)(2,1)} async-done(((bf16[128,2048]{1,0:T(8,128)(2,1)}), bf16[2048,2048]{1,0:T(8,128)(2,1)}) %all-gather.15.cloned.1.call-update) | async-done | bytes 8388624 | tf_op jit(solution)/shard_map/all_gather | solution.py:94
  475.1 135.5 %all-gather.19.cloned.1.call-done = bf16[2048,2816]{1,0:T(8,128)(2,1)} async-done(((bf16[128,2816]{1,0:T(8,128)(2,1)}), bf16[2048,2816]{1,0:T(8,128)(2,1)}) %all-gather.19.cloned.1.call-update) | async-done | bytes 11534352 | tf_op jit(solution)/shard_map/all_gather | solution.py:98
  610.7 9.3 fusion.65
  620.0 133.7 %all-gather.17.cloned.1.call-done = bf16[2048,2816]{1,0:T(8,128)(2,1)} async-done(((bf16[128,2816]{1,0:T(8,128)(2,1)}), bf16[2048,2816]{1,0:T(8,128)(2,1)}) %all-gather.17.cloned.1.call-update) | async-done | bytes 11534352 | tf_op jit(solution)/shard_map/all_gather | solution.py:97
  753.7 9.3 fusion.64
  763.0 186.5 %all-gather.21.cloned.1.call-done = bf16[2816,2048]{1,0:T(8,128)(2,1)} async-done(((bf16[2816,128]{1,0:T(8,128)(2,1)}), bf16[2816,2048]{1,0:T(8,128)(2,1)}) %all-gather.21.cloned.1.call-update) | async-done | bytes 11534352 | tf_op jit(solution)/shard_map/all_gather | solution.py:99
  949.5 21.4 multiply_convert_fusion
  1181.0 9.0 slice.515
  1225.9 16.7 rev.2
  1281.7 9.1 convolution_convert_fusion.2
  1290.7 15.2 copy.28
  1306.1 9.1 convolution_convert_fusion
  1315.5 9.1 convolution_convert_fusion.1
  1343.4 74.7 %all-reduce.37 = (bf16[2048]{0:T(1024)(128)(2,1)S(1)}, bf16[2048]{0:T(1024)(128)(2,1)S(1)}, bf16[2048]{0:T(1024)(128)(2,1)S(1)}) all-reduce(bf16[2048]{0:T(1024)(128)(2,1)S(1)} %get-tuple-element.17, bf16[2048]{0:T(1024)(128)(2,1)S(1)} %copy-done.46, ...), channel_id=10, replica_groups=mesh['dp'=16,'tensor'=2] {'dp'}, use_global_device_ids=true, to_apply=%region_20.21.clone | all-reduce | flops 6144 | bytes 24576
  1426.9 76.6 %reduce-scatter.22.cloned.1.call-done = bf16[128,2048]{1,0:T(8,128)(2,1)} async-done(((bf16[2048,2048]{1,0:T(8,128)(2,1)}), bf16[128,2048]{1,0:T(8,128)(2,1)}) %reduce-scatter.22.cloned.1.call-update) | async-done | bytes 524304 | tf_op jit(solution)/shard_map/reduce_scatter | solution.py:197
  1505.7 180.4 %reduce-scatter.16.cloned.1.call-done = bf16[128,2048]{1,0:T(8,128)(2,1)} async-done(((bf16[2048,2048]{1,0:T(8,128)(2,1)}), bf16[128,2048]{1,0:T(8,128)(2,1)}) %reduce-scatter.16.cloned.1.call-update) | async-done | bytes 524304 | tf_op jit(solution)/shard_map/reduce_scatter | solution.py:188
  1688.2 180.4 %reduce-scatter.20.cloned.1.call-done = bf16[128,2048]{1,0:T(8,128)(2,1)} async-done(((bf16[2048,2048]{1,0:T(8,128)(2,1)}), bf16[128,2048]{1,0:T(8,128)(2,1)}) %reduce-scatter.20.cloned.1.call-update) | async-done | bytes 524304 | tf_op jit(solution)/shard_map/reduce_scatter | solution.py:194
  1870.7 180.4 %reduce-scatter.18.cloned.1.call-done = bf16[128,2048]{1,0:T(8,128)(2,1)} async-done(((bf16[2048,2048]{1,0:T(8,128)(2,1)}), bf16[128,2048]{1,0:T(8,128)(2,1)}) %reduce-scatter.18.cloned.1.call-update) | async-done | bytes 524304 | tf_op jit(solution)/shard_map/reduce_scatter | solution.py:191
  2053.2 243.5 %reduce-scatter.28.cloned.1.call-done = bf16[128,2816]{1,0:T(8,128)(2,1)} async-done(((bf16[2048,2816]{1,0:T(8,128)(2,1)}), bf16[128,2816]{1,0:T(8,128)(2,1)}) %reduce-scatter.28.cloned.1.call-update) | async-done | bytes 720912
  2299.4 245.1 %reduce-scatter.26.cloned.1.call-done = bf16[128,2816]{1,0:T(8,128)(2,1)} async-done(((bf16[2048,2816]{1,0:T(8,128)(2,1)}), bf16[128,2816]{1,0:T(8,128)(2,1)}) %reduce-scatter.26.cloned.1.call-update) | async-done | bytes 720912 | tf_op jit(solution)/shard_map/reduce_scatter | solution.py:203
  2546.8 245.5 %reduce-scatter.24.cloned.1.call-done = bf16[128,2816]{1,0:T(8,128)(2,1)} async-done(((bf16[2048,2816]{1,0:T(8,128)(2,1)}), bf16[128,2816]{1,0:T(8,128)(2,1)}) %reduce-scatter.24.cloned.1.call-update) | async-done | bytes 720912 | tf_op jit(solution)/shard_map/reduce_scatter | solution.py:200
  (391 shorter events, 426.8 us)
Async XLA Ops:
  7.2 119.2 %all-gather.9.cloned.1.call-start = ((), (), s32[]{:S(2)}) async-start(), calls=%async_computation.9 | async-start | bytes 8912896 | tf_op jit(solution)/shard_map/all_gather | solution.py:91
  7.9 232.3 %all-gather.11.cloned.1.call-start = ((), (), s32[]{:S(2)}) async-start(), calls=%async_computation.10 | async-start | bytes 8912896 | tf_op jit(solution)/shard_map/all_gather | solution.py:92
  8.7 345.3 %all-gather.13.cloned.1.call-start = ((), (), s32[]{:S(2)}) async-start(), calls=%async_computation.11 | async-start | bytes 8912896 | tf_op jit(solution)/shard_map/all_gather | solution.py:93
  9.4 458.3 %all-gather.15.cloned.1.call-start = ((), (), s32[]{:S(2)}) async-start(), calls=%async_computation.12 | async-start | bytes 8912896 | tf_op jit(solution)/shard_map/all_gather | solution.py:94
  10.0 600.7 %all-gather.19.cloned.1.call-start = ((), (), s32[]{:S(2)}) async-start(), calls=%async_computation.14 | async-start | bytes 12255232 | tf_op jit(solution)/shard_map/all_gather | solution.py:98
  10.6 743.1 %all-gather.17.cloned.1.call-start = ((), (), s32[]{:S(2)}) async-start(), calls=%async_computation.13 | async-start | bytes 12255232 | tf_op jit(solution)/shard_map/all_gather | solution.py:97
  11.2 751.9 %all-gather.23.cloned.1.call-start = ((), (), s32[]{:S(2)}) async-start(), calls=%async_computation.17 | async-start | bytes 1572864 | tf_op jit(solution)/shard_map/all_gather | solution.py:131
  12.3 227.9 %copy-start.42 = (f32[256]{0:T(256)}, f32[256]{0:T(256)S(1)}, u32[]{:S(2)}) copy-start(f32[256]{0:T(256)S(1)} %get-tuple-element.78) | copy-start | bytes 3076
  12.3 227.9 %copy-start.44 = (f32[256]{0:T(256)}, f32[256]{0:T(256)S(1)}, u32[]{:S(2)}) copy-start(f32[256]{0:T(256)S(1)} %get-tuple-element.79) | copy-start | bytes 3076
  13.3 936.2 %all-gather.21.cloned.1.call-start = ((), (), s32[]{:S(2)}) async-start(), calls=%async_computation.15 | async-start | bytes 12255232 | tf_op jit(solution)/shard_map/all_gather | solution.py:99
  14.1 1031.9 %all-reduce.40.cloned.1.call-start = ((), (), s32[]{:S(2)}) async-start(), calls=%async_computation.18 | async-start | bytes 4194304 | tf_op jit(solution)/shard_map/psum | solution.py:150
  14.2 119.3 %copy-start.28 = (f32[2048]{0:T(1024)}, f32[2048]{0:T(1024)S(1)}, u32[]{:S(2)}) copy-start(f32[2048]{0:T(1024)S(1)} %reduce_max.9) | copy-start | bytes 24580
  14.7 118.7 %copy-start.31 = (f32[2048]{0:T(1024)}, f32[2048]{0:T(1024)S(1)}, u32[]{:S(2)}) copy-start(f32[2048]{0:T(1024)S(1)} %fusion.26) | copy-start | bytes 24580
  15.7 338.3 %copy-start.35 = (f32[256]{0:T(256)}, f32[256]{0:T(256)S(1)}, u32[]{:S(2)}) copy-start(f32[256]{0:T(256)S(1)} %get-tuple-element.66) | copy-start | bytes 3076
  15.7 224.5 %copy-start.33 = (f32[2048]{0:T(1024)}, f32[2048]{0:T(1024)S(1)}, u32[]{:S(2)}) copy-start(f32[2048]{0:T(1024)S(1)} %broadcast_subtract_fusion) | copy-start | bytes 24580
  986.9 433.0 %reduce-scatter.14.cloned.1.call-start = ((), (), s32[]{:S(2)}) async-start(), calls=%async_computation.16 | async-start | bytes 1572864 | tf_op jit(solution)/shard_map/reduce_scatter | solution.py:124
  1045.9 379.6 %reduce-scatter.30.cloned.1.call-start = ((), (), s32[]{:S(2)}) async-start(), calls=%async_computation.26 | async-start | bytes 557056
  1249.4 254.1 %reduce-scatter.22.cloned.1.call-start = ((), (), s32[]{:S(2)}) async-start(), calls=%async_computation.22 | async-start | bytes 8912896 | tf_op jit(solution)/shard_map/reduce_scatter | solution.py:197
  1257.1 429.0 %reduce-scatter.16.cloned.1.call-start = ((), (), s32[]{:S(2)}) async-start(), calls=%async_computation.19 | async-start | bytes 8912896 | tf_op jit(solution)/shard_map/reduce_scatter | solution.py:188
  1264.7 603.9 %reduce-scatter.20.cloned.1.call-start = ((), (), s32[]{:S(2)}) async-start(), calls=%async_computation.21 | async-start | bytes 8912896 | tf_op jit(solution)/shard_map/reduce_scatter | solution.py:194
  1272.1 779.0 %reduce-scatter.18.cloned.1.call-start = ((), (), s32[]{:S(2)}) async-start(), calls=%async_computation.20 | async-start | bytes 8912896 | tf_op jit(solution)/shard_map/reduce_scatter | solution.py:191
  1281.6 1015.1 %reduce-scatter.28.cloned.1.call-start = ((), (), s32[]{:S(2)}) async-start(), calls=%async_computation.25 | async-start | bytes 12255232
  1306.0 1238.5 %reduce-scatter.26.cloned.1.call-start = ((), (), s32[]{:S(2)}) async-start(), calls=%async_computation.24 | async-start | bytes 12255232 | tf_op jit(solution)/shard_map/reduce_scatter | solution.py:203
  1315.2 1477.1 %reduce-scatter.24.cloned.1.call-start = ((), (), s32[]{:S(2)}) async-start(), calls=%async_computation.23 | async-start | bytes 12255232 | tf_op jit(solution)/shard_map/reduce_scatter | solution.py:200
  (47 other events, 490.5 us)
Sparse Core Ops, SparseCore 0:
  10.8 115.5 all-gather.8
  129.1 111.0 all-gather.10
  243.0 111.0 all-gather.12
  356.6 111.0 all-gather.14
  470.3 140.3 all-gather.18
  613.3 140.3 all-gather.16
  755.8 7.2 all-gather.22
  765.7 183.7 all-gather.20
  987.0 19.3 all-reduce.39
  1046.0 6.6 reduce-scatter.13
  1249.6 74.7 reduce-scatter.29
  1326.6 176.9 reduce-scatter.21
  1506.0 180.0 reduce-scatter.15
  1688.3 180.2 reduce-scatter.19
  1870.8 180.2 reduce-scatter.17
  2053.4 243.2 reduce-scatter.27
  2299.0 245.4 reduce-scatter.25
  2546.8 245.5 reduce-scatter.23
where the time goes:
time: 2820 us; the launch traced here: 2800 us
  waiting for transfers between devices  2180 us (77%)
  local copies, waits for them, and re-layouts  263 us (9%)
  matrix products  175 us (6%)
  other arithmetic  91.7 us (3%)
  blocking collectives  74.7 us (3%)
    unnamed x20, waiting for transfers between devices  248 us
    reduce_scatter x1, waiting for transfers between devices, body(): lax.psum_scatter(grad_w_gate.astype(jnp.bfloat16), 'dp', scatter_dimensio...  246 us
    reduce_scatter x1, waiting for transfers between devices, body(): lax.psum_scatter(grad_w_up.astype(jnp.bfloat16), 'dp', scatter_dimension=...  245 us
    all_gather x1, waiting for transfers between devices, body(): lax.all_gather(glu_down, 'dp', axis=1, tiled=True)  186 us
    reduce_scatter x1, waiting for transfers between devices, body(): lax.psum_scatter(grad_w_outgate.astype(jnp.bfloat16), 'dp', scatter_dimen...  180 us
    reduce_scatter x1, waiting for transfers between devices, body(): lax.psum_scatter(grad_w_input.astype(jnp.bfloat16), 'dp', scatter_dimensi...  180 us
    reduce_scatter x1, waiting for transfers between devices, body(): lax.psum_scatter(grad_w_forget.astype(jnp.bfloat16), 'dp', scatter_dimens...  180 us
    all_gather x1, waiting for transfers between devices, body(): lax.all_gather(glu_up, 'dp', axis=0, tiled=True)  136 us
  transfers between devices with their start and end apart: 18, of which 14 were waited for; matrix products, arithmetic and copies ran while one was open for 17% of the time, Pallas kernels for 0%

commit v1 on v0

v1 whole, which is shorter than its diff:
```python
import functools

import jax
import jax.numpy as jnp
from jax import lax
from jax.experimental import pallas as pl
from jax.experimental.pallas import tpu as pltpu
from jax.sharding import PartitionSpec as P

LAYER = 12
epsilon = 1e-06
bf16 = jnp.bfloat16
f32 = jnp.float32


def rms_scale(values):
    return lax.rsqrt(jnp.mean(values * values, axis=-1, keepdims=True) + epsilon)


def norm_back(values, row_scale, gain_row, incoming):
    weighted = incoming * gain_row
    cubed = row_scale * row_scale * row_scale
    return row_scale * weighted - values * cubed * jnp.mean(
        weighted * values, axis=-1, keepdims=True
    )


def silu_slope(values):
    logistic = jax.nn.sigmoid(values)
    return logistic * (1.0 + values * (1.0 - logistic))


def matmul(first_op, second_op):
    return jnp.dot(first_op, second_op, preferred_element_type=f32)


def cross_rows(first_op, second_op):
    return lax.dot_general(
        first_op, second_op, (((0,), (0,)), ((), ())), preferred_element_type=f32
    )


def cross_cols(first_op, second_op):
    return lax.dot_general(
        first_op, second_op, (((1,), (1,)), ((), ())), preferred_element_type=f32
    )


def pick(values, index, axis):
    return lax.dynamic_index_in_dim(values, index, axis, keepdims=False)


def layout(lengths, bucket, row_count):
    slot_len = row_count // jnp.left_shift(jnp.int32(1), bucket)
    position = jnp.arange(row_count, dtype=jnp.int32)
    slot_index = position // slot_len
    offset = position - slot_index * slot_len
    slot_ids = jnp.arange(lengths.shape[0], dtype=jnp.int32)
    chosen = (slot_index[:, None] == slot_ids[None, :]).astype(jnp.int32)
    slot_limit = jnp.sum(chosen * lengths[None, :], axis=1)
    valid_mask = (offset < slot_limit).astype(f32)[:, None]
    keep_mask = (offset > 0).astype(f32)[:, None]
    return (valid_mask, keep_mask)


def bound_parts(bound_table):
    shares = jax.nn.softmax(bound_table, axis=0)
    layer_ids = jnp.arange(bound_table.shape[0], dtype=jnp.int32)[:, None]
    picked = ((layer_ids >= 1) & (layer_ids <= LAYER)).astype(f32)
    return (shares, picked, jnp.sum(shares * picked, axis=0))


def scan_rows(decay_ref, add_ref, out_ref, reverse):
    rows, width = out_ref.shape
    tiles = rows // 8
    sub = lax.broadcasted_iota(jnp.int32, (8, width), 0)

    def step(i, carry):
        j = tiles - 1 - i if reverse else i
        at = pl.ds(pl.multiple_of(j * 8, 8), 8)
        a = decay_ref[at, :]
        b = add_ref[at, :]
        for s in (1, 2, 4):
            shift = 8 - s if reverse else s
            inside = sub < 8 - s if reverse else sub >= s
            b = jnp.where(inside, b + a * pltpu.roll(b, shift, 0), b)
            a = jnp.where(inside, a * pltpu.roll(a, shift, 0), a)
        h = b + a * carry
        out_ref[at, :] = h
        edge = h[0:1, :] if reverse else h[7:8, :]
        return jnp.broadcast_to(edge, (8, width))

    lax.fori_loop(0, tiles, step, jnp.zeros((8, width), f32), unroll=4)


def mixer_forward_kernel(pre_ref, aux_ref, par_ref, state_ref, mix_ref, sq_ref, decay_ref, add_ref):
    width = state_ref.shape[1]
    input_pre = pre_ref[:, :width]
    forget_pre = pre_ref[:, width : 2 * width]
    outgate_pre = pre_ref[:, 2 * width :]
    valid = aux_ref[:, 0:1]
    keep = aux_ref[:, 1:2]
    bound = par_ref[0:1, :]
    gain = par_ref[1:2, :]
    forget = bound + (1.0 - bound) * jax.nn.sigmoid(forget_pre)
    add_ref[...] = input_pre * jax.nn.sigmoid(input_pre) * (1.0 - forget) * valid
    decay_ref[...] = forget * keep
    scan_rows(decay_ref, add_ref, state_ref, False)
    state = state_ref[...]
    mix_ref[...] = (state * gain * (outgate_pre * jax.nn.sigmoid(outgate_pre))).astype(bf16)
    sq_ref[...] = jnp.sum(state * state, axis=1, keepdims=True)


def mixer_forward(pre, aux, par, seq_rows):
    rows, width = pre.shape[0], pre.shape[1] // 3
    row_block = lambda n: pl.BlockSpec((seq_rows, n), lambda i: (i, 0))
    return pl.pallas_call(
        mixer_forward_kernel,
        grid=(rows // seq_rows,),
        in_specs=[
            row_block(3 * width),
            row_block(aux.shape[1]),
            pl.BlockSpec(par.shape, lambda i: (0, 0)),
        ],
        out_specs=[row_block(width), row_block(width), row_block(1)],
        out_shape=[
            jax.ShapeDtypeStruct((rows, width), f32),
            jax.ShapeDtypeStruct((rows, width), bf16),
            jax.ShapeDtypeStruct((rows, 1), f32),
        ],
        scratch_shapes=[pltpu.VMEM((seq_rows, width), f32)] * 2,
        cost_estimate=pl.CostEstimate(
            flops=rows * width * 60, bytes_accessed=rows * width * 20, transcendentals=rows * width * 3
        ),
        name="mixer_forward",
    )(pre, aux, par)


def mixer_backward_kernel(
    pre_ref, state_ref, up_ref, aux_ref, par_ref, grad_ref, sums_ref, decay_ref, add_ref, out_ref
):
    rows, width = state_ref.shape
    input_pre = pre_ref[:, :width]
    forget_pre = pre_ref[:, width : 2 * width]
    outgate_pre = pre_ref[:, 2 * width :]
    valid = aux_ref[:, 0:1]
    keep = aux_ref[:, 1:2]
    scale = aux_ref[:, 2:3]
    dot_mean = aux_ref[:, 3:4]
    bound = par_ref[0:1, :]
    gain = par_ref[1:2, :]
    state = state_ref[...]
    incoming = up_ref[...]
    at_row = lax.broadcasted_iota(jnp.int32, (rows, width), 0)
    sig_out = jax.nn.sigmoid(outgate_pre)
    act_out = outgate_pre * sig_out
    scaled = incoming * (state * scale)
    grad_ref[:, 2 * width :] = (
        scaled * gain * (sig_out * (1.0 + outgate_pre * (1.0 - sig_out)))
    ).astype(bf16)
    add_ref[...] = scale * (gain * act_out * incoming) - state * (scale * scale * scale * dot_mean)
    sig_forget = jax.nn.sigmoid(forget_pre)
    forget = bound + (1.0 - bound) * sig_forget
    decay_ref[...] = jnp.where(
        at_row < rows - 1, pltpu.roll(forget * keep, rows - 1, 0), 0.0
    )
    scan_rows(decay_ref, add_ref, out_ref, True)
    grad_state = out_ref[...]
    before = jnp.where(at_row > 0, pltpu.roll(state, 1, 0), 0.0)
    sig_in = jax.nn.sigmoid(input_pre)
    grad_forget = grad_state * (before * keep - input_pre * sig_in * valid)
    grad_ref[:, :width] = (
        grad_state * (1.0 - forget) * valid * (sig_in * (1.0 + input_pre * (1.0 - sig_in)))
    ).astype(bf16)
    grad_ref[:, width : 2 * width] = (
        grad_forget * (1.0 - bound) * sig_forget * (1.0 - sig_forget)
    ).astype(bf16)

    @pl.when(pl.program_id(0) == 0)
    def _():
        sums_ref[...] = jnp.zeros_like(sums_ref)

    sums_ref[0:1, :] += jnp.sum(scaled * act_out, axis=0, keepdims=True)
    sums_ref[1:2, :] += jnp.sum(grad_forget * (1.0 - sig_forget), axis=0, keepdims=True)


def mixer_backward(pre, state, incoming, aux, par, seq_rows):
    rows, width = state.shape
    row_block = lambda n: pl.BlockSpec((seq_rows, n), lambda i: (i, 0))
    whole = lambda shape: pl.BlockSpec(shape, lambda i: (0, 0))
    return pl.pallas_call(
        mixer_backward_kernel,
        grid=(rows // seq_rows,),
        in_specs=[
            row_block(3 * width),
            row_block(width),
            row_block(width),
            row_block(aux.shape[1]),
            whole(par.shape),
        ],
        out_specs=[row_block(3 * width), whole((2, width))],
        out_shape=[
            jax.ShapeDtypeStruct((rows, 3 * width), bf16),
            jax.ShapeDtypeStruct((2, width), f32),
        ],
        scratch_shapes=[pltpu.VMEM((seq_rows, width), f32)] * 3,
        cost_estimate=pl.CostEstimate(
            flops=rows * width * 90, bytes_accessed=rows * width * 26, transcendentals=rows * width * 3
        ),
        name="mixer_backward",
    )(pre, state, incoming, aux, par)


def body(
    n_dp,
    n_t,
    tokens_in,
    input_proj,
    forget_proj,
    outgate_proj,
    output_proj,
    glu_gate,
    glu_up,
    glu_down,
    norm_gain,
    mixer_gain,
    ffn_gain,
    bound_table,
    lengths,
    bucket,
    cotangent,
):
    depth = n_dp.bit_length() - 1
    tp_bits = (2, 0)
    fs_bits = tuple(b for b in reversed(range(depth)) if b not in tp_bits)
    t_depth = n_t.bit_length() - 1
    own_bits, free_bits = fs_bits[len(fs_bits) - t_depth :], fs_bits[: len(fs_bits) - t_depth]
    n_tp = 4
    tp_mask = (0, 1, 4, 5)
    axis_of = {b: depth - 1 - b for b in range(depth)}

    me = lax.axis_index("dp")
    t = lax.axis_index("tensor")
    bit = {b: (me >> b) & 1 for b in range(depth)}
    t_bit = {b: (t >> (t_depth - 1 - i)) & 1 for i, b in enumerate(own_bits)}
    q = bit[2] * 2 + bit[0]

    rows, width = tokens_in.shape
    share = cotangent.shape[0]
    block = width // n_dp
    free = 2 ** len(free_bits)
    feat = free * block

    def swap(values, mask):
        return lax.ppermute(values, "dp", [(i, i ^ mask) for i in range(n_dp)])

    def t_swap(values):
        return lax.ppermute(values, "tensor", [(0, 1), (1, 0)])

    def by_bit(which, own, other):
        return jnp.where(which == 0, own, other), jnp.where(which == 0, other, own)

    def in_order(parts, bits):
        parts = list(parts)
        for i, b in enumerate(reversed(bits)):
            step = 1 << i
            for r in range(len(parts)):
                if not r & step:
                    parts[r], parts[r | step] = by_bit(bit[b], parts[r], parts[r | step])
        return parts

    def t_gather(values):
        if n_t == 2:
            return jnp.stack(by_bit(t, values, t_swap(values)))
        return lax.all_gather(values, "tensor", axis=0)

    def t_scatter(values):
        if n_t == 2:
            return pick(values, t, 0).astype(f32) + t_swap(pick(values, 1 - t, 0)).astype(f32)
        return lax.psum_scatter(values, "tensor", scatter_dimension=0, tiled=False).astype(f32)

    def tp_gather(values):
        return [t_gather(values if r == 0 else swap(values, tp_mask[r])) for r in range(n_tp)]

    def tp_scatter(parts, kind):
        halves = [t_scatter(part) for part in parts]
        total = halves[0]
        for r in range(1, n_tp):
            total = total + swap(halves[r].astype(kind), tp_mask[r]).astype(f32)
        return total

    def exchange(values):
        parts = [pick(values, q, 0)]
        for r in range(1, n_tp):
            parts.append(swap(pick(values, q ^ r, 0), tp_mask[r]))
        return in_order(parts, tp_bits)

    def fs_gather(values):
        parts = [values]
        for b in fs_bits:
            parts = parts + [None] * 0 + [swap(v, 1 << b) for v in parts]
        return parts

    def weight_parts(shards):
        return fs_gather(jnp.stack(exchange(shards)))

    def weight_whole(parts):
        count = len(parts)
        flip = [0] * count
        for r in range(count):
            flip[sum(((r >> i) & 1) << (len(fs_bits) - 1 - i) for i in range(len(fs_bits)))] = parts[r]
        ordered = jnp.stack(in_order(flip, fs_bits))
        cols = ordered.shape[-1]
        ordered = ordered.reshape((2,) * depth + (block, cols))
        have = fs_bits + tp_bits
        axes = [have.index(b) for b in reversed(range(depth))]
        return ordered.transpose(axes + [depth, depth + 1]).reshape(width, cols)

    def weight_back(grad):
        cols = grad.shape[1]
        grad = grad.reshape((2,) * depth + (block, cols))
        for b in reversed(fs_bits):
            send = lax.dynamic_slice_in_dim(grad, 1 - bit[b], 1, axis_of[b]).astype(bf16)
            hold = lax.dynamic_slice_in_dim(grad, bit[b], 1, axis_of[b]).astype(f32)
            grad = hold + swap(send, 1 << b).astype(f32)
        return exchange(grad.reshape(n_tp, block, cols).astype(bf16))

    def my_columns(values):
        lead = values.shape[:-1]
        n = len(lead)
        values = values.reshape(lead + (2,) * depth + (block,))
        bits = list(reversed(range(depth)))
        for b in own_bits:
            values = pick(values, t_bit[b], n + bits.index(b))
            bits.remove(b)
        order = [n + bits.index(b) for b in tp_bits] + list(range(n)) + [n + bits.index(b) for b in free_bits]
        return values.transpose(order + [n + len(bits)]).reshape((n_tp,) + lead + (feat,))

    def my_half(values):
        return lax.dynamic_slice_in_dim(values, t * share, share, 0)

    inputs = tokens_in.astype(f32)
    scale_one = rms_scale(inputs)
    normed_mine = (inputs * scale_one * norm_gain).astype(bf16)
    normed_half = my_half(normed_mine)
    normed_parts = [normed_mine] + [
        t_gather(swap(normed_half, tp_mask[r])).reshape(rows, width) for r in range(1, n_tp)
    ]
    where_from = jnp.concatenate([lengths, bucket])
    masks = []
    for r in range(n_tp):
        got = where_from if r == 0 else swap(where_from, tp_mask[r])
        masks.append(layout(got[: lengths.shape[0]], got[lengths.shape[0] :], rows))
    valid_all = jnp.concatenate([m[0] for m in masks])
    keep_all = jnp.concatenate([m[1] for m in masks])

    mix_shards = jnp.concatenate(
        [my_columns(w) for w in (input_proj, forget_proj, outgate_proj)], axis=-1
    )
    mix_parts = weight_parts(mix_shards)
    out_piece = output_proj
    for b in own_bits:
        out_piece = jnp.where(t_bit[b] == bit[b], out_piece, swap(out_piece, 1 << b))
    out_pieces = [out_piece]
    for b in reversed(free_bits):
        out_pieces = out_pieces + [swap(v, 1 << b) for v in out_pieces]
    out_full = jnp.concatenate(in_order(out_pieces, free_bits))

    valid_mine = my_half(masks[0][0])
    grad_out_rows = (cotangent.astype(f32) * valid_mine).astype(bf16)

    hidden_cols = glu_gate.shape[1] // n_tp
    split_cols = lambda w: w.reshape(block, n_tp, hidden_cols).transpose(1, 0, 2)
    gate_parts = weight_parts(split_cols(glu_gate))
    up_parts = weight_parts(split_cols(glu_up))
    down_parts = weight_parts(glu_down.reshape(n_tp, hidden_cols, block).transpose(0, 2, 1))
    grad_out_all = jnp.stack(tp_gather(grad_out_rows)).reshape(n_tp * rows, width)

    normed_one = jnp.concatenate(normed_parts)
    mix_full = weight_whole(mix_parts)
    pre = matmul(normed_one, mix_full)
    my_table = pick(my_columns(bound_table), q, 0)
    bound_mine = bound_parts(my_table)[2]
    gain_mine = pick(my_columns(mixer_gain), q, 0)
    par = jnp.stack([bound_mine, gain_mine])
    aux = jnp.concatenate([valid_all, keep_all], axis=1)
    state, mix_raw, square = mixer_forward(pre, aux, par, rows)
    out_parts = matmul(mix_raw, out_full).astype(bf16).reshape(n_tp, n_t, share, width)
    square_parts = square.reshape(n_tp, n_t, share)
    square_sum = tp_scatter([square_parts[r] for r in range(n_tp)], f32)
    out_sum = tp_scatter([out_parts[r] for r in range(n_tp)], bf16)
    scale_state = lax.rsqrt(square_sum / width + epsilon)[:, None]
    mixed_out = out_sum * scale_state
    inputs_half = my_half(inputs)
    scale_one_half = my_half(scale_one)
    residual = inputs_half + mixed_out

    scale_two = rms_scale(residual)
    normed_two_half = (residual * scale_two * ffn_gain).astype(bf16)
    normed_two = jnp.stack(tp_gather(normed_two_half)).reshape(n_tp * rows, width)
    gate_full = weight_whole(gate_parts)
    up_full = weight_whole(up_parts)
    down_full = weight_whole(down_parts)
    gate_pre = matmul(normed_two, gate_full)
    up_pre = matmul(normed_two, up_full)
    grad_hidden = matmul(grad_out_all, down_full)
    gate_act = jax.nn.silu(gate_pre)
    hidden = (gate_act * up_pre).astype(bf16)
    grad_up = (grad_hidden * gate_act).astype(bf16)
    grad_gate = (grad_hidden * up_pre * silu_slope(gate_pre)).astype(bf16)
    grad_two_parts = (
        (cross_cols(grad_gate, gate_full) + cross_cols(grad_up, up_full))
        .astype(bf16)
        .reshape(n_tp, n_t, share, width)
    )
    grad_normed_two = tp_scatter([grad_two_parts[r] for r in range(n_tp)], bf16)
    block_parts = cross_cols(hidden, down_full).astype(bf16).reshape(n_tp, n_t, share, width)
    block_out = (residual + tp_scatter([block_parts[r] for r in range(n_tp)], bf16)).astype(bf16)
    grad_down_t = jnp.stack(weight_back(cross_rows(grad_out_all, hidden).astype(bf16)))
    grad_w_gate = jnp.stack(weight_back(cross_rows(normed_two, grad_gate).astype(bf16)))
    grad_w_up = jnp.stack(weight_back(cross_rows(normed_two, grad_up).astype(bf16)))
    grad_glu_down = grad_down_t.transpose(0, 2, 1).reshape(glu_down.shape).astype(f32)
    grad_glu_gate = grad_w_gate.transpose(1, 0, 2).reshape(glu_gate.shape).astype(f32)
    grad_glu_up = grad_w_up.transpose(1, 0, 2).reshape(glu_up.shape).astype(f32)

    grad_residual = grad_out_rows.astype(f32) + norm_back(
        residual, scale_two, ffn_gain, grad_normed_two
    )
    ffn_gain_sum = jnp.sum(grad_normed_two * residual * scale_two, axis=0)
    grad_mix_half = grad_residual.astype(bf16)
    dot_mean = jnp.sum(grad_mix_half.astype(f32) * mixed_out, axis=1, keepdims=True) / (
        scale_state * width
    )
    row_values = jnp.concatenate([scale_state, dot_mean], axis=1).T
    row_all = jnp.stack(tp_gather(row_values)).transpose(0, 1, 3, 2).reshape(n_tp * rows, 2)
    grad_mix = jnp.stack(tp_gather(grad_mix_half)).reshape(n_tp * rows, width)
    grad_mixed = cross_cols(grad_mix, out_full)
    aux_back = jnp.concatenate([valid_all, keep_all, row_all], axis=1)
    grads, sums = mixer_backward(pre, state, grad_mixed, aux_back, par, rows)
    one_parts = cross_cols(grads, mix_full).astype(bf16).reshape(n_tp, n_t, share, width)
    grad_normed_one = tp_scatter([one_parts[r] for r in range(n_tp)], bf16)
    grad_mix_w = jnp.stack(weight_back(cross_rows(normed_one, grads).astype(bf16)))

    mixed = (mix_raw.astype(f32) * row_all[:, :1]).astype(bf16)
    grad_out_w = cross_rows(mixed, grad_mix).astype(bf16).reshape((2,) * len(free_bits) + (block, width))
    for i, b in enumerate(free_bits):
        send = lax.dynamic_slice_in_dim(grad_out_w, 1 - bit[b], 1, i)
        hold = lax.dynamic_slice_in_dim(grad_out_w, bit[b], 1, i)
        grad_out_w = (hold.astype(f32) + swap(send, 1 << b).astype(f32)).astype(bf16)
    grad_out_w = grad_out_w.reshape(block, width)
    for b in own_bits:
        grad_out_w = (grad_out_w.astype(f32) + swap(grad_out_w, 1 << b).astype(f32)).astype(bf16)
    mine_t = jnp.int32(0)
    for b in own_bits:
        mine_t = mine_t * 2 + bit[b]
    if n_t == 2:
        other = t_swap(grad_out_w)
        grad_output_proj = jnp.where(mine_t == t, grad_out_w, other).astype(f32)
    else:
        grad_output_proj = pick(lax.all_gather(grad_out_w, "tensor", axis=0), mine_t, 0).astype(f32)

    mix_all = t_gather(grad_mix_w)
    mix_all = mix_all.reshape((2,) * t_depth + (2, 2) + (block, 3) + (2,) * len(free_bits) + (block,))
    order = list(own_bits) + list(tp_bits) + ["row", "which"] + list(free_bits) + ["col"]
    axes = [order.index(k) for k in ["which", "row"] + list(reversed(range(depth))) + ["col"]]
    mix_all = mix_all.transpose(axes).reshape(3, block, width).astype(f32)

    grad_tokens_half = my_half_residual = grad_residual + norm_back(
        inputs_half, scale_one_half, norm_gain, grad_normed_one
    )
    grad_tokens = t_gather(grad_tokens_half).reshape(rows, width)
    norm_gain_sum = jnp.sum(grad_normed_one * inputs_half * scale_one_half, axis=0)

    gains = jnp.stack([norm_gain_sum, ffn_gain_sum]).reshape((2,) + (2,) * depth + (block,))
    for b in reversed(range(depth)):
        at = 1 + axis_of[b]
        send = lax.dynamic_slice_in_dim(gains, 1 - bit[b], 1, at)
        hold = lax.dynamic_slice_in_dim(gains, bit[b], 1, at)
        gains = hold + swap(send, 1 << b)
    gains = gains.reshape(2, block)
    gains = gains + t_swap(gains) if n_t == 2 else lax.psum(gains, "tensor")

    for b in fs_bits:
        sums = sums + swap(sums, 1 << b)
    sums = t_gather(sums)
    sums = pick(sums, mine_t, 0).reshape((2,) + (2,) * len(free_bits) + (block,))
    for b in free_bits:
        sums = pick(sums, bit[b], 1)
    shares, picked, lower = bound_parts(lax.dynamic_slice_in_dim(bound_table, me * block, block, 1))
    grad_table = shares * (picked - lower[None, :]) * sums[1][None, :]

    return (
        block_out,
        grad_tokens,
        mix_all[0],
        mix_all[1],
        mix_all[2],
        grad_output_proj,
        grad_glu_gate,
        grad_glu_up,
        grad_glu_down,
        gains[0],
        sums[0],
        gains[1],
        grad_table,
    )


def solution(mesh):
    return jax.shard_map(
        functools.partial(body, mesh.shape["dp"], mesh.shape["tensor"]),
        mesh=mesh,
        in_specs=(
            P("dp", None),
            P("dp", None),
            P("dp", None),
            P("dp", None),
            P("dp", None),
            P("dp", "tensor"),
            P("dp", "tensor"),
            P("tensor", "dp"),
            P(),
            P(),
            P(),
            P(),
            P("dp"),
            P("dp"),
            P(("dp", "tensor"), None),
        ),
        out_specs=(
            P(("dp", "tensor"), None),
            P("dp", None),
            P("dp", None),
            P("dp", None),
            P("dp", None),
            P("dp", None),
            P("dp", "tensor"),
            P("dp", "tensor"),
            P("tensor", "dp"),
            P("dp"),
            P("dp"),
            P("dp"),
            P(None, "dp"),
        ),
        check_vma=False,
    )
```

time: 2820 us -> 916 us (0.32)
  waiting for transfers between devices: 2180 us -> 463 us
  starting transfers between devices: 1.11 us -> 118 us
  local copies, waits for them, and re-layouts: 263 us -> 151 us
  matrix products: 175 us -> 64.5 us
  blocking collectives: 74.7 us -> 0 us
    reduce_scatter x7 -> x0, waiting for transfers between devices: 1110 us -> none  [the longest x1 246 us: body(): lax.psum_scatter(grad_w_gate.astype(jnp.bfloat16), 'dp', scatter_dimensio...]
    all_gather x8 -> x0, waiting for transfers between devices: 823 us -> none  [the longest x1 186 us: body(): lax.all_gather(glu_down, 'dp', axis=1, tiled=True)]
    ppermute x0 -> x131, waiting for transfers between devices: none -> 463 us  [the longest x87 458 us: swap(): return lax.ppermute(values, 'dp', [(i, i ^ mask) for i in range(n_dp)])]
    unnamed x20 -> x0, waiting for transfers between devices: 248 us -> none
    slice x99 -> x13, local copies, waits for them, and re-layouts: 169 us -> 11.2 us  [the longest x3 3.7 us: body(): masks.append(layout(got[:lengths.shape[0]], got[lengths.shape[0]:], rows))]
    ppermute x0 -> x131, starting transfers between devices: none -> 118 us  [the longest x87 110 us: swap(): return lax.ppermute(values, 'dp', [(i, i ^ mask) for i in range(n_dp)])]
    unnamed x1 -> x0, blocking collectives: 74.7 us -> none
    reshape x0 -> x15, local copies, waits for them, and re-layouts: none -> 67.8 us  [the longest x3 23.3 us: weight_back(): grad = grad.reshape((2,) * depth + (block, cols))]
  transfers between devices with their start and end apart: 18 -> 131, of which waited for: 14 -> 51; matrix products, arithmetic and copies ran while one was open for 17% -> 26% of each run, Pallas kernels for 0% -> 1%
where the time goes in v1:
time: 916 us; the launch traced here: 904 us
  waiting for transfers between devices  463 us (51%)
  local copies, waits for them, and re-layouts  151 us (16%)
  starting transfers between devices  118 us (13%)
  other arithmetic  89.9 us (10%)
  matrix products  64.5 us (7%)
  Pallas kernels  11.1 us (1%)
    ppermute x87, waiting for transfers between devices, swap(): return lax.ppermute(values, 'dp', [(i, i ^ mask) for i in range(n_dp)])  458 us
    ppermute x87, starting transfers between devices, swap(): return lax.ppermute(values, 'dp', [(i, i ^ mask) for i in range(n_dp)])  110 us
    unnamed x255, local copies, waits for them, and re-layouts  25.3 us
    reshape x3, local copies, waits for them, and re-layouts, weight_back(): grad = grad.reshape((2,) * depth + (block, cols))  23.3 us
    reshape x3, local copies, waits for them, and re-layouts, weight_whole(): return ordered.transpose(axes + [depth, depth + 1]).reshape(width, cols)  22.3 us
    dot_general x5, matrix products, matmul(): return jnp.dot(first_op, second_op, preferred_element_type=f32)  22.2 us
    dot_general x5, matrix products, cross_cols(): lax.dot_general(first_op, second_op, (((1,), (1,)), ((), ())), preferred_...  21.4 us
    dot_general x5, matrix products, cross_rows(): lax.dot_general(first_op, second_op, (((0,), (0,)), ((), ())), preferred_...  20.9 us
  transfers between devices with their start and end apart: 131, of which 51 were waited for; matrix products, arithmetic and copies ran while one was open for 26% of the time, Pallas kernels for 1%

profile of v1, /device:TPU:0, one launch (start us, length us, event | category | flops | bytes accessed | tf_op | source)
XLA Modules:
  0.0 904.1 jit_solution(8078509130845247238)
XLA Ops:
  91.0 8.0 collective-permute-done.4
  99.8 9.8 %collective-permute-done.2 = bf16[128,2048]{1,0:T(8,128)(2,1)S(1)} collective-permute-done((bf16[128,2048]{1,0:T(8,128)(2,1)S(1)}, bf16[128,2048]{1,0:T(8,128)(2,1)S(1)}, u32[]{:S(2)}, u32[]{:S(2)}) %collective-permute-start.2) | collective-permute-done | bytes 524320 | tf_op jit(solution)/shard_map/ppermute | solution.py:255
  127.9 12.9 %collective-permute-done.16 = bf16[128,2048]{1,0:T(8,128)(2,1)S(1)} collective-permute-done((bf16[128,2048]{1,0:T(8,128)(2,1)S(1)}, bf16[128,2048]{1,0:T(8,128)(2,1)S(1)}, u32[]{:S(2)}, u32[]{:S(2)}) %collective-permute-start.16) | collective-permute-done | bytes 524320 | tf_op jit(solution)/shard_map/ppermute | solution.py:255
  147.6 37.9 %collective-permute-done.42 = bf16[4,128,704]{1,2,0:T(8,128)(2,1)S(1)} collective-permute-done((bf16[4,128,704]{1,2,0:T(8,128)(2,1)S(1)}, bf16[4,128,704]{1,2,0:T(8,128)(2,1)S(1)}, u32[]{:S(2)}, u32[]{:S(2)}) %collective-permute-start.42) | collective-permute-done | bytes 720928 | tf_op jit(solution)/shard_map/ppermute | solution.py:255
  190.7 42.6 %collective-permute-done.54 = bf16[4,128,704]{1,2,0:T(8,128)(2,1)S(1)} collective-permute-done((bf16[4,128,704]{1,2,0:T(8,128)(2,1)S(1)}, bf16[4,128,704]{1,2,0:T(8,128)(2,1)S(1)}, u32[]{:S(2)}, u32[]{:S(2)}) %collective-permute-start.54) | collective-permute-done | bytes 720928 | tf_op jit(solution)/shard_map/ppermute | solution.py:255
  237.8 27.0 %collective-permute-done.48 = bf16[4,128,704]{1,2,0:T(8,128)(2,1)S(1)} collective-permute-done((bf16[4,128,704]{1,2,0:T(8,128)(2,1)S(1)}, bf16[4,128,704]{1,2,0:T(8,128)(2,1)S(1)}, u32[]{:S(2)}, u32[]{:S(2)}) %collective-permute-start.48) | collective-permute-done | bytes 720928 | tf_op jit(solution)/shard_map/ppermute | solution.py:255
  271.7 29.0 %collective-permute-done.49 = bf16[4,128,704]{1,2,0:T(8,128)(2,1)S(1)} collective-permute-done((bf16[4,128,704]{1,2,0:T(8,128)(2,1)S(1)}, bf16[4,128,704]{1,2,0:T(8,128)(2,1)S(1)}, u32[]{:S(2)}, u32[]{:S(2)}) %collective-permute-start.49) | collective-permute-done | bytes 720928 | tf_op jit(solution)/shard_map/ppermute | solution.py:255
  302.2 13.6 %collective-permute-done.11 = bf16[4,128,768]{2,1,0:T(8,128)(2,1)S(1)} collective-permute-done((bf16[4,128,768]{2,1,0:T(8,128)(2,1)S(1)}, bf16[4,128,768]{2,1,0:T(8,128)(2,1)S(1)}, u32[]{:S(2)}, u32[]{:S(2)}) %collective-permute-start.11) | collective-permute-done | bytes 786464 | tf_op jit(solution)/shard_map/ppermute | solution.py:255
  318.7 7.8 fusion.28.pre_ref
  360.8 7.5 reshape.366
  402.0 7.7 collective-permute-done.32
  451.6 7.7 reshape.382
  484.2 7.7 reshape.381
  501.0 7.9 reshape.380
  531.3 9.4 %collective-permute-done.76 = bf16[128,2048]{1,0:T(8,128)(2,1)S(1)} collective-permute-done((bf16[128,2048]{1,0:T(8,128)(2,1)S(1)}, bf16[128,2048]{1,0:T(8,128)(2,1)S(1)}, u32[]{:S(2)}, u32[]{:S(2)}) %collective-permute-start.76) | collective-permute-done | bytes 524320 | tf_op jit(solution)/shard_map/ppermute | solution.py:255
  544.2 7.6 collective-permute-done.58
  552.2 10.2 %collective-permute-done.62 = bf16[128,2048]{1,0:T(8,128)(2,1)S(1)} collective-permute-done((bf16[128,2048]{1,0:T(8,128)(2,1)S(1)}, bf16[128,2048]{1,0:T(8,128)(2,1)S(1)}, u32[]{:S(2)}, u32[]{:S(2)}) %collective-permute-start.62) | collective-permute-done | bytes 524320 | tf_op jit(solution)/shard_map/ppermute | solution.py:255
  594.9 14.1 %collective-permute-done.113 = bf16[2,2,1,2,128,704]{4,5,3,2,1,0:T(8,128)(2,1)} collective-permute-done((bf16[2,2,1,2,128,704]{4,5,3,2,1,0:T(8,128)(2,1)}, bf16[2,2,1,2,128,704]{4,5,3,2,1,0:T(8,128)(2,1)}, u32[]{:S(2)}, u32[]{:S(2)}) %collective-permute-start.113) | collective-permute-done | bytes 1441824 | tf_op jit(solution)/shard_map/ppermute | solution.py:255
  611.9 27.7 %collective-permute-done.108 = bf16[2,2,1,2,128,704]{4,5,3,2,1,0:T(8,128)(2,1)} collective-permute-done((bf16[2,2,1,2,128,704]{4,5,3,2,1,0:T(8,128)(2,1)}, bf16[2,2,1,2,128,704]{4,5,3,2,1,0:T(8,128)(2,1)}, u32[]{:S(2)}, u32[]{:S(2)}) %collective-permute-start.108) | collective-permute-done | bytes 1441824 | tf_op jit(solution)/shard_map/ppermute | solution.py:255
  679.1 57.5 %collective-permute-done.128 = f32[2,256]{1,0:T(2,128)S(1)} collective-permute-done((f32[2,256]{1,0:T(2,128)S(1)}, f32[2,256]{1,0:T(2,128)S(1)}, u32[]{:S(2)}, u32[]{:S(2)}) %collective-permute-start.128) | collective-permute-done | bytes 2080 | tf_op jit(solution)/shard_map/ppermute | solution.py:255
  755.5 10.6 %collective-permute-done.122 = bf16[128,704]{0,1:T(8,128)(2,1)S(1)} collective-permute-done((bf16[128,704]{0,1:T(8,128)(2,1)S(1)}, bf16[128,704]{0,1:T(8,128)(2,1)S(1)}, u32[]{:S(2)}, u32[]{:S(2)}) %collective-permute-start.122) | collective-permute-done | bytes 180256 | tf_op jit(solution)/shard_map/ppermute | solution.py:255
  802.6 11.4 %collective-permute-done.97 = bf16[128,2048]{1,0:T(8,128)(2,1)S(1)} collective-permute-done((bf16[128,2048]{1,0:T(8,128)(2,1)S(1)}, bf16[128,2048]{1,0:T(8,128)(2,1)S(1)}, u32[]{:S(2)}, u32[]{:S(2)}) %collective-permute-start.97) | collective-permute-done | bytes 524320 | tf_op jit(solution)/shard_map/ppermute | solution.py:255
  826.1 12.6 %collective-permute-done.106 = bf16[128,2048]{1,0:T(8,128)(2,1)} collective-permute-done((bf16[128,2048]{1,0:T(8,128)(2,1)}, bf16[128,2048]{1,0:T(8,128)(2,1)}, u32[]{:S(2)}, u32[]{:S(2)}) %collective-permute-start.106) | collective-permute-done | bytes 524320 | tf_op jit(solution)/shard_map/ppermute | solution.py:255
  849.8 33.3 %collective-permute-done.100 = bf16[1,2,1,2,128,768]{5,4,3,2,1,0:T(8,128)(2,1)S(1)} collective-permute-done((bf16[1,2,1,2,128,768]{5,4,3,2,1,0:T(8,128)(2,1)S(1)}, bf16[1,2,1,2,128,768]{5,4,3,2,1,0:T(8,128)(2,1)S(1)}, u32[]{:S(2)}, u32[]{:S(2)}) %collective-permute-start.100) | collective-permute-done | bytes 786464 | tf_op jit(solution)/shard_map/ppermute | solution.py:255
  (757 shorter events, 476.4 us)
Async XLA Ops:
  12.5 72.0 %collective-permute-start.6 = (bf16[128,768]{1,0:T(8,128)(2,1)}, bf16[128,768]{1,0:T(8,128)(2,1)}, u32[]{:S(2)}, u32[]{:S(2)}) collective-permute-start(bf16[128,768]{1,0:T(8,128)(2,1)} %bitcast.19), channel_id=1, source_target_pairs={{0,2},{2,0},{4,6},{6,4},{8,10},{10,8},{12,14},{14,12},{16,18},{18,... | collective-permute-start | bytes 589832 | tf_op jit(solution)/shard_map/ppermute | solution.py:255
  15.2 69.5 %collective-permute-start.7 = (bf16[128,768]{1,0:T(8,128)(2,1)}, bf16[128,768]{1,0:T(8,128)(2,1)}, u32[]{:S(2)}, u32[]{:S(2)}) collective-permute-start(bf16[128,768]{1,0:T(8,128)(2,1)} %bitcast.20), channel_id=1, source_target_pairs={{0,8},{2,10},{4,12},{6,14},{8,0},{10,2},{12,4},{14,6},{16,24},{18,... | collective-permute-start | bytes 589832 | tf_op jit(solution)/shard_map/ppermute | solution.py:255
  114.9 70.6 %collective-permute-start.42 = (bf16[4,128,704]{1,2,0:T(8,128)(2,1)S(1)}, bf16[4,128,704]{1,2,0:T(8,128)(2,1)S(1)}, u32[]{:S(2)}, u32[]{:S(2)}) collective-permute-start(bf16[4,128,704]{1,2,0:T(8,128)(2,1)S(1)} %pad_maximum_fusion.16), channel_id=1, source_target_pairs={{0,16},{2,18},{4,20},{6,22},{8,24},{10,26},{12,28},{14,30},{16,0},... | collective-permute-start | bytes 2162696 | tf_op jit(solution)/shard_map/ppermute | solution.py:255
  119.3 68.1 %collective-permute-start.41 = (bf16[4,128,704]{1,2,0:T(8,128)(2,1)S(1)}, bf16[4,128,704]{1,2,0:T(8,128)(2,1)S(1)}, u32[]{:S(2)}, u32[]{:S(2)}) collective-permute-start(bf16[4,128,704]{1,2,0:T(8,128)(2,1)S(1)} %pad_maximum_fusion.16), channel_id=1, source_target_pairs={{0,4},{2,6},{4,0},{6,2},{8,12},{10,14},{12,8},{14,10},{16,20},{18,... | collective-permute-start | bytes 2162696 | tf_op jit(solution)/shard_map/ppermute | solution.py:255
  143.1 90.2 %collective-permute-start.54 = (bf16[4,128,704]{1,2,0:T(8,128)(2,1)S(1)}, bf16[4,128,704]{1,2,0:T(8,128)(2,1)S(1)}, u32[]{:S(2)}, u32[]{:S(2)}) collective-permute-start(bf16[4,128,704]{1,2,0:T(8,128)(2,1)S(1)} %pad_maximum_fusion.18), channel_id=1, source_target_pairs={{0,16},{2,18},{4,20},{6,22},{8,24},{10,26},{12,28},{14,30},{16,0},... | collective-permute-start | bytes 2162696 | tf_op jit(solution)/shard_map/ppermute | solution.py:255
  146.0 120.3 %collective-permute-start.53 = (bf16[4,128,704]{1,2,0:T(8,128)(2,1)S(1)}, bf16[4,128,704]{1,2,0:T(8,128)(2,1)S(1)}, u32[]{:S(2)}, u32[]{:S(2)}) collective-permute-start(bf16[4,128,704]{1,2,0:T(8,128)(2,1)S(1)} %pad_maximum_fusion.18), channel_id=1, source_target_pairs={{0,4},{2,6},{4,0},{6,2},{8,12},{10,14},{12,8},{14,10},{16,20},{18,... | collective-permute-start | bytes 2162696 | tf_op jit(solution)/shard_map/ppermute | solution.py:255
  185.6 81.3 %collective-permute-start.10 = (bf16[4,128,768]{2,1,0:T(8,128)(2,1)S(1)}, bf16[4,128,768]{2,1,0:T(8,128)(2,1)S(1)}, u32[]{:S(2)}, u32[]{:S(2)}) collective-permute-start(bf16[4,128,768]{2,1,0:T(8,128)(2,1)S(1)} %pad_maximum_fusion.14), channel_id=1, source_target_pairs={{0,16},{2,18},{4,20},{6,22},{8,24},{10,26},{12,28},{14,30},{16,0},... | collective-permute-start | bytes 2359304 | tf_op jit(solution)/shard_map/ppermute | solution.py:255
  185.6 51.5 %collective-permute-start.43 = (bf16[4,128,704]{1,2,0:T(8,128)(2,1)S(1)}, bf16[4,128,704]{1,2,0:T(8,128)(2,1)S(1)}, u32[]{:S(2)}, u32[]{:S(2)}) collective-permute-start(bf16[4,128,704]{1,2,0:T(8,128)(2,1)S(1)} %collective-permute-done.42), channel_id=1, source_target_pairs={{0,4},{2,6},{4,0},{6,2},{8,12},{10,14},{12,8},{14,10},{16,20},{18,... | collective-permute-start | bytes 2162696 | tf_op jit(solution)/shard_map/ppermute | solution.py:255
  187.5 77.3 %collective-permute-start.48 = (bf16[4,128,704]{1,2,0:T(8,128)(2,1)S(1)}, bf16[4,128,704]{1,2,0:T(8,128)(2,1)S(1)}, u32[]{:S(2)}, u32[]{:S(2)}) collective-permute-start(bf16[4,128,704]{1,2,0:T(8,128)(2,1)S(1)} %pad_maximum_fusion.17), channel_id=1, source_target_pairs={{0,16},{2,18},{4,20},{6,22},{8,24},{10,26},{12,28},{14,30},{16,0},... | collective-permute-start | bytes 2162696 | tf_op jit(solution)/shard_map/ppermute | solution.py:255
  266.8 49.0 %collective-permute-start.11 = (bf16[4,128,768]{2,1,0:T(8,128)(2,1)S(1)}, bf16[4,128,768]{2,1,0:T(8,128)(2,1)S(1)}, u32[]{:S(2)}, u32[]{:S(2)}) collective-permute-start(bf16[4,128,768]{2,1,0:T(8,128)(2,1)S(1)} %collective-permute-done.10), channel_id=1, source_target_pairs={{0,4},{2,6},{4,0},{6,2},{8,12},{10,14},{12,8},{14,10},{16,20},{18,... | collective-permute-start | bytes 2359304 | tf_op jit(solution)/shard_map/ppermute | solution.py:255
  466.1 50.5 %collective-permute-start.59 = (bf16[128,2048]{1,0:T(8,128)(2,1)}, bf16[128,2048]{1,0:T(8,128)(2,1)}, u32[]{:S(2)}, u32[]{:S(2)}) collective-permute-start(bf16[128,2048]{1,0:T(8,128)(2,1)} %dynamic-slice_bitcast_fusion.9), channel_id=1, source_target_pairs={{0,1},{1,0},{2,3},{3,2},{4,5},{5,4},{6,7},{7,6},{8,9},{9,8},{10,11... | collective-permute-start | bytes 1572872 | tf_op jit(solution)/shard_map/ppermute | solution.py:258
  466.1 52.0 %collective-permute-start.61 = (bf16[128,2048]{1,0:T(8,128)(2,1)}, bf16[128,2048]{1,0:T(8,128)(2,1)}, u32[]{:S(2)}, u32[]{:S(2)}) collective-permute-start(bf16[128,2048]{1,0:T(8,128)(2,1)} %dynamic-slice_bitcast_fusion.8), channel_id=1, source_target_pairs={{0,1},{1,0},{2,3},{3,2},{4,5},{5,4},{6,7},{7,6},{8,9},{9,8},{10,11... | collective-permute-start | bytes 1572872 | tf_op jit(solution)/shard_map/ppermute | solution.py:258
  519.6 71.1 %collective-permute-start.118 = (bf16[2,2,1,2,128,704]{4,5,3,2,1,0:T(8,128)(2,1)}, bf16[2,2,1,2,128,704]{4,5,3,2,1,0:T(8,128)(2,1)}, u32[]{:S(2)}, u32[]{:S(2)}) collective-permute-start(bf16[2,2,1,2,128,704]{4,5,3,2,1,0:T(8,128)(2,1)} %copy.264), channel_id=1, source_target_pairs={{0,4},{2,6},{4,0},{6,2},{8,12},{10,14},{12,8},{14,10},{16,20},{18,... | collective-permute-start | bytes 4325384 | tf_op jit(solution)/shard_map/ppermute | solution.py:255
  575.9 63.6 %collective-permute-start.108 = (bf16[2,2,1,2,128,704]{4,5,3,2,1,0:T(8,128)(2,1)}, bf16[2,2,1,2,128,704]{4,5,3,2,1,0:T(8,128)(2,1)}, u32[]{:S(2)}, u32[]{:S(2)}) collective-permute-start(bf16[2,2,1,2,128,704]{4,5,3,2,1,0:T(8,128)(2,1)} %copy.260), channel_id=1, source_target_pairs={{0,4},{2,6},{4,0},{6,2},{8,12},{10,14},{12,8},{14,10},{16,20},{18,... | collective-permute-start | bytes 4325384 | tf_op jit(solution)/shard_map/ppermute | solution.py:255
  584.4 61.2 %collective-permute-start.80 = (bf16[128,2048]{1,0:T(8,128)(2,1)}, bf16[128,2048]{1,0:T(8,128)(2,1)}, u32[]{:S(2)}, u32[]{:S(2)}) collective-permute-start(bf16[128,2048]{1,0:T(8,128)(2,1)} %get-tuple-element.127), channel_id=1, source_target_pairs={{0,8},{2,10},{4,12},{6,14},{8,0},{10,2},{12,4},{14,6},{16,24},{18,... | collective-permute-start | bytes 1572872 | tf_op jit(solution)/shard_map/ppermute | solution.py:255
  587.2 58.5 %collective-permute-start.78 = (bf16[128,2048]{1,0:T(8,128)(2,1)}, bf16[128,2048]{1,0:T(8,128)(2,1)}, u32[]{:S(2)}, u32[]{:S(2)}) collective-permute-start(bf16[128,2048]{1,0:T(8,128)(2,1)} %get-tuple-element.127), channel_id=1, source_target_pairs={{0,2},{2,0},{4,6},{6,4},{8,10},{10,8},{12,14},{14,12},{16,18},{18,... | collective-permute-start | bytes 1572872 | tf_op jit(solution)/shard_map/ppermute | solution.py:255
  590.6 56.9 %collective-permute-start.82 = (bf16[128,2048]{1,0:T(8,128)(2,1)}, bf16[128,2048]{1,0:T(8,128)(2,1)S(1)}, u32[]{:S(2)}, u32[]{:S(2)}) collective-permute-start(bf16[128,2048]{1,0:T(8,128)(2,1)} %get-tuple-element.127), channel_id=1, source_target_pairs={{0,10},{2,8},{4,14},{6,12},{8,2},{10,0},{12,6},{14,4},{16,26},{18,... | collective-permute-start | bytes 1572872 | tf_op jit(solution)/shard_map/ppermute | solution.py:255
  639.6 104.7 %collective-permute-start.119 = (bf16[1,2,1,2,128,704]{4,5,3,2,1,0:T(8,128)(2,1)}, bf16[1,2,1,2,128,704]{4,5,3,2,1,0:T(8,128)(2,1)}, u32[]{:S(2)}, u32[]{:S(2)}) collective-permute-start(bf16[1,2,1,2,128,704]{4,5,3,2,1,0:T(8,128)(2,1)} %dynamic-slice_convert_fusion.1), channel_id=1, source_target_pairs={{0,16},{2,18},{4,20},{6,22},{8,24},{10,26},{12,28},{14,30},{16,0},... | collective-permute-start | bytes 2162696 | tf_op jit(solution)/shard_map/ppermute | solution.py:255
  645.7 101.0 %collective-permute-start.114 = (bf16[1,2,1,2,128,704]{4,5,3,2,1,0:T(8,128)(2,1)}, bf16[1,2,1,2,128,704]{4,5,3,2,1,0:T(8,128)(2,1)}, u32[]{:S(2)}, u32[]{:S(2)}) collective-permute-start(bf16[1,2,1,2,128,704]{4,5,3,2,1,0:T(8,128)(2,1)} %dynamic-slice_convert_fusion.2), channel_id=1, source_target_pairs={{0,16},{2,18},{4,20},{6,22},{8,24},{10,26},{12,28},{14,30},{16,0},... | collective-permute-start | bytes 2162696 | tf_op jit(solution)/shard_map/ppermute | solution.py:255
  647.5 103.3 %collective-permute-start.109 = (bf16[1,2,1,2,128,704]{4,5,3,2,1,0:T(8,128)(2,1)}, bf16[1,2,1,2,128,704]{4,5,3,2,1,0:T(8,128)(2,1)}, u32[]{:S(2)}, u32[]{:S(2)}) collective-permute-start(bf16[1,2,1,2,128,704]{4,5,3,2,1,0:T(8,128)(2,1)} %dynamic-slice_convert_fusion.3), channel_id=1, source_target_pairs={{0,16},{2,18},{4,20},{6,22},{8,24},{10,26},{12,28},{14,30},{16,0},... | collective-permute-start | bytes 2162696 | tf_op jit(solution)/shard_map/ppermute | solution.py:255
  675.0 61.6 %collective-permute-start.128 = (f32[2,256]{1,0:T(2,128)S(1)}, f32[2,256]{1,0:T(2,128)S(1)}, u32[]{:S(2)}, u32[]{:S(2)}) collective-permute-start(f32[2,256]{1,0:T(2,128)S(1)} %copy-done.112), channel_id=1, source_target_pairs={{0,16},{2,18},{4,20},{6,22},{8,24},{10,26},{12,28},{14,30},{16,0},... | collective-permute-start | bytes 6152 | tf_op jit(solution)/shard_map/ppermute | solution.py:255
  739.0 52.1 %collective-permute-start.105 = (bf16[1,128,2048]{2,1,0:T(8,128)(2,1)}, bf16[1,128,2048]{2,1,0:T(8,128)(2,1)}, u32[]{:S(2)}, u32[]{:S(2)}) collective-permute-start(bf16[1,128,2048]{2,1,0:T(8,128)(2,1)} %constant_dynamic-slice_fusion.21), channel_id=1, source_target_pairs={{0,16},{2,18},{4,20},{6,22},{8,24},{10,26},{12,28},{14,30},{16,0},... | collective-permute-start | bytes 1572872 | tf_op jit(solution)/shard_map/ppermute | solution.py:255
  791.1 53.4 %collective-permute-start.99 = (bf16[2,2,1,2,128,768]{5,4,3,2,1,0:T(8,128)(2,1)}, bf16[2,2,1,2,128,768]{5,4,3,2,1,0:T(8,128)(2,1)}, u32[]{:S(2)}, u32[]{:S(2)}) collective-permute-start(bf16[2,2,1,2,128,768]{5,4,3,2,1,0:T(8,128)(2,1)} %constant_dynamic-slice_fusion.22), channel_id=1, source_target_pairs={{0,4},{2,6},{4,0},{6,2},{8,12},{10,14},{12,8},{14,10},{16,20},{18,... | collective-permute-start | bytes 4718600 | tf_op jit(solution)/shard_map/ppermute | solution.py:255
  848.5 47.4 %collective-permute-start.98 = (f32[128,2048]{1,0:T(8,128)S(1)}, f32[128,2048]{1,0:T(8,128)S(1)}, u32[]{:S(2)}, u32[]{:S(2)}) collective-permute-start(f32[128,2048]{1,0:T(8,128)S(1)} %subtract_add_fusion), channel_id=1, source_target_pairs={{0,1},{1,0},{2,3},{3,2},{4,5},{5,4},{6,7},{7,6},{8,9},{9,8},{10,11... | collective-permute-start | bytes 3145736 | tf_op jit(solution)/shard_map/ppermute | solution.py:258
  (228 other events, 4707.1 us)

commit v2 on v1

--- a/solution.py
+++ b/solution.py
@@ -211,6 +211,332 @@
     )(pre, state, incoming, aux, par)
 
 
+MESH = pl.DeviceIdType.MESH
+
+
+class Copies:
+    def __init__(self, send, recv, local):
+        self.send, self.recv, self.local = send, recv, local
+        self.n_remote = self.n_local = 0
+        self.open = []
+
+    def remote(self, src, dst, device):
+        k = self.n_remote
+        self.n_remote += 1
+        copy = pltpu.make_async_remote_copy(
+            src_ref=src,
+            dst_ref=dst,
+            send_sem=self.send.at[k],
+            recv_sem=self.recv.at[k],
+            device_id=device,
+            device_id_type=MESH,
+        )
+        copy.start()
+        self.open.append(copy.wait_send)
+        return copy
+
+    def here(self, src, dst, keep=False):
+        k = self.n_local
+        self.n_local += 1
+        copy = pltpu.make_async_copy(src, dst, self.local.at[k])
+        copy.start()
+        if keep:
+            self.open.append(copy.wait)
+        return copy
+
+    def close(self):
+        assert self.n_remote <= self.send.shape[0] and self.n_local <= self.local.shape[0]
+        for wait in self.open:
+            wait()
+
+
+def position():
+    me = lax.axis_index("dp")
+    t = lax.axis_index("tensor")
+    zf, zn, y, x = me // 8, (me // 4) % 2, (me // 2) % 2, me % 2
+    to_x, to_zn = 1 - 2 * x, 4 - 8 * zn
+    group = [None, (me + to_x, t), (me + to_zn, t), (me + to_x + to_zn, t)]
+    q = [zn * 2 + x, zn * 2 + 1 - x, (1 - zn) * 2 + x, (1 - zn) * 2 + 1 - x]
+    far = (me + 8 - 16 * zf, t)
+    side = (me + 2 - 4 * y, t)
+    core = (me, 1 - t)
+    return me, t, (zf, zn, y, x), q, group, far, side, core
+
+
+def meet(devices):
+    barrier = pltpu.get_barrier_semaphore()
+    for device in devices:
+        pl.semaphore_signal(barrier, inc=1, device_id=device, device_id_type=MESH)
+    pl.semaphore_wait(barrier, len(devices))
+
+
+def fold_lanes(values):
+    width = values.shape[1]
+    if width % 128:
+        return values
+    total = values[:, :128]
+    for i in range(128, width, 128):
+        total = total + values[:, i : i + 128]
+    return total
+
+
+def front_kernel(
+    s_mix, s_out, s_g, s_u, s_d, n1_own, go_own, aux_own, par, inp, gain2,
+    o_mix, o_out, o_g, o_u, o_d, o_n1, o_go, o_n2, o_pre, o_state, o_raw, o_res, o_mo, o_sc, o_aux,
+    w_mix, w_out, out2, n1, aux, pre, state, raw, part, core_in, half, peer_in,
+    sq, sq_core, sq_half, sq_peer, res, mo, sc, n2, decay, add,
+    send, recv, local, core_send, core_recv, sqc_send, sqc_recv,
+):
+    me, t, (zf, zn, y, x), q, group, far, side, core = position()
+    share, width = inp.shape
+    rows = 2 * share
+    block = s_out.shape[0]
+    feat = par.shape[1]
+    link = Copies(send, recv, local)
+    meet(group[1:] + [far, side, core])
+
+    def at(start, size, unit):
+        return pl.ds(pl.multiple_of(start, unit), size)
+
+    def pair(fz, c, fy):
+        return at(fz * (8 * block) + c * (4 * block) + fy * (2 * block), 2 * block, 2 * block)
+
+    mine = at(me * block, block, block)
+
+    def row(r, tt):
+        return at(r * rows + tt * share, share, share)
+
+    mix_in = [link.remote(s_mix.at[q[r]], w_mix.at[mine], group[r]) for r in (1, 2, 3)]
+    mix_own = link.here(s_mix.at[q[0]], w_mix.at[mine])
+    side_out = link.remote(s_out, out2.at[y], side)
+    own_out = link.here(s_out, out2.at[y])
+    aux_in = [link.remote(aux_own, aux.at[r], group[r]) for r in (1, 2, 3)]
+    aux_mine = link.here(aux_own, aux.at[0])
+    n1_in = [link.remote(n1_own.at[at(t * share, share, share)], n1.at[row(r, t)], group[r]) for r in (1, 2, 3)]
+    n1_mine = link.here(n1_own, n1.at[pl.ds(0, rows)])
+    shards = ((s_g, o_g), (s_u, o_u), (s_d, o_d))
+    ffn_in, ffn_own = [], []
+    for s, o in shards:
+        ffn_in += [link.remote(s.at[q[r]], o.at[:, mine], group[r]) for r in (1, 2, 3)]
+        ffn_own.append(link.here(s.at[q[0]], o.at[:, mine]))
+
+    mix_own.wait()
+    for c in mix_in:
+        c.wait_recv()
+    far_mix = [link.remote(w_mix.at[pair(zf, c, y)], w_mix.at[pair(zf, c, y)], far) for c in (0, 1)]
+    side_mix = [link.remote(w_mix.at[pair(zf, c, y)], w_mix.at[pair(zf, c, y)], side) for c in (0, 1)]
+    side_out.wait_recv()
+    own_out.wait()
+    far_out = link.remote(out2.at[t], w_out.at[at(zf * block, block, block)], far)
+    here_out = link.here(out2.at[t], w_out.at[at(zf * block, block, block)])
+    n1_core = []
+    for i, r in enumerate((1, 2, 3)):
+        n1_in[i].wait_recv()
+        n1_core.append(link.remote(n1.at[row(r, t)], n1.at[row(r, t)], core))
+    for c in (0, 1):
+        far_mix[c].wait_recv()
+        side_mix.append(link.remote(w_mix.at[pair(1 - zf, c, y)], w_mix.at[pair(1 - zf, c, y)], side))
+
+    for c in ffn_own:
+        c.wait()
+    for c in ffn_in:
+        c.wait_recv()
+    far_ffn, side_ffn = [], []
+    for s, o in shards:
+        far_ffn.append([link.remote(o.at[:, pair(zf, c, y)], o.at[:, pair(zf, c, y)], far) for c in (0, 1)])
+    for s, o in shards:
+        side_ffn += [link.remote(o.at[:, pair(zf, c, y)], o.at[:, pair(zf, c, y)], side) for c in (0, 1)]
+
+    def forward_ffn(i):
+        o = shards[i][1]
+        for c in (0, 1):
+            far_ffn[i][c].wait_recv()
+            side_ffn.append(link.remote(o.at[:, pair(1 - zf, c, y)], o.at[:, pair(1 - zf, c, y)], side))
+
+    go_in = [link.remote(go_own, o_go.at[row(r, t)], group[r]) for r in (1, 2, 3)]
+    go_core = [link.remote(go_own, o_go.at[row(0, t)], core)]
+    link.here(go_own, o_go.at[row(0, t)], keep=True)
+
+    n1_mine.wait()
+    aux_mine.wait()
+    for c in side_mix + n1_core + aux_in + [far_out]:
+        c.wait_recv()
+    here_out.wait()
+
+    def core_copy(r):
+        return pltpu.make_async_remote_copy(
+            src_ref=part.at[row(r, 1 - t)],
+            dst_ref=core_in.at[at(r * share, share, share)],
+            send_sem=core_send.at[r],
+            recv_sem=core_recv.at[r],
+            device_id=core,
+            device_id_type=MESH,
+        )
+
+    def sq_copy(r):
+        return pltpu.make_async_remote_copy(
+            src_ref=sq.at[row(r, 1 - t)],
+            dst_ref=sq_core.at[at(r * share, share, share)],
+            send_sem=sqc_send.at[r],
+            recv_sem=sqc_recv.at[r],
+            device_id=core,
+            device_id_type=MESH,
+        )
+
+    bound = par[0:1, :]
+    gain = par[1:2, :]
+
+    def piece(i, carry):
+        r = 3 - i
+        here = at(r * rows, rows, rows)
+        pre[here, :] = jnp.dot(n1[here, :], w_mix[...], preferred_element_type=f32)
+        columns = aux[r].T
+        valid = columns[:, 0:1]
+        keep = columns[:, 1:2]
+        forget = bound + (1.0 - bound) * jax.nn.sigmoid(pre[here, feat : 2 * feat])
+        input_pre = pre[here, 0:feat]
+        add[...] = input_pre * jax.nn.sigmoid(input_pre) * (1.0 - forget) * valid
+        decay[...] = forget * keep
+        scan_rows(decay, add, state.at[here, :], False)
+        held = state[here, :]
+        outgate_pre = pre[here, 2 * feat :]
+        raw[here, :] = (held * gain * (outgate_pre * jax.nn.sigmoid(outgate_pre))).astype(bf16)
+        sq[here, :] = fold_lanes(held * held)
+        part[here, :] = jnp.dot(raw[here, :], w_out[...], preferred_element_type=f32).astype(bf16)
+        core_copy(r).start()
+        sq_copy(r).start()
+        return carry
+
+    lax.fori_loop(0, 4, piece, 0)
+
+    link.here(w_mix, o_mix, keep=True)
+    link.here(w_out, o_out, keep=True)
+    link.here(n1, o_n1, keep=True)
+    link.here(pre, o_pre, keep=True)
+    link.here(state, o_state, keep=True)
+    link.here(raw, o_raw, keep=True)
+    link.here(aux, o_aux, keep=True)
+
+    out_in, sq_in = [], []
+    for r in (3, 2, 1):
+        core_copy(r).wait()
+        sq_copy(r).wait()
+        to = at(r * share, share, share)
+        half[to, :] = (part[row(r, t), :].astype(f32) + core_in[to, :].astype(f32)).astype(bf16)
+        sq_half[to, :] = sq[row(r, t), :] + sq_core[to, :]
+        out_in.append(link.remote(half.at[to], peer_in.at[to], group[r]))
+        sq_in.append(link.remote(sq_half.at[to], sq_peer.at[to], group[r]))
+    core_copy(0).wait()
+    sq_copy(0).wait()
+    forward_ffn(0)
+    for c in out_in + sq_in:
+        c.wait_recv()
+    total_sq = sq[row(0, t), :] + sq_core[0:share, :]
+    for r in (1, 2, 3):
+        total_sq = total_sq + sq_peer[r * share : (r + 1) * share, :]
+    scale = lax.rsqrt(jnp.sum(total_sq, axis=1, keepdims=True) / width + epsilon)
+    sc[...] = jnp.broadcast_to(scale, sc.shape)
+    chunk = min(share, 16)
+
+    def finish(i, carry):
+        to = at(i * chunk, chunk, chunk)
+        total = part[at(t * share + i * chunk, chunk, chunk), :].astype(f32) + core_in[to, :].astype(f32)
+        for r in (1, 2, 3):
+            total = total + peer_in[at(r * share + i * chunk, chunk, chunk), :].astype(f32)
+        mixed = total * sc[to, 0:1]
+        value = inp[to, :] + mixed
+        mo[to, :] = mixed
+        res[to, :] = value
+        scale_two = lax.rsqrt(jnp.mean(value * value, axis=1, keepdims=True) + epsilon)
+        n2[to, :] = (value * scale_two * gain2[...]).astype(bf16)
+        return carry
+
+    lax.fori_loop(0, share // chunk, finish, 0)
+    n2_in = [link.remote(n2, o_n2.at[row(r, t)], group[r]) for r in (1, 2, 3)]
+    n2_core = [link.remote(n2, o_n2.at[row(0, t)], core)]
+    link.here(n2, o_n2.at[row(0, t)], keep=True)
+    link.here(res, o_res, keep=True)
+    link.here(mo, o_mo, keep=True)
+    link.here(sc, o_sc, keep=True)
+    for i, r in enumerate((1, 2, 3)):
+        go_in[i].wait_recv()
+        go_core.append(link.remote(o_go.at[row(r, t)], o_go.at[row(r, t)], core))
+    forward_ffn(1)
+    for i, r in enumerate((1, 2, 3)):
+        n2_in[i].wait_recv()
+        n2_core.append(link.remote(o_n2.at[row(r, t)], o_n2.at[row(r, t)], core))
+    forward_ffn(2)
+    for c in side_ffn + go_core + n2_core:
+        c.wait_recv()
+    link.close()
+
+
+def front(s_mix, s_out, s_g, s_u, s_d, n1_own, go_own, aux_own, par, inp, gain2):
+    share, width = inp.shape
+    rows, group_rows = 2 * share, 8 * share
+    feat, hid = par.shape[1], s_g.shape[1]
+    block = s_out.shape[0]
+    lanes = 128 if feat % 128 == 0 else feat
+    any_spec = pl.BlockSpec(memory_space=pl.ANY)
+    vmem_spec = pl.BlockSpec(memory_space=pltpu.VMEM)
+    made = jax.ShapeDtypeStruct
+    outs = [
+        made((width, 3 * feat), bf16),
+        made((feat, width), bf16),
+        made((hid, width), bf16),
+        made((hid, width), bf16),
+        made((hid, width), bf16),
+        made((group_rows, width), bf16),
+        made((group_rows, width), bf16),
+        made((group_rows, width), bf16),
+        made((group_rows, 3 * feat), f32),
+        made((group_rows, feat), f32),
+        made((group_rows, feat), bf16),
+        made((share, width), f32),
+        made((share, width), f32),
+        made((share, 128), f32),
+        made((4,) + aux_own.shape, f32),
+    ]
+    scratch = [
+        pltpu.VMEM((width, 3 * feat), bf16),
+        pltpu.VMEM((feat, width), bf16),
+        pltpu.VMEM((2, block, width), bf16),
+        pltpu.VMEM((group_rows, width), bf16),
+        pltpu.VMEM((4,) + aux_own.shape, f32),
+        pltpu.VMEM((group_rows, 3 * feat), f32),
+        pltpu.VMEM((group_rows, feat), f32),
+        pltpu.VMEM((group_rows, feat), bf16),
+        pltpu.VMEM((group_rows, width), bf16),
+        pltpu.VMEM((4 * share, width), bf16),
+        pltpu.VMEM((4 * share, width), bf16),
+        pltpu.VMEM((4 * share, width), bf16),
+        pltpu.VMEM((group_rows, lanes), f32),
+        pltpu.VMEM((4 * share, lanes), f32),
+        pltpu.VMEM((4 * share, lanes), f32),
+        pltpu.VMEM((4 * share, lanes), f32),
+        pltpu.VMEM((share, width), f32),
+        pltpu.VMEM((share, width), f32),
+        pltpu.VMEM((share, 128), f32),
+        pltpu.VMEM((share, width), bf16),
+        pltpu.VMEM((rows, feat), f32),
+        pltpu.VMEM((rows, feat), f32),
+        pltpu.SemaphoreType.DMA((68,)),
+        pltpu.SemaphoreType.DMA((68,)),
+        pltpu.SemaphoreType.DMA((24,)),
+    ] + [pltpu.SemaphoreType.DMA((4,))] * 4
+    return pl.pallas_call(
+        front_kernel,
+        in_specs=[any_spec] * 7 + [any_spec] + [vmem_spec] * 3,
+        out_specs=[any_spec] * len(outs),
+        out_shape=outs,
+        scratch_shapes=scratch,
+        compiler_params=pltpu.CompilerParams(
+            collective_id=1, has_side_effects=True, vmem_limit_bytes=56 << 20
+        ),
+        name="front",
+    )(s_mix, s_out, s_g, s_u, s_d, n1_own, go_own, aux_own, par, inp, gain2)
+
+
 def body(
     n_dp,
     n_t,
@@ -342,79 +668,78 @@
     inputs = tokens_in.astype(f32)
     scale_one = rms_scale(inputs)
     normed_mine = (inputs * scale_one * norm_gain).astype(bf16)
-    normed_half = my_half(normed_mine)
-    normed_parts = [normed_mine] + [
-        t_gather(swap(normed_half, tp_mask[r])).reshape(rows, width) for r in range(1, n_tp)
-    ]
-    where_from = jnp.concatenate([lengths, bucket])
-    masks = []
-    for r in range(n_tp):
-        got = where_from if r == 0 else swap(where_from, tp_mask[r])
-        masks.append(layout(got[: lengths.shape[0]], got[lengths.shape[0] :], rows))
-    valid_all = jnp.concatenate([m[0] for m in masks])
-    keep_all = jnp.concatenate([m[1] for m in masks])
-
+    inputs_half = my_half(inputs)
+    scale_one_half = my_half(scale_one)
     mix_shards = jnp.concatenate(
         [my_columns(w) for w in (input_proj, forget_proj, outgate_proj)], axis=-1
     )
-    mix_parts = weight_parts(mix_shards)
-    out_piece = output_proj
-    for b in own_bits:
-        out_piece = jnp.where(t_bit[b] == bit[b], out_piece, swap(out_piece, 1 << b))
-    out_pieces = [out_piece]
-    for b in reversed(free_bits):
-        out_pieces = out_pieces + [swap(v, 1 << b) for v in out_pieces]
-    out_full = jnp.concatenate(in_order(out_pieces, free_bits))
-
-    valid_mine = my_half(masks[0][0])
-    grad_out_rows = (cotangent.astype(f32) * valid_mine).astype(bf16)
-
-    hidden_cols = glu_gate.shape[1] // n_tp
-    split_cols = lambda w: w.reshape(block, n_tp, hidden_cols).transpose(1, 0, 2)
-    gate_parts = weight_parts(split_cols(glu_gate))
-    up_parts = weight_parts(split_cols(glu_up))
-    down_parts = weight_parts(glu_down.reshape(n_tp, hidden_cols, block).transpose(0, 2, 1))
-    grad_out_all = jnp.stack(tp_gather(grad_out_rows)).reshape(n_tp * rows, width)
-
-    normed_one = jnp.concatenate(normed_parts)
-    mix_full = weight_whole(mix_parts)
-    pre = matmul(normed_one, mix_full)
+    hid = glu_gate.shape[1] // n_tp
+    gate_shards = glu_gate.T.reshape(n_tp, hid, block)
+    up_shards = glu_up.T.reshape(n_tp, hid, block)
+    down_shards = glu_down.reshape(n_tp, hid, block)
     my_table = pick(my_columns(bound_table), q, 0)
-    bound_mine = bound_parts(my_table)[2]
-    gain_mine = pick(my_columns(mixer_gain), q, 0)
-    par = jnp.stack([bound_mine, gain_mine])
-    aux = jnp.concatenate([valid_all, keep_all], axis=1)
-    state, mix_raw, square = mixer_forward(pre, aux, par, rows)
-    out_parts = matmul(mix_raw, out_full).astype(bf16).reshape(n_tp, n_t, share, width)
-    square_parts = square.reshape(n_tp, n_t, share)
-    square_sum = tp_scatter([square_parts[r] for r in range(n_tp)], f32)
-    out_sum = tp_scatter([out_parts[r] for r in range(n_tp)], bf16)
-    scale_state = lax.rsqrt(square_sum / width + epsilon)[:, None]
-    mixed_out = out_sum * scale_state
-    inputs_half = my_half(inputs)
-    scale_one_half = my_half(scale_one)
-    residual = inputs_half + mixed_out
+    par = jnp.stack([bound_parts(my_table)[2], pick(my_columns(mixer_gain), q, 0)])
+    valid_own, keep_own = layout(lengths, bucket, rows)
+    grad_out_rows = (cotangent.astype(f32) * my_half(valid_own)).astype(bf16)
+    if n_dp == 16 and n_t == 2:
+        aux_own = jnp.concatenate([valid_own.T, keep_own.T, jnp.zeros((6, rows), f32)])
+        (
+            mix_full, out_full, gate_full, up_full, down_full, normed_one, grad_out_all, normed_two,
+            pre, state, mix_raw, residual, mixed_out, scale_lanes, aux_rows,
+        ) = front(
+            mix_shards, output_proj, gate_shards, up_shards, down_shards, normed_mine, grad_out_rows,
+            aux_own, par, inputs_half, ffn_gain[None, :],
+        )
+        scale_state = scale_lanes[:, :1]
+        aux = aux_rows[:, :2].transpose(0, 2, 1).reshape(n_tp * rows, 2)
+    else:
+        normed_half = my_half(normed_mine)
+        normed_parts = [normed_mine] + [
+            t_gather(swap(normed_half, tp_mask[r])).reshape(rows, width) for r in range(1, n_tp)
+        ]
+        normed_one = jnp.concatenate(normed_parts)
+        aux_own = jnp.concatenate([valid_own, keep_own], axis=1)
+        aux = jnp.concatenate([aux_own] + [swap(aux_own, tp_mask[r]) for r in range(1, n_tp)])
+        mix_full = weight_whole(weight_parts(mix_shards))
+        out_piece = output_proj
+        for b in own_bits:
+            out_piece = jnp.where(t_bit[b] == bit[b], out_piece, swap(out_piece, 1 << b))
+        out_pieces = [out_piece]
+        for b in reversed(free_bits):
+            out_pieces = out_pieces + [swap(v, 1 << b) for v in out_pieces]
+        out_full = jnp.concatenate(in_order(out_pieces, free_bits))
+        gate_full, up_full, down_full = (
+            weight_whole(weight_parts(w.transpose(0, 2, 1))).T
+            for w in (gate_shards, up_shards, down_shards)
+        )
+        grad_out_all = jnp.stack(tp_gather(grad_out_rows)).reshape(n_tp * rows, width)
+        pre = matmul(normed_one, mix_full)
+        state, mix_raw, square = mixer_forward(pre, aux, par, rows)
+        out_parts = matmul(mix_raw, out_full).astype(bf16).reshape(n_tp, n_t, share, width)
+        square_parts = square.reshape(n_tp, n_t, share)
+        square_sum = tp_scatter([square_parts[r] for r in range(n_tp)], f32)
+        out_sum = tp_scatter([out_parts[r] for r in range(n_tp)], bf16)
+        scale_state = lax.rsqrt(square_sum / width + epsilon)[:, None]
+        mixed_out = out_sum * scale_state
+        residual = inputs_half + mixed_out
+        normed_two_half = (residual * rms_scale(residual) * ffn_gain).astype(bf16)
+        normed_two = jnp.stack(tp_gather(normed_two_half)).reshape(n_tp * rows, width)
 
     scale_two = rms_scale(residual)
-    normed_two_half = (residual * scale_two * ffn_gain).astype(bf16)
-    normed_two = jnp.stack(tp_gather(normed_two_half)).reshape(n_tp * rows, width)
-    gate_full = weight_whole(gate_parts)
-    up_full = weight_whole(up_parts)
-    down_full = weight_whole(down_parts)
-    gate_pre = matmul(normed_two, gate_full)
-    up_pre = matmul(normed_two, up_full)
-    grad_hidden = matmul(grad_out_all, down_full)
+    gate_pre = cross_cols(normed_two, gate_full)
+    up_pre = cross_cols(normed_two, up_full)
+    grad_hidden = cross_cols(grad_out_all, down_full)
     gate_act = jax.nn.silu(gate_pre)
     hidden = (gate_act * up_pre).astype(bf16)
     grad_up = (grad_hidden * gate_act).astype(bf16)
     grad_gate = (grad_hidden * up_pre * silu_slope(gate_pre)).astype(bf16)
     grad_two_parts = (
-        (cross_cols(grad_gate, gate_full) + cross_cols(grad_up, up_full))
+        (matmul(grad_gate, gate_full) + matmul(grad_up, up_full))
         .astype(bf16)
         .reshape(n_tp, n_t, share, width)
     )
     grad_normed_two = tp_scatter([grad_two_parts[r] for r in range(n_tp)], bf16)
-    block_parts = cross_cols(hidden, down_full).astype(bf16).reshape(n_tp, n_t, share, width)
+    block_parts = matmul(hidden, down_full).astype(bf16).reshape(n_tp, n_t, share, width)
     block_out = (residual + tp_scatter([block_parts[r] for r in range(n_tp)], bf16)).astype(bf16)
     grad_down_t = jnp.stack(weight_back(cross_rows(grad_out_all, hidden).astype(bf16)))
     grad_w_gate = jnp.stack(weight_back(cross_rows(normed_two, grad_gate).astype(bf16)))
@@ -435,7 +760,7 @@
     row_all = jnp.stack(tp_gather(row_values)).transpose(0, 1, 3, 2).reshape(n_tp * rows, 2)
     grad_mix = jnp.stack(tp_gather(grad_mix_half)).reshape(n_tp * rows, width)
     grad_mixed = cross_cols(grad_mix, out_full)
-    aux_back = jnp.concatenate([valid_all, keep_all, row_all], axis=1)
+    aux_back = jnp.concatenate([aux, row_all], axis=1)
     grads, sums = mixer_backward(pre, state, grad_mixed, aux_back, par, rows)
     one_parts = cross_cols(grads, mix_full).astype(bf16).reshape(n_tp, n_t, share, width)
     grad_normed_one = tp_scatter([one_parts[r] for r in range(n_tp)], bf16)

time: 916 us -> 734 us (0.80)
  waiting for transfers between devices: 463 us -> 231 us
  Pallas kernels: 11.1 us -> 229 us
  starting transfers between devices: 118 us -> 54.9 us
  local copies, waits for them, and re-layouts: 151 us -> 93.5 us
  other arithmetic: 89.9 us -> 56.7 us
    ppermute x87 -> x43, waiting for transfers between devices: 458 us -> 229 us  [swap(): return lax.ppermute(values, 'dp', [(i, i ^ mask) for i in range(n_dp)])]
    pallas_call x1, Pallas kernels: 4.88 us -> 223 us  [front(): pl.pallas_call(front_kernel, in_specs=[any_spec] * 7 + [any_spec] + [vmem...]
    ppermute x87 -> x43, starting transfers between devices: 110 us -> 51.3 us  [swap(): return lax.ppermute(values, 'dp', [(i, i ^ mask) for i in range(n_dp)])]
    reshape x6 -> x1, local copies, waits for them, and re-layouts: 37.9 us -> 0.02 us  [body(): jnp.stack(tp_gather(row_values)).transpose(0, 1, 3, 2)]
    another operation x35 -> x1, other arithmetic: 18 us -> 0.56 us  [body(): jnp.stack([bound_parts(my_table)[2], pick(my_columns(mixer_gain), q, 0)])]
    dot_general x5 -> x3, matrix products: 22.2 us -> 13.1 us  [matmul(): return jnp.dot(first_op, second_op, preferred_element_type=f32)]
    unnamed x255 -> x190, local copies, waits for them, and re-layouts: 25.3 us -> 16.7 us
    squeeze x27 -> x15, local copies, waits for them, and re-layouts: 18.4 us -> 12.1 us  [pick(): return lax.dynamic_index_in_dim(values, index, axis, keepdims=False)]
  transfers between devices with their start and end apart: 131 -> 68, of which waited for: 51 -> 32; matrix products, arithmetic and copies ran while one was open for 26% -> 21% of each run, Pallas kernels for 1% -> 1%
where the time goes in v2:
time: 734 us; the launch traced here: 727 us
  waiting for transfers between devices  231 us (31%)
  Pallas kernels  229 us (31%)
  local copies, waits for them, and re-layouts  93.5 us (13%)
  matrix products  58.3 us (8%)
  other arithmetic  56.7 us (8%)
  starting transfers between devices  54.9 us (7%)
    ppermute x43, waiting for transfers between devices, swap(): return lax.ppermute(values, 'dp', [(i, i ^ mask) for i in range(n_dp)])  229 us
    pallas_call x1, Pallas kernels, front(): pl.pallas_call(front_kernel, in_specs=[any_spec] * 7 + [any_spec] + [vmem...  223 us
    ppermute x43, starting transfers between devices, swap(): return lax.ppermute(values, 'dp', [(i, i ^ mask) for i in range(n_dp)])  51.3 us
    dot_general x5, matrix products, cross_rows(): lax.dot_general(first_op, second_op, (((0,), (0,)), ((), ())), preferred_...  24.4 us
    reshape x3, local copies, waits for them, and re-layouts, weight_back(): grad = grad.reshape((2,) * depth + (block, cols))  22.2 us
    dot_general x5, matrix products, cross_cols(): lax.dot_general(first_op, second_op, (((1,), (1,)), ((), ())), preferred_...  20.8 us
    unnamed x190, local copies, waits for them, and re-layouts  16.7 us
  transfers between devices with their start and end apart: 68, of which 32 were waited for; matrix products, arithmetic and copies ran while one was open for 21% of the time, Pallas kernels for 1%

profile of v2, /device:TPU:0, one launch (start us, length us, event | category | flops | bytes accessed | tf_op | source)
XLA Modules:
  0.0 727.2 jit_solution(209013219473680423)
XLA Ops:
  27.3 222.8 %front.1 = (bf16[2048,768]{1,0:T(8,128)(2,1)}, bf16[256,2048]{1,0:T(8,128)(2,1)}, bf16[704,2048]{1,0:T(8,128)(2,1)}, bf16[704,2048]{1,0:T(8,128)(2,1)}, bf16[704...) custom-call(bf16[4,128,768]{2,1,0:T(8,128)(2,1)} %pad_maximum_fusion, ...), custom_call_target="tpu_custom_call" | custom-call | tf_op jit(solution)/shard_map/front/pallas_call | solution.py:527
  250.2 6.0 fusion.47
  259.4 5.4 multiply_convert_fusion
  264.9 4.1 convolution_convert_fusion
  275.1 5.0 fusion.49
  288.4 7.5 %convolution_convert_fusion.3 = bf16[2048,704]{0,1:T(8,128)(2,1)} fusion(bf16[1024,704]{0,1:T(8,128)(2,1)} %copy-done.88, bf16[1024,2048]{1,0:T(8,128)(2,1)} %get-tuple-element.35), kind=kOutput, calls=%fused_computation.5 | convolution fusion | flops 2954231808 | bytes 8519680 | tf_op jit(solution)/shard_map/dot_general | solution.py:38
  296.0 4.5 convolution_convert_fusion.4
  300.5 4.6 convolution_convert_fusion.5
  308.6 7.7 %reshape.355 = bf16[2,2,2,2,128,704]{4,3,2,1,0,5:T(2,128)(2,1)} reshape(bf16[2048,704]{0,1:T(8,128)(2,1)} %convolution_convert_fusion.3) | data formatting | bytes 5767168 | tf_op jit(solution)/shard_map/reshape | solution.py:647
  317.1 6.6 reshape.353
  323.8 7.9 %reshape.354 = bf16[2,2,2,2,128,704]{4,3,2,1,0,5:T(2,128)(2,1)} reshape(bf16[2048,704]{0,1:T(8,128)(2,1)} %convolution_convert_fusion.4) | data formatting | bytes 5767168 | tf_op jit(solution)/shard_map/reshape | solution.py:647
  331.6 5.6 constant_dynamic-slice_fusion.16
  375.7 10.6 %collective-permute-done.13 = bf16[128,2048]{1,0:T(8,128)(2,1)S(1)} collective-permute-done((bf16[128,2048]{1,0:T(8,128)(2,1)S(1)}, bf16[128,2048]{1,0:T(8,128)(2,1)S(1)}, u32[]{:S(2)}, u32[]{:S(2)}) %collective-permute-start.13) | collective-permute-done | bytes 524320 | tf_op jit(solution)/shard_map/ppermute | solution.py:581
  396.2 11.9 %collective-permute-done.6 = bf16[128,2048]{1,0:T(8,128)(2,1)S(1)} collective-permute-done((bf16[128,2048]{1,0:T(8,128)(2,1)S(1)}, bf16[128,2048]{1,0:T(8,128)(2,1)S(1)}, u32[]{:S(2)}, u32[]{:S(2)}) %collective-permute-start.6) | collective-permute-done | bytes 524320 | tf_op jit(solution)/shard_map/ppermute | solution.py:581
  437.1 24.2 %collective-permute-done.45 = bf16[2,2,1,2,128,704]{4,5,3,2,1,0:T(8,128)(2,1)} collective-permute-done((bf16[2,2,1,2,128,704]{4,5,3,2,1,0:T(8,128)(2,1)}, bf16[2,2,1,2,128,704]{4,5,3,2,1,0:T(8,128)(2,1)}, u32[]{:S(2)}, u32[]{:S(2)}) %collective-permute-start.45) | collective-permute-done | bytes 1441824 | tf_op jit(solution)/shard_map/ppermute | solution.py:581
  477.9 6.1 mixer_backward.1
  484.0 6.4 convolution_convert_fusion.2
  501.6 57.2 %collective-permute-done.65 = f32[2,256]{1,0:T(2,128)S(1)} collective-permute-done((f32[2,256]{1,0:T(2,128)S(1)}, f32[2,256]{1,0:T(2,128)S(1)}, u32[]{:S(2)}, u32[]{:S(2)}) %collective-permute-start.65) | collective-permute-done | bytes 2080 | tf_op jit(solution)/shard_map/ppermute | solution.py:581
  577.7 10.9 %collective-permute-done.59 = bf16[128,704]{0,1:T(8,128)(2,1)S(1)} collective-permute-done((bf16[128,704]{0,1:T(8,128)(2,1)S(1)}, bf16[128,704]{0,1:T(8,128)(2,1)S(1)}, u32[]{:S(2)}, u32[]{:S(2)}) %collective-permute-start.59) | collective-permute-done | bytes 180256 | tf_op jit(solution)/shard_map/ppermute | solution.py:581
  600.9 4.2 collective-permute-done.49
  616.0 7.2 collective-permute-done.30
  625.2 10.7 %collective-permute-done.34 = bf16[128,2048]{1,0:T(8,128)(2,1)S(1)} collective-permute-done((bf16[128,2048]{1,0:T(8,128)(2,1)S(1)}, bf16[128,2048]{1,0:T(8,128)(2,1)S(1)}, u32[]{:S(2)}, u32[]{:S(2)}) %collective-permute-start.34) | collective-permute-done | bytes 524320 | tf_op jit(solution)/shard_map/ppermute | solution.py:581
  647.4 13.2 %collective-permute-done.43 = bf16[128,2048]{1,0:T(8,128)(2,1)} collective-permute-done((bf16[128,2048]{1,0:T(8,128)(2,1)}, bf16[128,2048]{1,0:T(8,128)(2,1)}, u32[]{:S(2)}, u32[]{:S(2)}) %collective-permute-start.43) | collective-permute-done | bytes 524320 | tf_op jit(solution)/shard_map/ppermute | solution.py:581
  673.1 33.1 %collective-permute-done.37 = bf16[1,2,1,2,128,768]{5,4,3,2,1,0:T(8,128)(2,1)S(1)} collective-permute-done((bf16[1,2,1,2,128,768]{5,4,3,2,1,0:T(8,128)(2,1)S(1)}, bf16[1,2,1,2,128,768]{5,4,3,2,1,0:T(8,128)(2,1)S(1)}, u32[]{:S(2)}, u32[]{:S(2)}) %collective-permute-start.37) | collective-permute-done | bytes 786464 | tf_op jit(solution)/shard_map/ppermute | solution.py:581
  (481 shorter events, 240.1 us)
Async XLA Ops:
  272.9 79.1 %collective-permute-start.1 = (bf16[128,2048]{1,0:T(8,128)(2,1)}, bf16[128,2048]{1,0:T(8,128)(2,1)}, u32[]{:S(2)}, u32[]{:S(2)}) collective-permute-start(bf16[128,2048]{1,0:T(8,128)(2,1)} %dynamic-slice_bitcast_fusion.10), channel_id=1, source_target_pairs={{0,1},{1,0},{2,3},{3,2},{4,5},{5,4},{6,7},{7,6},{8,9},{9,8},{10,11... | collective-permute-start | bytes 1572872 | tf_op jit(solution)/shard_map/ppermute | solution.py:584
  273.7 87.4 %collective-permute-start.3 = (bf16[128,2048]{1,0:T(8,128)(2,1)}, bf16[128,2048]{1,0:T(8,128)(2,1)}, u32[]{:S(2)}, u32[]{:S(2)}) collective-permute-start(bf16[128,2048]{1,0:T(8,128)(2,1)} %dynamic-slice_bitcast_fusion.9), channel_id=1, source_target_pairs={{0,1},{1,0},{2,3},{3,2},{4,5},{5,4},{6,7},{7,6},{8,9},{9,8},{10,11... | collective-permute-start | bytes 1572872 | tf_op jit(solution)/shard_map/ppermute | solution.py:584
  275.1 88.7 %collective-permute-start.5 = (bf16[128,2048]{1,0:T(8,128)(2,1)}, bf16[128,2048]{1,0:T(8,128)(2,1)}, u32[]{:S(2)}, u32[]{:S(2)}) collective-permute-start(bf16[128,2048]{1,0:T(8,128)(2,1)} %dynamic-slice_bitcast_fusion.8), channel_id=1, source_target_pairs={{0,1},{1,0},{2,3},{3,2},{4,5},{5,4},{6,7},{7,6},{8,9},{9,8},{10,11... | collective-permute-start | bytes 1572872 | tf_op jit(solution)/shard_map/ppermute | solution.py:584
  286.9 66.8 %collective-permute-start.8 = (bf16[128,2048]{1,0:T(8,128)(2,1)}, bf16[128,2048]{1,0:T(8,128)(2,1)}, u32[]{:S(2)}, u32[]{:S(2)}) collective-permute-start(bf16[128,2048]{1,0:T(8,128)(2,1)} %dynamic-slice_bitcast_fusion.6), channel_id=1, source_target_pairs={{0,1},{1,0},{2,3},{3,2},{4,5},{5,4},{6,7},{7,6},{8,9},{9,8},{10,11... | collective-permute-start | bytes 1572872 | tf_op jit(solution)/shard_map/ppermute | solution.py:584
  288.2 67.2 %collective-permute-start.10 = (bf16[128,2048]{1,0:T(8,128)(2,1)}, bf16[128,2048]{1,0:T(8,128)(2,1)}, u32[]{:S(2)}, u32[]{:S(2)}) collective-permute-start(bf16[128,2048]{1,0:T(8,128)(2,1)} %dynamic-slice_bitcast_fusion.5), channel_id=1, source_target_pairs={{0,1},{1,0},{2,3},{3,2},{4,5},{5,4},{6,7},{7,6},{8,9},{9,8},{10,11... | collective-permute-start | bytes 1572872 | tf_op jit(solution)/shard_map/ppermute | solution.py:584
  365.3 63.5 %collective-permute-start.55 = (bf16[2,2,1,2,128,704]{4,5,3,2,1,0:T(8,128)(2,1)}, bf16[2,2,1,2,128,704]{4,5,3,2,1,0:T(8,128)(2,1)}, u32[]{:S(2)}, u32[]{:S(2)}) collective-permute-start(bf16[2,2,1,2,128,704]{4,5,3,2,1,0:T(8,128)(2,1)} %copy.243), channel_id=1, source_target_pairs={{0,4},{2,6},{4,0},{6,2},{8,12},{10,14},{12,8},{14,10},{16,20},{18,... | collective-permute-start | bytes 4325384 | tf_op jit(solution)/shard_map/ppermute | solution.py:581
  388.7 44.5 %collective-permute-start.50 = (bf16[2,2,1,2,128,704]{4,5,3,2,1,0:T(8,128)(2,1)}, bf16[2,2,1,2,128,704]{4,5,3,2,1,0:T(8,128)(2,1)S(1)}, u32[]{:S(2)}, u32[]{:S(2)}) collective-permute-start(bf16[2,2,1,2,128,704]{4,5,3,2,1,0:T(8,128)(2,1)} %copy.241), channel_id=1, source_target_pairs={{0,4},{2,6},{4,0},{6,2},{8,12},{10,14},{12,8},{14,10},{16,20},{18,... | collective-permute-start | bytes 4325384 | tf_op jit(solution)/shard_map/ppermute | solution.py:581
  394.1 67.2 %collective-permute-start.45 = (bf16[2,2,1,2,128,704]{4,5,3,2,1,0:T(8,128)(2,1)}, bf16[2,2,1,2,128,704]{4,5,3,2,1,0:T(8,128)(2,1)}, u32[]{:S(2)}, u32[]{:S(2)}) collective-permute-start(bf16[2,2,1,2,128,704]{4,5,3,2,1,0:T(8,128)(2,1)} %copy.239), channel_id=1, source_target_pairs={{0,4},{2,6},{4,0},{6,2},{8,12},{10,14},{12,8},{14,10},{16,20},{18,... | collective-permute-start | bytes 4325384 | tf_op jit(solution)/shard_map/ppermute | solution.py:581
  424.4 43.7 %collective-permute-start.17 = (bf16[128,2048]{1,0:T(8,128)(2,1)S(1)}, bf16[128,2048]{1,0:T(8,128)(2,1)}, u32[]{:S(2)}, u32[]{:S(2)}) collective-permute-start(bf16[128,2048]{1,0:T(8,128)(2,1)S(1)} %get-tuple-element.146), channel_id=1, source_target_pairs={{0,8},{2,10},{4,12},{6,14},{8,0},{10,2},{12,4},{14,6},{16,24},{18,... | collective-permute-start | bytes 1572872 | tf_op jit(solution)/shard_map/ppermute | solution.py:581
  427.3 40.8 %collective-permute-start.15 = (bf16[128,2048]{1,0:T(8,128)(2,1)S(1)}, bf16[128,2048]{1,0:T(8,128)(2,1)}, u32[]{:S(2)}, u32[]{:S(2)}) collective-permute-start(bf16[128,2048]{1,0:T(8,128)(2,1)S(1)} %get-tuple-element.146), channel_id=1, source_target_pairs={{0,2},{2,0},{4,6},{6,4},{8,10},{10,8},{12,14},{14,12},{16,18},{18,... | collective-permute-start | bytes 1572872 | tf_op jit(solution)/shard_map/ppermute | solution.py:581
  428.8 40.0 %collective-permute-start.19 = (bf16[128,2048]{1,0:T(8,128)(2,1)S(1)}, bf16[128,2048]{1,0:T(8,128)(2,1)S(1)}, u32[]{:S(2)}, u32[]{:S(2)}) collective-permute-start(bf16[128,2048]{1,0:T(8,128)(2,1)S(1)} %get-tuple-element.146), channel_id=1, source_target_pairs={{0,10},{2,8},{4,14},{6,12},{8,2},{10,0},{12,6},{14,4},{16,26},{18,... | collective-permute-start | bytes 1572872 | tf_op jit(solution)/shard_map/ppermute | solution.py:581
  433.2 34.9 %collective-permute-start.14 = (bf16[128,2048]{1,0:T(8,128)(2,1)S(1)}, bf16[128,2048]{1,0:T(8,128)(2,1)S(1)}, u32[]{:S(2)}, u32[]{:S(2)}) collective-permute-start(bf16[128,2048]{1,0:T(8,128)(2,1)S(1)} %get-tuple-element.146), channel_id=1, source_target_pairs={{0,1},{1,0},{2,3},{3,2},{4,5},{5,4},{6,7},{7,6},{8,9},{9,8},{10,11... | collective-permute-start | bytes 1572872 | tf_op jit(solution)/shard_map/ppermute | solution.py:584
  461.3 104.8 %collective-permute-start.56 = (bf16[1,2,1,2,128,704]{4,5,3,2,1,0:T(8,128)(2,1)}, bf16[1,2,1,2,128,704]{4,5,3,2,1,0:T(8,128)(2,1)}, u32[]{:S(2)}, u32[]{:S(2)}) collective-permute-start(bf16[1,2,1,2,128,704]{4,5,3,2,1,0:T(8,128)(2,1)} %dynamic-slice_convert_fusion.1), channel_id=1, source_target_pairs={{0,16},{2,18},{4,20},{6,22},{8,24},{10,26},{12,28},{14,30},{16,0},... | collective-permute-start | bytes 2162696 | tf_op jit(solution)/shard_map/ppermute | solution.py:581
  468.0 101.4 %collective-permute-start.51 = (bf16[1,2,1,2,128,704]{4,5,3,2,1,0:T(8,128)(2,1)}, bf16[1,2,1,2,128,704]{4,5,3,2,1,0:T(8,128)(2,1)}, u32[]{:S(2)}, u32[]{:S(2)}) collective-permute-start(bf16[1,2,1,2,128,704]{4,5,3,2,1,0:T(8,128)(2,1)} %dynamic-slice_convert_fusion.2), channel_id=1, source_target_pairs={{0,16},{2,18},{4,20},{6,22},{8,24},{10,26},{12,28},{14,30},{16,0},... | collective-permute-start | bytes 2162696 | tf_op jit(solution)/shard_map/ppermute | solution.py:581
  468.8 102.9 %collective-permute-start.46 = (bf16[1,2,1,2,128,704]{4,5,3,2,1,0:T(8,128)(2,1)}, bf16[1,2,1,2,128,704]{4,5,3,2,1,0:T(8,128)(2,1)}, u32[]{:S(2)}, u32[]{:S(2)}) collective-permute-start(bf16[1,2,1,2,128,704]{4,5,3,2,1,0:T(8,128)(2,1)} %dynamic-slice_convert_fusion.3), channel_id=1, source_target_pairs={{0,16},{2,18},{4,20},{6,22},{8,24},{10,26},{12,28},{14,30},{16,0},... | collective-permute-start | bytes 2162696 | tf_op jit(solution)/shard_map/ppermute | solution.py:581
  495.0 63.8 %collective-permute-start.65 = (f32[2,256]{1,0:T(2,128)S(1)}, f32[2,256]{1,0:T(2,128)S(1)}, u32[]{:S(2)}, u32[]{:S(2)}) collective-permute-start(f32[2,256]{1,0:T(2,128)S(1)} %copy-done.69), channel_id=1, source_target_pairs={{0,16},{2,18},{4,20},{6,22},{8,24},{10,26},{12,28},{14,30},{16,0},... | collective-permute-start | bytes 6152 | tf_op jit(solution)/shard_map/ppermute | solution.py:581
  560.2 52.8 %collective-permute-start.42 = (bf16[1,128,2048]{2,1,0:T(8,128)(2,1)}, bf16[1,128,2048]{2,1,0:T(8,128)(2,1)S(1)}, u32[]{:S(2)}, u32[]{:S(2)}) collective-permute-start(bf16[1,128,2048]{2,1,0:T(8,128)(2,1)} %constant_dynamic-slice_fusion.21), channel_id=1, source_target_pairs={{0,16},{2,18},{4,20},{6,22},{8,24},{10,26},{12,28},{14,30},{16,0},... | collective-permute-start | bytes 1572872 | tf_op jit(solution)/shard_map/ppermute | solution.py:581
  563.7 43.9 %collective-permute-start.29 = (bf16[128,2048]{1,0:T(8,128)(2,1)}, bf16[128,2048]{1,0:T(8,128)(2,1)}, u32[]{:S(2)}, u32[]{:S(2)}) collective-permute-start(bf16[128,2048]{1,0:T(8,128)(2,1)} %dynamic-slice_bitcast_fusion.2), channel_id=1, source_target_pairs={{0,1},{1,0},{2,3},{3,2},{4,5},{5,4},{6,7},{7,6},{8,9},{9,8},{10,11... | collective-permute-start | bytes 1572872 | tf_op jit(solution)/shard_map/ppermute | solution.py:584
  610.6 25.3 %collective-permute-start.34 = (bf16[128,2048]{1,0:T(8,128)(2,1)S(1)}, bf16[128,2048]{1,0:T(8,128)(2,1)S(1)}, u32[]{:S(2)}, u32[]{:S(2)}) collective-permute-start(bf16[128,2048]{1,0:T(8,128)(2,1)S(1)} %fusion.1), channel_id=1, source_target_pairs={{0,10},{2,8},{4,14},{6,12},{8,2},{10,0},{12,6},{14,4},{16,26},{18,... | collective-permute-start | bytes 1572872 | tf_op jit(solution)/shard_map/ppermute | solution.py:581
  612.9 54.8 %collective-permute-start.36 = (bf16[2,2,1,2,128,768]{5,4,3,2,1,0:T(8,128)(2,1)}, bf16[2,2,1,2,128,768]{5,4,3,2,1,0:T(8,128)(2,1)}, u32[]{:S(2)}, u32[]{:S(2)}) collective-permute-start(bf16[2,2,1,2,128,768]{5,4,3,2,1,0:T(8,128)(2,1)} %constant_dynamic-slice_fusion.26), channel_id=1, source_target_pairs={{0,4},{2,6},{4,0},{6,2},{8,12},{10,14},{12,8},{14,10},{16,20},{18,... | collective-permute-start | bytes 4718600 | tf_op jit(solution)/shard_map/ppermute | solution.py:581
  614.6 45.9 %collective-permute-start.43 = (bf16[128,2048]{1,0:T(8,128)(2,1)}, bf16[128,2048]{1,0:T(8,128)(2,1)}, u32[]{:S(2)}, u32[]{:S(2)}) collective-permute-start(bf16[128,2048]{1,0:T(8,128)(2,1)} %fusion.21), channel_id=1, source_target_pairs={{0,4},{2,6},{4,0},{6,2},{8,12},{10,14},{12,8},{14,10},{16,20},{18,... | collective-permute-start | bytes 1572872 | tf_op jit(solution)/shard_map/ppermute | solution.py:581
  662.6 47.9 %collective-permute-start.44 = (bf16[128,2048]{1,0:T(8,128)(2,1)}, bf16[128,2048]{1,0:T(8,128)(2,1)}, u32[]{:S(2)}, u32[]{:S(2)}) collective-permute-start(bf16[128,2048]{1,0:T(8,128)(2,1)} %add_convert_fusion.5), channel_id=1, source_target_pairs={{0,1},{1,0},{2,3},{3,2},{4,5},{5,4},{6,7},{7,6},{8,9},{9,8},{10,11... | collective-permute-start | bytes 1572872 | tf_op jit(solution)/shard_map/ppermute | solution.py:584
  670.1 36.1 %collective-permute-start.37 = (bf16[1,2,1,2,128,768]{5,4,3,2,1,0:T(8,128)(2,1)S(1)}, bf16[1,2,1,2,128,768]{5,4,3,2,1,0:T(8,128)(2,1)S(1)}, u32[]{:S(2)}, u32[]{:S(2)}) collective-permute-start(bf16[1,2,1,2,128,768]{5,4,3,2,1,0:T(8,128)(2,1)S(1)} %dynamic-slice_convert_fusion), channel_id=1, source_target_pairs={{0,16},{2,18},{4,20},{6,22},{8,24},{10,26},{12,28},{14,30},{16,0},... | collective-permute-start | bytes 2359304 | tf_op jit(solution)/shard_map/ppermute | solution.py:581
  671.8 47.9 %collective-permute-start.35 = (f32[128,2048]{1,0:T(8,128)S(1)}, f32[128,2048]{1,0:T(8,128)S(1)}, u32[]{:S(2)}, u32[]{:S(2)}) collective-permute-start(f32[128,2048]{1,0:T(8,128)S(1)} %subtract_add_fusion), channel_id=1, source_target_pairs={{0,1},{1,0},{2,3},{3,2},{4,5},{5,4},{6,7},{7,6},{8,9},{9,8},{10,11... | collective-permute-start | bytes 3145736 | tf_op jit(solution)/shard_map/ppermute | solution.py:584
  (134 other events, 2076.0 us)

commit v3 on v2

--- a/solution.py
+++ b/solution.py
@@ -244,6 +244,11 @@
             self.open.append(copy.wait)
         return copy
 
+    def sent(self, copies):
+        for copy in copies:
+            copy.wait_send()
+            self.open.remove(copy.wait_send)
+
     def close(self):
         assert self.n_remote <= self.send.shape[0] and self.n_local <= self.local.shape[0]
         for wait in self.open:
@@ -283,9 +288,9 @@
 def front_kernel(
     s_mix, s_out, s_g, s_u, s_d, n1_own, go_own, aux_own, par, inp, gain2,
     o_mix, o_out, o_g, o_u, o_d, o_n1, o_go, o_n2, o_pre, o_state, o_raw, o_res, o_mo, o_sc, o_aux,
-    w_mix, w_out, out2, n1, aux, pre, state, raw, part, core_in, half, peer_in,
+    w_mix, w_out, n1, aux, pre, state, raw, part, core_in, half, peer_in,
     sq, sq_core, sq_half, sq_peer, res, mo, sc, n2, decay, add,
-    send, recv, local, core_send, core_recv, sqc_send, sqc_recv,
+    send, recv, local, core_send, core_recv, sqc_send, sqc_recv, out_send, out_recv,
 ):
     me, t, (zf, zn, y, x), q, group, far, side, core = position()
     share, width = inp.shape
@@ -308,34 +313,67 @@
 
     mix_in = [link.remote(s_mix.at[q[r]], w_mix.at[mine], group[r]) for r in (1, 2, 3)]
     mix_own = link.here(s_mix.at[q[0]], w_mix.at[mine])
-    side_out = link.remote(s_out, out2.at[y], side)
-    own_out = link.here(s_out, out2.at[y])
+    out_rows = [at(z * block, block, block) for z in (zf, 1 - zf)]
+
+    def out_copy(k, src, dst, device):
+        return pltpu.make_async_remote_copy(
+            src_ref=src,
+            dst_ref=w_out.at[dst],
+            send_sem=out_send.at[k],
+            recv_sem=out_recv.at[k],
+            device_id=device,
+            device_id_type=MESH,
+        )
+
+    out_far = out_copy(0, s_out, out_rows[0], far)
+    out_side = out_copy(1, s_out, out_rows[0], side)
+    out_next = out_copy(2, w_out.at[out_rows[1]], out_rows[1], side)
+    out_here = pltpu.make_async_copy(s_out, w_out.at[out_rows[0]], out_send.at[3])
+
+    @pl.when(t == y)
+    def _():
+        out_far.start()
+        out_side.start()
+        out_here.start()
+
     aux_in = [link.remote(aux_own, aux.at[r], group[r]) for r in (1, 2, 3)]
     aux_mine = link.here(aux_own, aux.at[0])
-    n1_in = [link.remote(n1_own.at[at(t * share, share, share)], n1.at[row(r, t)], group[r]) for r in (1, 2, 3)]
+    n1_in = [link.remote(n1_own.at[at(t * share, share, share)], n1.at[row(r, t)], group[r]) for r in (1, 2)]
     n1_mine = link.here(n1_own, n1.at[pl.ds(0, rows)])
+    mix_own.wait()
+    for c in mix_in:
+        c.wait_recv()
+    far_mix = [link.remote(w_mix.at[pair(zf, c, y)], w_mix.at[pair(zf, c, y)], far) for c in (0, 1)]
+    side_mix = [link.remote(w_mix.at[pair(zf, c, y)], w_mix.at[pair(zf, c, y)], side) for c in (0, 1)]
+    n1_in[1].wait_recv()
+    n1_in.append(link.remote(n1.at[row(2, t)], n1.at[row(3, t)], group[1]))
+    n1_core = [link.remote(n1.at[row(2, t)], n1.at[row(2, t)], core)]
+    n1_in[0].wait_recv()
+    n1_core.append(link.remote(n1.at[row(1, t)], n1.at[row(1, t)], core))
     shards = ((s_g, o_g), (s_u, o_u), (s_d, o_d))
     ffn_in, ffn_own = [], []
     for s, o in shards:
         ffn_in += [link.remote(s.at[q[r]], o.at[:, mine], group[r]) for r in (1, 2, 3)]
         ffn_own.append(link.here(s.at[q[0]], o.at[:, mine]))
-
-    mix_own.wait()
-    for c in mix_in:
-        c.wait_recv()
-    far_mix = [link.remote(w_mix.at[pair(zf, c, y)], w_mix.at[pair(zf, c, y)], far) for c in (0, 1)]
-    side_mix = [link.remote(w_mix.at[pair(zf, c, y)], w_mix.at[pair(zf, c, y)], side) for c in (0, 1)]
-    side_out.wait_recv()
-    own_out.wait()
-    far_out = link.remote(out2.at[t], w_out.at[at(zf * block, block, block)], far)
-    here_out = link.here(out2.at[t], w_out.at[at(zf * block, block, block)])
-    n1_core = []
-    for i, r in enumerate((1, 2, 3)):
-        n1_in[i].wait_recv()
-        n1_core.append(link.remote(n1.at[row(r, t)], n1.at[row(r, t)], core))
+    n1_in[2].wait_recv()
+    n1_core.append(link.remote(n1.at[row(3, t)], n1.at[row(3, t)], core))
     for c in (0, 1):
         far_mix[c].wait_recv()
         side_mix.append(link.remote(w_mix.at[pair(1 - zf, c, y)], w_mix.at[pair(1 - zf, c, y)], side))
+
+    @pl.when(t == y)
+    def _():
+        out_far.wait_recv()
+        out_next.start()
+        out_far.wait_send()
+        out_side.wait_send()
+        out_here.wait()
+        out_next.wait_send()
+
+    @pl.when(t != y)
+    def _():
+        out_side.wait_recv()
+        out_next.wait_recv()
 
     for c in ffn_own:
         c.wait()
@@ -353,15 +391,14 @@
             far_ffn[i][c].wait_recv()
             side_ffn.append(link.remote(o.at[:, pair(1 - zf, c, y)], o.at[:, pair(1 - zf, c, y)], side))
 
-    go_in = [link.remote(go_own, o_go.at[row(r, t)], group[r]) for r in (1, 2, 3)]
+    go_in = [link.remote(go_own, o_go.at[row(r, t)], group[r]) for r in (1, 2)]
     go_core = [link.remote(go_own, o_go.at[row(0, t)], core)]
     link.here(go_own, o_go.at[row(0, t)], keep=True)
 
     n1_mine.wait()
     aux_mine.wait()
-    for c in side_mix + n1_core + aux_in + [far_out]:
+    for c in side_mix + n1_core + aux_in:
         c.wait_recv()
-    here_out.wait()
 
     def core_copy(r):
         return pltpu.make_async_remote_copy(
@@ -452,19 +489,29 @@
         return carry
 
     lax.fori_loop(0, share // chunk, finish, 0)
-    n2_in = [link.remote(n2, o_n2.at[row(r, t)], group[r]) for r in (1, 2, 3)]
+    n2_in = [link.remote(n2, o_n2.at[row(r, t)], group[r]) for r in (1, 2)]
     n2_core = [link.remote(n2, o_n2.at[row(0, t)], core)]
     link.here(n2, o_n2.at[row(0, t)], keep=True)
     link.here(res, o_res, keep=True)
     link.here(mo, o_mo, keep=True)
     link.here(sc, o_sc, keep=True)
-    for i, r in enumerate((1, 2, 3)):
-        go_in[i].wait_recv()
-        go_core.append(link.remote(o_go.at[row(r, t)], o_go.at[row(r, t)], core))
+
+    def spread(o, incoming, cores):
+        incoming[1].wait_recv()
+        incoming.append(link.remote(o.at[row(2, t)], o.at[row(3, t)], group[1]))
+        cores.append(link.remote(o.at[row(2, t)], o.at[row(2, t)], core))
+        incoming[0].wait_recv()
+        cores.append(link.remote(o.at[row(1, t)], o.at[row(1, t)], core))
+
+    def spread_last(o, incoming, cores):
+        incoming[2].wait_recv()
+        cores.append(link.remote(o.at[row(3, t)], o.at[row(3, t)], core))
+
+    spread(o_go, go_in, go_core)
+    spread(o_n2, n2_in, n2_core)
     forward_ffn(1)
-    for i, r in enumerate((1, 2, 3)):
-        n2_in[i].wait_recv()
-        n2_core.append(link.remote(o_n2.at[row(r, t)], o_n2.at[row(r, t)], core))
+    spread_last(o_go, go_in, go_core)
+    spread_last(o_n2, n2_in, n2_core)
     forward_ffn(2)
     for c in side_ffn + go_core + n2_core:
         c.wait_recv()
@@ -500,7 +547,6 @@
     scratch = [
         pltpu.VMEM((width, 3 * feat), bf16),
         pltpu.VMEM((feat, width), bf16),
-        pltpu.VMEM((2, block, width), bf16),
         pltpu.VMEM((group_rows, width), bf16),
         pltpu.VMEM((4,) + aux_own.shape, f32),
         pltpu.VMEM((group_rows, 3 * feat), f32),
@@ -523,7 +569,7 @@
         pltpu.SemaphoreType.DMA((68,)),
         pltpu.SemaphoreType.DMA((68,)),
         pltpu.SemaphoreType.DMA((24,)),
-    ] + [pltpu.SemaphoreType.DMA((4,))] * 4
+    ] + [pltpu.SemaphoreType.DMA((4,))] * 6
     return pl.pallas_call(
         front_kernel,
         in_specs=[any_spec] * 7 + [any_spec] + [vmem_spec] * 3,
@@ -535,6 +581,502 @@
         ),
         name="front",
     )(s_mix, s_out, s_g, s_u, s_d, n1_own, go_own, aux_own, par, inp, gain2)
+
+
+def back_kernel(
+    h_d, h_g, h_u, n2, go, p_two, p_block, n1, w_mix_in, w_out_in, pre, state, raw, aux_in,
+    par, inp, res, mo, sc, go_own, gains,
+    o_g, o_u, o_d, o_mix, o_out, o_tok, o_blk, o_vec,
+    left, right, gmix, dw_d, dw_g, dw_u, dw_mix, yr_d, yr_g, yr_u, yr_mix, zr_d, zr_g, zr_u, zr_mix,
+    own, half, core_in, core_blk, peer_in, peer_blk, w_mix, w_out, aux, pre_b, state_b, raw_b,
+    grads, grads_t, decay, add, hold, yr_out, zr_out, hid_a, hid_b,
+    gres, gm_own, scalars, scal_all, sums, vec, vec_in,
+    send, recv, local, core_send, core_recv, out_send, out_recv, piece_sem,
+):
+    me, t, (zf, zn, y, x), q, group, far, side, core = position()
+    share, width = inp.shape
+    rows = 2 * share
+    block = width // 16
+    feat = par.shape[1]
+    link = Copies(send, recv, local)
+    meet(group[1:] + [far, side, core])
+
+    def at(start, size, unit):
+        return pl.ds(pl.multiple_of(start, unit), size)
+
+    def pair(fz, c, fy):
+        return at(fz * (8 * block) + c * (4 * block) + fy * (2 * block), 2 * block, 2 * block)
+
+    def row(r, tt):
+        return at(r * rows + tt * share, share, share)
+
+    def rel(r):
+        return pl.ds(r * share, share)
+
+    two_core = [link.remote(p_two.at[row(r, 1 - t)], core_in.at[rel(r)], core) for r in (3, 2, 1, 0)]
+    two_own = [link.here(p_two.at[row(r, t)], own.at[rel(r)]) for r in (3, 2, 1, 0)]
+    get_d = [link.here(h_d, hid_a), link.here(go, left)]
+    get_g = [link.here(h_g, hid_b), link.here(n2, right)]
+    get_aux = [link.here(aux_in, aux), link.here(w_out_in, w_out), link.here(w_mix_in, w_mix)]
+
+    def over_cores(arrived, mine, source, peers):
+        sent = []
+        for i, r in enumerate((3, 2, 1)):
+            for c in mine[i]:
+                c.wait()
+            arrived[i].wait_recv()
+
+            def add_rows(j, carry):
+                to = at(r * share + j * 16, 16, 16)
+                half[to, :] = (source(r, j) + core_in_now[to, :].astype(f32)).astype(bf16)
+                return carry
+
+            lax.fori_loop(0, share // 16, add_rows, 0)
+            sent.append(link.remote(half.at[rel(r)], peers.at[rel(r - 1)], group[r]))
+        for c in mine[3]:
+            c.wait()
+        arrived[3].wait_recv()
+        return sent
+
+    def own_rows(r, j):
+        return own[at(r * share + j * 16, 16, 16), :].astype(f32)
+
+    core_in_now = core_in
+    two_peer = over_cores(two_core, [[c] for c in two_own], own_rows, peer_in)
+
+    def weight_grad(hid, other, dw, first, count):
+        wide = 4 * block
+
+        def columns(i, carry):
+            to = at(((1 - zf) * 2 + i - (i // 2) * 4 * (1 - zf)) * wide, wide, wide)
+            dw[:, to] = jnp.dot(hid[...], other[:, to], preferred_element_type=f32).astype(bf16)
+            return carry
+
+        lax.fori_loop(first, first + count, columns, 0)
+
+    def side_send(dw, yr, slot):
+        fz = 1 - zf if slot == 0 else zf
+        return [
+            link.remote(dw.at[:, pair(fz, c, 1 - y)], yr.at[:, pl.ds((slot * 2 + c) * 2 * block, 2 * block)], side)
+            for c in (0, 1)
+        ]
+
+    def first_hop(hid, other, dw, yr):
+        weight_grad(hid, other, dw, 0, 2)
+        sent = [side_send(dw, yr, 0)]
+        weight_grad(hid, other, dw, 2, 2)
+        sent.append(side_send(dw, yr, 1))
+        return sent
+
+    for c in get_d:
+        c.wait()
+    hop_d = first_hop(hid_a, left, dw_d, yr_d)
+    get_u = link.here(h_u, hid_a)
+    get_n1 = link.here(n1, left)
+    for c in get_g:
+        c.wait()
+    hop_g = first_hop(hid_b, right, dw_g, yr_g)
+
+    for c in two_peer:
+        c.wait_recv()
+    gain_two = gains[1:2, :]
+    sums[...] = jnp.zeros_like(sums)
+    step = 16
+
+    def residual_rows(j, carry):
+        to = at(j * step, step, step)
+        total = own[to, :].astype(f32) + core_in[to, :].astype(f32)
+        for r in (0, 1, 2):
+            total = total + peer_in[at(r * share + j * step, step, step), :].astype(f32)
+        value = res[to, :]
+        s = lax.rsqrt(jnp.mean(value * value, axis=1, keepdims=True) + epsilon)
+        weighted = total * gain_two
+        grad = (
+            go_own[to, :].astype(f32)
+            + s * weighted
+            - value * (s * s * s) * jnp.mean(weighted * value, axis=1, keepdims=True)
+        )
+        gres[to, :] = grad
+        low = grad.astype(bf16)
+        gm_own[to, :] = low
+        dot = jnp.sum(low.astype(f32) * mo[to, :], axis=1, keepdims=True)
+        scale = sc[to, 0:1]
+        sc[to, 1:2] = dot / (scale * width)
+        sums[1:2, :] += jnp.sum(total * value * s, axis=0, keepdims=True)
+        return carry
+
+    lax.fori_loop(0, share // step, residual_rows, 0)
+    scalars[...] = sc[...].T[0:8, :]
+
+    def scal(r, tt):
+        return scal_all.at[r * 2 + tt]
+
+    gm_in = [link.remote(gm_own, gmix.at[row(r, t)], group[r]) for r in (1, 2)]
+    sc_in = [link.remote(scalars, scal(r, t), group[r]) for r in (1, 2, 3)]
+    gm_core = [link.remote(gm_own, gmix.at[row(0, t)], core), link.remote(scalars, scal(0, t), core)]
+    gm_here = [link.here(gm_own, gmix.at[row(0, t)]), link.here(scalars, scal(0, t))]
+    blk_core = [link.remote(p_block.at[row(r, 1 - t)], core_blk.at[rel(r)], core) for r in (3, 2, 1, 0)]
+
+    get_u.wait()
+    hop_u = first_hop(hid_a, right, dw_u, yr_u)
+
+    def add_columns(dw, to, others):
+        size = 64 if dw.shape[0] % 64 == 0 else dw.shape[0]
+
+        def some(j, carry):
+            at_rows = at(j * size, size, size)
+            total = dw[at_rows, to].astype(f32)
+            for ref, cols in others:
+                total = total + ref[at_rows, cols].astype(f32)
+            dw[at_rows, to] = total.astype(bf16)
+            return carry
+
+        lax.fori_loop(0, dw.shape[0] // size, some, 0)
+
+    def part_of(i):
+        return pl.ds(i * 2 * block, 2 * block)
+
+    def second_hop(hop, dw, yr, zr):
+        sent = []
+        for c in (0, 1):
+            hop[0][c].wait_recv()
+            add_columns(dw, pair(1 - zf, c, y), [(yr, part_of(c))])
+            sent.append(link.remote(dw.at[:, pair(1 - zf, c, y)], zr.at[:, part_of(c)], far))
+        return sent
+
+    def last_hop(hop, sent, dw, yr, zr, out):
+        for c in (0, 1):
+            hop[1][c].wait_recv()
+            sent[c].wait_recv()
+            add_columns(dw, pair(zf, c, y), [(yr, part_of(2 + c)), (zr, part_of(c))])
+
+        def owner(r):
+            fx = x if r in (0, 2) else 1 - x
+            fzn = zn if r in (0, 1) else 1 - zn
+            return at((zf * 8 + fzn * 4 + y * 2 + fx) * block, block, block)
+
+        link.here(dw.at[:, owner(0)], out.at[q[0]], keep=True)
+        return [link.remote(dw.at[:, owner(r)], out.at[q[0]], group[r]) for r in (1, 2, 3)]
+
+    far_d = second_hop(hop_d, dw_d, yr_d, zr_d)
+
+    gm_in[1].wait_recv()
+    gm_in.append(link.remote(gmix.at[row(2, t)], gmix.at[row(3, t)], group[1]))
+    gm_core.append(link.remote(gmix.at[row(2, t)], gmix.at[row(2, t)], core))
+    gm_in[0].wait_recv()
+    gm_core.append(link.remote(gmix.at[row(1, t)], gmix.at[row(1, t)], core))
+    for i, r in enumerate((1, 2, 3)):
+        sc_in[i].wait_recv()
+        gm_core.append(link.remote(scal(r, t), scal(r, t), core))
+    far_g = second_hop(hop_g, dw_g, yr_g, zr_g)
+    gm_in[2].wait_recv()
+    gm_core.append(link.remote(gmix.at[row(3, t)], gmix.at[row(3, t)], core))
+
+    link.sent(two_peer)
+    blk_own = [link.here(p_block.at[row(r, t)], own.at[rel(r)]) for r in (3, 2, 1, 0)]
+    for c in get_aux + [get_n1] + gm_here:
+        c.wait()
+    for c in gm_core:
+        c.wait_recv()
+
+    def one_core(r):
+        return pltpu.make_async_remote_copy(
+            src_ref=right.at[row(r, 1 - t)],
+            dst_ref=core_in.at[at(r * share, share, share)],
+            send_sem=core_send.at[r],
+            recv_sem=core_recv.at[r],
+            device_id=core,
+            device_id_type=MESH,
+        )
+
+    def fetch(r):
+        here = at(r * rows, rows, rows)
+        return [
+            pltpu.make_async_copy(pre.at[here], pre_b, piece_sem.at[0]),
+            pltpu.make_async_copy(state.at[here], state_b, piece_sem.at[1]),
+            pltpu.make_async_copy(raw.at[here], raw_b, piece_sem.at[2]),
+        ]
+
+    bound = par[0:1, :]
+    gain = par[1:2, :]
+    gain_sums = sums.at[2:4, 0:feat]
+    mixed_t = hid_b.at[0:feat]
+    dw_out = w_out
+
+    def piece(i, carry):
+        r = 3 - i
+        here = at(r * rows, rows, rows)
+        copies = fetch(r)
+        for c in copies:
+            c.start()
+        up = lax.dot_general(
+            gmix[here, :], w_out[...], (((1,), (1,)), ((), ())), preferred_element_type=f32
+        )
+        masks = aux[r].T
+        valid = masks[:, 0:1]
+        keep = masks[:, 1:2]
+        scale_parts = [scal_all[r * 2 + tt].T for tt in (0, 1)]
+        scale = jnp.concatenate([p[:, 0:1] for p in scale_parts], axis=0)
+        dot_mean = jnp.concatenate([p[:, 1:2] for p in scale_parts], axis=0)
+        for c in copies:
+            c.wait()
+        at_row = lax.broadcasted_iota(jnp.int32, (rows, feat), 0)
+        input_pre = pre_b[:, :feat]
+        outgate_pre = pre_b[:, 2 * feat :]
+        held = state_b[...]
+        sig_out = jax.nn.sigmoid(outgate_pre)
+        act_out = outgate_pre * sig_out
+        scaled = up * (held * scale)
+        grads[:, 2 * feat :] = scaled * gain * (sig_out * (1.0 + outgate_pre * (1.0 - sig_out)))
+        add[...] = scale * (gain * act_out * up) - held * (scale * scale * scale * dot_mean)
+        gain_sums[0:1, :] += jnp.sum(scaled * act_out, axis=0, keepdims=True)
+        sig_forget = jax.nn.sigmoid(pre_b[:, feat : 2 * feat])
+        forget = bound + (1.0 - bound) * sig_forget
+        decay[...] = jnp.where(at_row < rows - 1, pltpu.roll(forget * keep, rows - 1, 0), 0.0)
+        scan_rows(decay, add, hold, True)
+        grad_state = hold[...]
+        before = jnp.where(at_row > 0, pltpu.roll(held, 1, 0), 0.0)
+        sig_in = jax.nn.sigmoid(input_pre)
+        grad_forget = grad_state * (before * keep - input_pre * sig_in * valid)
+        grads[:, :feat] = (
+            grad_state * (1.0 - forget) * valid * (sig_in * (1.0 + input_pre * (1.0 - sig_in)))
+        )
+        grads[:, feat : 2 * feat] = grad_forget * (1.0 - bound) * sig_forget * (1.0 - sig_forget)
+        gain_sums[1:2, :] += jnp.sum(grad_forget * (1.0 - sig_forget), axis=0, keepdims=True)
+        low = grads[...].astype(bf16)
+        right[here, :] = lax.dot_general(
+            low, w_mix[...], (((1,), (1,)), ((), ())), preferred_element_type=f32
+        ).astype(bf16)
+        one_core(r).start()
+        grads_t[:, here] = grads[...].T.astype(bf16)
+        mixed_t[:, here] = (raw_b[...].astype(f32) * scale).T.astype(bf16)
+        return carry
+
+    lax.fori_loop(0, 4, piece, 0)
+
+    core_in_now = core_in
+
+    class Arrival:
+        def __init__(self, copy):
+            self.wait_recv = copy.wait_recv
+
+    def one_rows(r, j):
+        return right[at(r * rows + t * share + j * 16, 16, 16), :].astype(f32)
+
+    one_arrived = [Arrival(one_core(r)) for r in (3, 2, 1, 0)]
+    one_peer = over_cores(one_arrived, [[], [], [], []], one_rows, peer_in)
+    for r in (3, 2, 1, 0):
+        one_core(r).wait_send()
+
+    hop_mix = first_hop(grads_t, left, dw_mix, yr_mix)
+
+    def out_columns(i, carry):
+        to = at(i * (4 * block), 4 * block, 4 * block)
+        dw_out[:, to] = jnp.dot(mixed_t[...], gmix[:, to], preferred_element_type=f32).astype(bf16)
+        return carry
+
+    lax.fori_loop(0, 4, out_columns, 0)
+    near_rows = at(zf * block, block, block)
+    far_rows = at((1 - zf) * block, block, block)
+
+    def out_copy(k, src, dst, device):
+        return pltpu.make_async_remote_copy(
+            src_ref=src,
+            dst_ref=dst,
+            send_sem=out_send.at[k],
+            recv_sem=out_recv.at[k],
+            device_id=device,
+            device_id_type=MESH,
+        )
+
+    out_side = out_copy(0, dw_out, yr_out, side)
+    out_far = out_copy(1, dw_out.at[far_rows], zr_out, far)
+    out_core = out_copy(2, dw_out.at[near_rows], o_out, core)
+    out_here = pltpu.make_async_copy(dw_out.at[near_rows], o_out, out_send.at[3])
+
+    @pl.when(t != y)
+    def _():
+        out_side.start()
+
+    far_u = second_hop(hop_u, dw_u, yr_u, zr_u)
+    back_d = last_hop(hop_d, far_d, dw_d, yr_d, zr_d, o_d)
+
+    for c in one_peer:
+        c.wait_recv()
+    gain_one = gains[0:1, :]
+
+    def token_rows(j, carry):
+        to = at(j * step, step, step)
+        total = one_rows(0, j) + core_in[to, :].astype(f32)
+        for r in (0, 1, 2):
+            total = total + peer_in[at(r * share + j * step, step, step), :].astype(f32)
+        value = inp[to, :]
+        s = lax.rsqrt(jnp.mean(value * value, axis=1, keepdims=True) + epsilon)
+        weighted = total * gain_one
+        gres[to, :] = (
+            gres[to, :]
+            + s * weighted
+            - value * (s * s * s) * jnp.mean(weighted * value, axis=1, keepdims=True)
+        )
+        sums[0:1, :] += jnp.sum(total * value * s, axis=0, keepdims=True)
+        return carry
+
+    lax.fori_loop(0, share // step, token_rows, 0)
+    tok_rows = at(t * share, share, share)
+    tok_core = link.remote(gres, o_tok.at[tok_rows], core)
+    link.here(gres, o_tok.at[tok_rows], keep=True)
+
+    vec[0] = jnp.zeros(vec.shape[1:], f32)
+    for k in (0, 1):
+        for i in range(16):
+            vec[0, k * 16 + i : k * 16 + i + 1, :] = sums[k : k + 1, i * block : (i + 1) * block]
+    for k in (2, 3):
+        for i in (0, 1):
+            vec[0, pl.ds(k * 16 + i * 8 + zn * 4 + t * 2 + x, 1), :] = sums[
+                k : k + 1, i * block : (i + 1) * block
+            ]
+    partners = [group[1], group[2], side, far, core]
+    turn = [link.remote(vec.at[0], vec_in.at[0], partners[0])]
+
+    def next_turn():
+        k = len(turn)
+        turn[k - 1].wait_recv()
+        vec[k] = vec[k - 1] + vec_in[k - 1]
+        if k < len(partners):
+            turn.append(link.remote(vec.at[k], vec_in.at[k], partners[k]))
+
+    link.sent(one_peer)
+    core_in_now = core_blk
+    blk_peer = over_cores(blk_core, [[c] for c in blk_own], own_rows, peer_blk)
+    next_turn()
+    far_mix = second_hop(hop_mix, dw_mix, yr_mix, zr_mix)
+
+    @pl.when(t == y)
+    def _():
+        out_side.wait_recv()
+        add_columns(dw_out, pl.ds(0, width), [(yr_out, pl.ds(0, width))])
+        out_far.start()
+
+    next_turn()
+    back_g = last_hop(hop_g, far_g, dw_g, yr_g, zr_g, o_g)
+    next_turn()
+    for c in blk_peer:
+        c.wait_recv()
+
+    def block_rows(j, carry):
+        to = at(j * step, step, step)
+        total = own_rows(0, j) + core_blk[to, :].astype(f32)
+        for r in (0, 1, 2):
+            total = total + peer_blk[at(r * share + j * step, step, step), :].astype(f32)
+        gm_own[to, :] = (res[to, :] + total).astype(bf16)
+        return carry
+
+    link.sent(gm_in[:2] + gm_core[:1])
+    lax.fori_loop(0, share // step, block_rows, 0)
+    link.here(gm_own, o_blk, keep=True)
+    next_turn()
+    back_u = last_hop(hop_u, far_u, dw_u, yr_u, zr_u, o_u)
+    next_turn()
+    link.here(vec.at[5], o_vec, keep=True)
+    back_mix = last_hop(hop_mix, far_mix, dw_mix, yr_mix, zr_mix, o_mix)
+
+    @pl.when(t == y)
+    def _():
+        out_far.wait_recv()
+
+        def some(j, carry):
+            to = at(zf * block + j * 16, 16, 16)
+            dw_out[to, :] = (
+                dw_out[to, :].astype(f32) + zr_out[at(j * 16, 16, 16), :].astype(f32)
+            ).astype(bf16)
+            return carry
+
+        lax.fori_loop(0, block // 16, some, 0)
+        out_core.start()
+        out_here.start()
+        out_far.wait_send()
+        out_core.wait_send()
+        out_here.wait()
+
+    @pl.when(t != y)
+    def _():
+        out_side.wait_send()
+        out_core.wait_recv()
+
+    for c in back_d + back_g + back_u + back_mix + [tok_core]:
+        c.wait_recv()
+    link.close()
+
+
+def back(*arrays):
+    par, inp = arrays[14], arrays[15]
+    share, width = inp.shape
+    rows, group_rows = 2 * share, 8 * share
+    feat, hid, block = par.shape[1], arrays[0].shape[0], width // 16
+    made = jax.ShapeDtypeStruct
+    vm = pltpu.VMEM
+    outs = [
+        made((4, hid, block), bf16),
+        made((4, hid, block), bf16),
+        made((4, hid, block), bf16),
+        made((4, 3 * feat, block), bf16),
+        made((block, width), bf16),
+        made((rows, width), f32),
+        made((share, width), bf16),
+        made((64, block), f32),
+    ]
+    scratch = (
+        [vm((group_rows, width), bf16)] * 3
+        + [vm((hid, width), bf16)] * 3
+        + [vm((3 * feat, width), bf16)]
+        + [vm((hid, width // 2), bf16)] * 3
+        + [vm((3 * feat, width // 2), bf16)]
+        + [vm((hid, width // 4), bf16)] * 3
+        + [vm((3 * feat, width // 4), bf16)]
+        + [vm((4 * share, width), bf16)] * 4
+        + [vm((3 * share, width), bf16)] * 2
+        + [
+            vm((width, 3 * feat), bf16),
+            vm((feat, width), bf16),
+            vm(arrays[13].shape, f32),
+            vm((rows, 3 * feat), f32),
+            vm((rows, feat), f32),
+            vm((rows, feat), bf16),
+            vm((rows, 3 * feat), f32),
+            vm((3 * feat, group_rows), bf16),
+            vm((rows, feat), f32),
+            vm((rows, feat), f32),
+            vm((rows, feat), f32),
+            vm((feat, width), bf16),
+            vm((block, width), bf16),
+            vm((hid, group_rows), bf16),
+            vm((hid, group_rows), bf16),
+            vm((share, width), f32),
+            vm((share, width), bf16),
+            vm((8, share), f32),
+            vm((8, 8, share), f32),
+            vm((4, width), f32),
+            vm((6, 64, block), f32),
+            vm((5, 64, block), f32),
+            pltpu.SemaphoreType.DMA((96,)),
+            pltpu.SemaphoreType.DMA((96,)),
+            pltpu.SemaphoreType.DMA((32,)),
+        ]
+        + [pltpu.SemaphoreType.DMA((4,))] * 5
+    )
+    any_spec = pl.BlockSpec(memory_space=pl.ANY)
+    vmem_spec = pl.BlockSpec(memory_space=pltpu.VMEM)
+    return pl.pallas_call(
+        back_kernel,
+        in_specs=[any_spec] * 14 + [vmem_spec] * 7,
+        out_specs=[any_spec] * len(outs),
+        out_shape=outs,
+        scratch_shapes=scratch,
+        compiler_params=pltpu.CompilerParams(
+            collective_id=2, has_side_effects=True, vmem_limit_bytes=62 << 20
+        ),
+        name="back",
+    )(*arrays)
 
 
 def body(
@@ -725,6 +1267,43 @@
         normed_two_half = (residual * rms_scale(residual) * ffn_gain).astype(bf16)
         normed_two = jnp.stack(tp_gather(normed_two_half)).reshape(n_tp * rows, width)
 
+    if n_dp == 16 and n_t == 2:
+        gate_pre = cross_cols(gate_full, normed_two)
+        up_pre = cross_cols(up_full, normed_two)
+        grad_hidden = cross_cols(down_full, grad_out_all)
+        gate_act = jax.nn.silu(gate_pre)
+        hidden = (gate_act * up_pre).astype(bf16)
+        grad_up = (grad_hidden * gate_act).astype(bf16)
+        grad_gate = (grad_hidden * up_pre * silu_slope(gate_pre)).astype(bf16)
+        two_parts = (cross_rows(grad_gate, gate_full) + cross_rows(grad_up, up_full)).astype(bf16)
+        block_parts = cross_rows(hidden, down_full).astype(bf16)
+        grad_g, grad_u, grad_d, grad_mix_w, grad_out_w, grad_tokens, block_out, vec = back(
+            hidden, grad_gate, grad_up, normed_two, grad_out_all, two_parts, block_parts, normed_one,
+            mix_full, out_full, pre, state, mix_raw, aux_rows, par, inputs_half, residual, mixed_out,
+            scale_lanes, grad_out_rows, jnp.stack([norm_gain, ffn_gain]),
+        )
+        mix_all = t_gather(grad_mix_w).reshape((2, 2, 2, 3, 2, block, block))
+        mix_all = mix_all.transpose((3, 6, 4, 1, 0, 2, 5)).reshape(3, block, width).astype(f32)
+        mine = lambda k: lax.dynamic_slice_in_dim(vec, k * n_dp + me, 1, 0)
+        shares, picked, lower = bound_parts(
+            lax.dynamic_slice_in_dim(bound_table, me * block, block, 1)
+        )
+        return (
+            block_out,
+            grad_tokens,
+            mix_all[0],
+            mix_all[1],
+            mix_all[2],
+            grad_out_w.astype(f32),
+            grad_g.reshape(n_tp * hid, block).T.astype(f32),
+            grad_u.reshape(n_tp * hid, block).T.astype(f32),
+            grad_d.reshape(n_tp * hid, block).astype(f32),
+            mine(0)[0],
+            mine(2)[0],
+            mine(1)[0],
+            shares * (picked - lower[None, :]) * mine(3),
+        )
+
     scale_two = rms_scale(residual)
     gate_pre = cross_cols(normed_two, gate_full)
     up_pre = cross_cols(normed_two, up_full)

time: 734 us -> 573 us (0.78)
  Pallas kernels: 229 us -> 475 us
  waiting for transfers between devices: 231 us -> 0.01 us
  local copies, waits for them, and re-layouts: 93.5 us -> 35.4 us
  starting transfers between devices: 54.9 us -> 0.07 us
  other arithmetic: 56.7 us -> 24.2 us
  matrix products: 58.3 us -> 27.6 us
    ppermute x43 -> x0, waiting for transfers between devices: 229 us -> none  [swap(): return lax.ppermute(values, 'dp', [(i, i ^ mask) for i in range(n_dp)])]
    pallas_call x1, Pallas kernels: 6.11 us -> 231 us  [back(): pl.pallas_call(back_kernel, in_specs=[any_spec] * 14 + [vmem_spec] * 7, o...]
    ppermute x43 -> x0, starting transfers between devices: 51.3 us -> none  [swap(): return lax.ppermute(values, 'dp', [(i, i ^ mask) for i in range(n_dp)])]
    reshape x5 -> x0, local copies, waits for them, and re-layouts: 22.2 us -> none  [the longest x3 22.2 us: weight_back(): grad = grad.reshape((2,) * depth + (block, cols))]
    pallas_call x1, Pallas kernels: 223 us -> 244 us  [front(): pl.pallas_call(front_kernel, in_specs=[any_spec] * 7 + [any_spec] + [vmem...]
    dynamic_slice x8 -> x0, local copies, waits for them, and re-layouts: 14.8 us -> none  [the longest x3 12.7 us: weight_back(): hold = lax.dynamic_slice_in_dim(grad, bit[b], 1, axis_of[b]).astype(f32)]
    convert_element_type x19 -> x5, other arithmetic: 20.1 us -> 6.04 us  [the longest x1 2.3 us: body(): grad_d.reshape(n_tp * hid, block).astype(f32)]
    dot_general x3 -> x0, matrix products: 13.1 us -> none  [matmul(): return jnp.dot(first_op, second_op, preferred_element_type=f32)]
  transfers between devices with their start and end apart: 68 -> 1, of which waited for: 32 -> 0; matrix products, arithmetic and copies ran while one was open for 21% -> 2% of each run, Pallas kernels for 1% -> 0%
where the time goes in v3:
time: 573 us; the launch traced here: 565 us
  Pallas kernels  475 us (83%)
  local copies, waits for them, and re-layouts  35.4 us (6%)
  matrix products  27.6 us (5%)
  other arithmetic  24.2 us (4%)
    pallas_call x1, Pallas kernels, front(): pl.pallas_call(front_kernel, in_specs=[any_spec] * 7 + [any_spec] + [vmem...  244 us
    pallas_call x1, Pallas kernels, back(): pl.pallas_call(back_kernel, in_specs=[any_spec] * 14 + [vmem_spec] * 7, o...  231 us
    dot_general x3, matrix products, cross_rows(): lax.dot_general(first_op, second_op, (((0,), (0,)), ((), ())), preferred_...  13.9 us
    dot_general x3, matrix products, cross_cols(): lax.dot_general(first_op, second_op, (((1,), (1,)), ((), ())), preferred_...  13.7 us
  transfers between devices with their start and end apart: 1, of which 0 were waited for; matrix products, arithmetic and copies ran while one was open for 2% of the time, Pallas kernels for 0%

profile of v3, /device:TPU:0, one launch (start us, length us, event | category | flops | bytes accessed | tf_op | source)
XLA Modules:
  0.0 564.9 jit_solution(9564989863648173489)
XLA Ops:
  1.4 1.5 multiply_reduce_fusion
  2.9 1.5 convert_element_type.97
  8.7 2.2 reshape.190
  13.2 2.3 copy.64
  15.5 2.2 copy.65
  18.3 1.8 reshape.199
  26.1 2.0 pad_maximum_fusion.s_mix
  28.1 2.3 multiply_convert_fusion.4
  31.1 244.3 %front.1 = (bf16[2048,768]{1,0:T(8,128)(2,1)}, bf16[256,2048]{1,0:T(8,128)(2,1)}, bf16[704,2048]{1,0:T(8,128)(2,1)}, bf16[704,2048]{1,0:T(8,128)(2,1)}, bf16[704...) custom-call(bf16[4,128,768]{2,1,0:T(8,128)(2,1)} %pad_maximum_fusion, ...), custom_call_target="tpu_custom_call" | custom-call | tf_op jit(solution)/shard_map/front/pallas_call | solution.py:573
  275.4 6.2 %fusion.11 = f32[704,1024]{1,0:T(8,128)S(1)} fusion(bf16[704,2048]{1,0:T(8,128)(2,1)} %get-tuple-element.36, bf16[1024,2048]{1,0:T(8,128)(2,1)} %get-tuple-element.37.n2), kind=kOutput, calls=%fused_computation.61 | convolution fusion | flops 2952790016 | bytes 9961472 | tf_op jit(solution)/shard_map/dot_general | solution.py:44
  281.7 3.3 fusion.12
  285.0 4.2 multiply_convert_fusion
  289.2 3.5 fusion.13
  292.8 5.1 convolution_convert_fusion.p_block
  298.5 5.3 add_convert_fusion.p_two
  303.9 231.1 %back.1 = (bf16[4,704,128]{2,1,0:T(8,128)(2,1)}, bf16[4,704,128]{2,1,0:T(8,128)(2,1)}, bf16[4,704,128]{2,1,0:T(8,128)(2,1)}, bf16[4,768,128]{2,1,0:T(8,128)(2,1)...) custom-call(bf16[704,1024]{1,0:T(8,128)(2,1)} %copy-done.7, ...), custom_call_target="tpu_custom_call" | custom-call | tf_op jit(solution)/shard_map/back/pallas_call | solution.py:1069
  543.4 1.5 copy.71
  545.0 1.5 copy.72
  546.5 2.3 bitcast_convert_fusion
  551.5 2.0 copy.68
  553.5 1.8 squeeze.48
  556.1 1.8 squeeze.49
  558.7 1.8 squeeze.50
  561.3 3.1 copy.85
  (85 shorter events, 28.0 us)
Async XLA Ops:
  0.6 17.6 %copy-start = (f32[2048]{0:T(1024)S(1)}, f32[2048]{0:T(1024)}, u32[]{:S(2)}) copy-start(f32[2048]{0:T(1024)} %param.24) | copy-start | bytes 24580
  0.7 3.7 copy-start.11
  8.7 9.2 %copy-start.15 = (s32[2]{0:T(128)S(1)}, s32[2]{0:T(128)}, u32[]{:S(2)}) copy-start(s32[2]{0:T(128)} %param.27) | copy-start | bytes 28
  10.9 12.3 %copy-start.2 = (bf16[256,2048]{1,0:T(8,128)(2,1)S(1)}, bf16[256,2048]{1,0:T(8,128)(2,1)}, u32[]{:S(2)}) copy-start(bf16[256,2048]{1,0:T(8,128)(2,1)} %param.15) | copy-start | bytes 3145732
  10.9 12.4 %copy-start.13 = (f32[2048]{0:T(1024)S(1)}, f32[2048]{0:T(1024)}, u32[]{:S(2)}) copy-start(f32[2048]{0:T(1024)} %param.23) | copy-start | bytes 24580
  13.2 12.9 %copy-start.8 = (bf16[4,128,256]{2,1,0:T(8,128)(2,1)S(1)}, bf16[4,128,256]{2,1,0:T(8,128)(2,1)}, u32[]{:S(2)}) copy-start(bf16[4,128,256]{2,1,0:T(8,128)(2,1)} %reshape.195) | copy-start | bytes 786436
  275.4 6.2 %copy-start.4 = (bf16[1024,2048]{1,0:T(8,128)(2,1)S(1)}, bf16[1024,2048]{1,0:T(8,128)(2,1)}, u32[]{:S(2)}) copy-start(bf16[1024,2048]{1,0:T(8,128)(2,1)} %get-tuple-element.37.n2) | copy-start | bytes 12582916
  275.4 6.2 %copy-start.16 = (bf16[704,2048]{1,0:T(8,128)(2,1)S(1)}, bf16[704,2048]{1,0:T(8,128)(2,1)}, u32[]{:S(2)}) copy-start(bf16[704,2048]{1,0:T(8,128)(2,1)} %get-tuple-element.38) | copy-start | bytes 8650756
  281.7 3.3 copy-start.3
  281.7 3.3 copy-start.17
  285.0 4.3 copy-start.18
  289.2 3.6 copy-start.6
  289.2 3.6 copy-start.7
  289.2 9.3 %copy-start.5 = (bf16[704,1024]{1,0:T(8,128)(2,1)}, bf16[704,1024]{1,0:T(8,128)(2,1)S(1)}, u32[]{:S(2)}) copy-start(bf16[704,1024]{1,0:T(8,128)(2,1)S(1)} %get-tuple-element.59.h_u) | copy-start | bytes 4325380
  292.8 5.1 copy-start.14
  534.9 7.4 %copy-start.10 = (bf16[128,2048]{1,0:T(8,128)(2,1)S(1)}, bf16[128,2048]{1,0:T(8,128)(2,1)}, u32[]{:S(2)}) copy-start(bf16[128,2048]{1,0:T(8,128)(2,1)} %get-tuple-element.54) | copy-start | bytes 1572868
  535.0 13.9 %collective-permute-start = (bf16[4,768,128]{2,1,0:T(8,128)(2,1)}, bf16[4,768,128]{2,1,0:T(8,128)(2,1)}, u32[]{:S(2)}, u32[]{:S(2)}) collective-permute-start(bf16[4,768,128]{2,1,0:T(8,128)(2,1)} %get-tuple-element.53), channel_id=1, source_target_pairs={{0,1},{1,0},{2,3},{3,2},{4,5},{5,4},{6,7},{7,6},{8,9},{9,8},{10,11... | collective-permute-start | bytes 2359304 | tf_op jit(solution)/shard_map/ppermute | solution.py:1126
  545.0 3.8 copy-start.9
  557.9 2.6 copy-start.12
  558.7 5.8 %copy-start.1 = (f32[2048]{0:T(1024)S(1)}, f32[2048]{0:T(1024)}, u32[]{:S(2)}) copy-start(f32[2048]{0:T(1024)} %param.24) | copy-start | bytes 24580

commit v4 on v3

--- a/solution.py
+++ b/solution.py
@@ -375,15 +375,15 @@
         out_side.wait_recv()
         out_next.wait_recv()
 
-    for c in ffn_own:
-        c.wait()
-    for c in ffn_in:
-        c.wait_recv()
     far_ffn, side_ffn = [], []
-    for s, o in shards:
+
+    def start_ffn(i):
+        o = shards[i][1]
+        ffn_own[i].wait()
+        for c in ffn_in[3 * i : 3 * i + 3]:
+            c.wait_recv()
         far_ffn.append([link.remote(o.at[:, pair(zf, c, y)], o.at[:, pair(zf, c, y)], far) for c in (0, 1)])
-    for s, o in shards:
-        side_ffn += [link.remote(o.at[:, pair(zf, c, y)], o.at[:, pair(zf, c, y)], side) for c in (0, 1)]
+        side_ffn.extend(link.remote(o.at[:, pair(zf, c, y)], o.at[:, pair(zf, c, y)], side) for c in (0, 1))
 
     def forward_ffn(i):
         o = shards[i][1]
@@ -391,6 +391,7 @@
             far_ffn[i][c].wait_recv()
             side_ffn.append(link.remote(o.at[:, pair(1 - zf, c, y)], o.at[:, pair(1 - zf, c, y)], side))
 
+    start_ffn(0)
     go_in = [link.remote(go_own, o_go.at[row(r, t)], group[r]) for r in (1, 2)]
     go_core = [link.remote(go_own, o_go.at[row(0, t)], core)]
     link.here(go_own, o_go.at[row(0, t)], keep=True)
@@ -454,6 +455,17 @@
     link.here(raw, o_raw, keep=True)
     link.here(aux, o_aux, keep=True)
 
+    def spread(o, incoming, cores):
+        incoming[1].wait_recv()
+        incoming.append(link.remote(o.at[row(2, t)], o.at[row(3, t)], group[1]))
+        cores.append(link.remote(o.at[row(2, t)], o.at[row(2, t)], core))
+        incoming[0].wait_recv()
+        cores.append(link.remote(o.at[row(1, t)], o.at[row(1, t)], core))
+
+    def spread_last(o, incoming, cores):
+        incoming[2].wait_recv()
+        cores.append(link.remote(o.at[row(3, t)], o.at[row(3, t)], core))
+
     out_in, sq_in = [], []
     for r in (3, 2, 1):
         core_copy(r).wait()
@@ -465,6 +477,8 @@
         sq_in.append(link.remote(sq_half.at[to], sq_peer.at[to], group[r]))
     core_copy(0).wait()
     sq_copy(0).wait()
+    start_ffn(1)
+    spread(o_go, go_in, go_core)
     forward_ffn(0)
     for c in out_in + sq_in:
         c.wait_recv()
@@ -495,22 +509,10 @@
     link.here(res, o_res, keep=True)
     link.here(mo, o_mo, keep=True)
     link.here(sc, o_sc, keep=True)
-
-    def spread(o, incoming, cores):
-        incoming[1].wait_recv()
-        incoming.append(link.remote(o.at[row(2, t)], o.at[row(3, t)], group[1]))
-        cores.append(link.remote(o.at[row(2, t)], o.at[row(2, t)], core))
-        incoming[0].wait_recv()
-        cores.append(link.remote(o.at[row(1, t)], o.at[row(1, t)], core))
-
-    def spread_last(o, incoming, cores):
-        incoming[2].wait_recv()
-        cores.append(link.remote(o.at[row(3, t)], o.at[row(3, t)], core))
-
-    spread(o_go, go_in, go_core)
+    start_ffn(2)
+    spread_last(o_go, go_in, go_core)
+    forward_ffn(1)
     spread(o_n2, n2_in, n2_core)
-    forward_ffn(1)
-    spread_last(o_go, go_in, go_core)
     spread_last(o_n2, n2_in, n2_core)
     forward_ffn(2)
     for c in side_ffn + go_core + n2_core:
@@ -661,21 +663,60 @@
             for c in (0, 1)
         ]
 
-    def first_hop(hid, other, dw, yr):
-        weight_grad(hid, other, dw, 0, 2)
-        sent = [side_send(dw, yr, 0)]
-        weight_grad(hid, other, dw, 2, 2)
-        sent.append(side_send(dw, yr, 1))
+    def add_columns(dw, to, others):
+        size = 64 if dw.shape[0] % 64 == 0 else dw.shape[0]
+
+        def some(j, carry):
+            at_rows = at(j * size, size, size)
+            total = dw[at_rows, to].astype(f32)
+            for ref, cols in others:
+                total = total + ref[at_rows, cols].astype(f32)
+            dw[at_rows, to] = total.astype(bf16)
+            return carry
+
+        lax.fori_loop(0, dw.shape[0] // size, some, 0)
+
+    def part_of(i):
+        return pl.ds(i * 2 * block, 2 * block)
+
+    def second_hop(hop, dw, yr, zr):
+        sent = []
+        for c in (0, 1):
+            hop[c].wait_recv()
+            add_columns(dw, pair(1 - zf, c, y), [(yr, part_of(c))])
+            sent.append(link.remote(dw.at[:, pair(1 - zf, c, y)], zr.at[:, part_of(c)], far))
         return sent
+
+    def last_hop(near, sent, dw, yr, zr, out):
+        for c in (0, 1):
+            near[c].wait_recv()
+            sent[c].wait_recv()
+            add_columns(dw, pair(zf, c, y), [(yr, part_of(2 + c)), (zr, part_of(c))])
+
+        def owner(r):
+            fx = x if r in (0, 2) else 1 - x
+            fzn = zn if r in (0, 1) else 1 - zn
+            return at((zf * 8 + fzn * 4 + y * 2 + fx) * block, block, block)
+
+        link.here(dw.at[:, owner(0)], out.at[q[0]], keep=True)
+        return [link.remote(dw.at[:, owner(r)], out.at[q[0]], group[r]) for r in (1, 2, 3)]
 
     for c in get_d:
         c.wait()
-    hop_d = first_hop(hid_a, left, dw_d, yr_d)
+    weight_grad(hid_a, left, dw_d, 0, 2)
+    hop_d = side_send(dw_d, yr_d, 0)
+    weight_grad(hid_a, left, dw_d, 2, 2)
     get_u = link.here(h_u, hid_a)
     get_n1 = link.here(n1, left)
     for c in get_g:
         c.wait()
-    hop_g = first_hop(hid_b, right, dw_g, yr_g)
+    weight_grad(hid_b, right, dw_g, 0, 2)
+    hop_g = side_send(dw_g, yr_g, 0)
+    weight_grad(hid_b, right, dw_g, 2, 2)
+    get_u.wait()
+    weight_grad(hid_a, right, dw_u, 0, 4)
+    far_d = second_hop(hop_d, dw_d, yr_d, zr_d)
+    hop_u = side_send(dw_u, yr_u, 0)
 
     for c in two_peer:
         c.wait_recv()
@@ -717,49 +758,8 @@
     gm_here = [link.here(gm_own, gmix.at[row(0, t)]), link.here(scalars, scal(0, t))]
     blk_core = [link.remote(p_block.at[row(r, 1 - t)], core_blk.at[rel(r)], core) for r in (3, 2, 1, 0)]
 
-    get_u.wait()
-    hop_u = first_hop(hid_a, right, dw_u, yr_u)
-
-    def add_columns(dw, to, others):
-        size = 64 if dw.shape[0] % 64 == 0 else dw.shape[0]
-
-        def some(j, carry):
-            at_rows = at(j * size, size, size)
-            total = dw[at_rows, to].astype(f32)
-            for ref, cols in others:
-                total = total + ref[at_rows, cols].astype(f32)
-            dw[at_rows, to] = total.astype(bf16)
-            return carry
-
-        lax.fori_loop(0, dw.shape[0] // size, some, 0)
-
-    def part_of(i):
-        return pl.ds(i * 2 * block, 2 * block)
-
-    def second_hop(hop, dw, yr, zr):
-        sent = []
-        for c in (0, 1):
-            hop[0][c].wait_recv()
-            add_columns(dw, pair(1 - zf, c, y), [(yr, part_of(c))])
-            sent.append(link.remote(dw.at[:, pair(1 - zf, c, y)], zr.at[:, part_of(c)], far))
-        return sent
-
-    def last_hop(hop, sent, dw, yr, zr, out):
-        for c in (0, 1):
-            hop[1][c].wait_recv()
-            sent[c].wait_recv()
-            add_columns(dw, pair(zf, c, y), [(yr, part_of(2 + c)), (zr, part_of(c))])
-
-        def owner(r):
-            fx = x if r in (0, 2) else 1 - x
-            fzn = zn if r in (0, 1) else 1 - zn
-            return at((zf * 8 + fzn * 4 + y * 2 + fx) * block, block, block)
-
-        link.here(dw.at[:, owner(0)], out.at[q[0]], keep=True)
-        return [link.remote(dw.at[:, owner(r)], out.at[q[0]], group[r]) for r in (1, 2, 3)]
-
-    far_d = second_hop(hop_d, dw_d, yr_d, zr_d)
-
+    far_g = second_hop(hop_g, dw_g, yr_g, zr_g)
+    near_d = side_send(dw_d, yr_d, 1)
     gm_in[1].wait_recv()
     gm_in.append(link.remote(gmix.at[row(2, t)], gmix.at[row(3, t)], group[1]))
     gm_core.append(link.remote(gmix.at[row(2, t)], gmix.at[row(2, t)], core))
@@ -768,9 +768,11 @@
     for i, r in enumerate((1, 2, 3)):
         sc_in[i].wait_recv()
         gm_core.append(link.remote(scal(r, t), scal(r, t), core))
-    far_g = second_hop(hop_g, dw_g, yr_g, zr_g)
+    near_g = side_send(dw_g, yr_g, 1)
+    far_u = second_hop(hop_u, dw_u, yr_u, zr_u)
     gm_in[2].wait_recv()
     gm_core.append(link.remote(gmix.at[row(3, t)], gmix.at[row(3, t)], core))
+    near_u = side_send(dw_u, yr_u, 1)
 
     link.sent(two_peer)
     blk_own = [link.here(p_block.at[row(r, t)], own.at[rel(r)]) for r in (3, 2, 1, 0)]
@@ -868,7 +870,9 @@
     for r in (3, 2, 1, 0):
         one_core(r).wait_send()
 
-    hop_mix = first_hop(grads_t, left, dw_mix, yr_mix)
+    weight_grad(grads_t, left, dw_mix, 0, 2)
+    hop_mix = side_send(dw_mix, yr_mix, 0)
+    weight_grad(grads_t, left, dw_mix, 2, 2)
 
     def out_columns(i, carry):
         to = at(i * (4 * block), 4 * block, 4 * block)
@@ -898,8 +902,16 @@
     def _():
         out_side.start()
 
-    far_u = second_hop(hop_u, dw_u, yr_u, zr_u)
-    back_d = last_hop(hop_d, far_d, dw_d, yr_d, zr_d, o_d)
+    near_mix = side_send(dw_mix, yr_mix, 1)
+    back_d = last_hop(near_d, far_d, dw_d, yr_d, zr_d, o_d)
+    back_g = last_hop(near_g, far_g, dw_g, yr_g, zr_g, o_g)
+    far_mix = second_hop(hop_mix, dw_mix, yr_mix, zr_mix)
+
+    @pl.when(t == y)
+    def _():
+        out_side.wait_recv()
+        add_columns(dw_out, pl.ds(0, width), [(yr_out, pl.ds(0, width))])
+        out_far.start()
 
     for c in one_peer:
         c.wait_recv()
@@ -949,16 +961,8 @@
     core_in_now = core_blk
     blk_peer = over_cores(blk_core, [[c] for c in blk_own], own_rows, peer_blk)
     next_turn()
-    far_mix = second_hop(hop_mix, dw_mix, yr_mix, zr_mix)
-
-    @pl.when(t == y)
-    def _():
-        out_side.wait_recv()
-        add_columns(dw_out, pl.ds(0, width), [(yr_out, pl.ds(0, width))])
-        out_far.start()
-
+    back_u = last_hop(near_u, far_u, dw_u, yr_u, zr_u, o_u)
     next_turn()
-    back_g = last_hop(hop_g, far_g, dw_g, yr_g, zr_g, o_g)
     next_turn()
     for c in blk_peer:
         c.wait_recv()
@@ -975,10 +979,9 @@
     lax.fori_loop(0, share // step, block_rows, 0)
     link.here(gm_own, o_blk, keep=True)
     next_turn()
-    back_u = last_hop(hop_u, far_u, dw_u, yr_u, zr_u, o_u)
     next_turn()
     link.here(vec.at[5], o_vec, keep=True)
-    back_mix = last_hop(hop_mix, far_mix, dw_mix, yr_mix, zr_mix, o_mix)
+    back_mix = last_hop(near_mix, far_mix, dw_mix, yr_mix, zr_mix, o_mix)
 
     @pl.when(t == y)
     def _():

time: 573 us -> 515 us (0.90)
  Pallas kernels: 475 us -> 417 us
    pallas_call x1, Pallas kernels: 244 us -> 198 us  [front(): pl.pallas_call(front_kernel, in_specs=[any_spec] * 7 + [any_spec] + [vmem...]
    pallas_call x1, Pallas kernels: 231 us -> 219 us  [back(): pl.pallas_call(back_kernel, in_specs=[any_spec] * 14 + [vmem_spec] * 7, o...]
  transfers between devices with their start and end apart: 1 -> 1, of which waited for: 0 -> 0; matrix products, arithmetic and copies ran while one was open for 2% -> 3% of each run, Pallas kernels for 0% -> 0%
where the time goes in v4:
time: 515 us; the launch traced here: 506 us
  Pallas kernels  417 us (81%)
  local copies, waits for them, and re-layouts  35.4 us (7%)
  matrix products  27.6 us (5%)
  other arithmetic  24.2 us (5%)
    pallas_call x1, Pallas kernels, back(): pl.pallas_call(back_kernel, in_specs=[any_spec] * 14 + [vmem_spec] * 7, o...  219 us
    pallas_call x1, Pallas kernels, front(): pl.pallas_call(front_kernel, in_specs=[any_spec] * 7 + [any_spec] + [vmem...  198 us
    dot_general x3, matrix products, cross_rows(): lax.dot_general(first_op, second_op, (((0,), (0,)), ((), ())), preferred_...  13.9 us
    dot_general x3, matrix products, cross_cols(): lax.dot_general(first_op, second_op, (((1,), (1,)), ((), ())), preferred_...  13.7 us
  transfers between devices with their start and end apart: 1, of which 0 were waited for; matrix products, arithmetic and copies ran while one was open for 3% of the time, Pallas kernels for 0%

profile of v4, /device:TPU:0, one launch (start us, length us, event | category | flops | bytes accessed | tf_op | source)
XLA Modules:
  0.0 506.4 jit_solution(10432028094374308582)
XLA Ops:
  1.4 1.5 multiply_reduce_fusion
  2.9 1.5 convert_element_type.97
  8.7 2.2 reshape.190
  13.2 2.3 copy.64
  15.5 2.2 copy.65
  18.3 1.8 reshape.199
  26.1 2.0 pad_maximum_fusion.s_mix
  28.1 2.3 multiply_convert_fusion.4
  31.1 197.7 %front.1 = (bf16[2048,768]{1,0:T(8,128)(2,1)}, bf16[256,2048]{1,0:T(8,128)(2,1)}, bf16[704,2048]{1,0:T(8,128)(2,1)}, bf16[704,2048]{1,0:T(8,128)(2,1)}, bf16[704...) custom-call(bf16[4,128,768]{2,1,0:T(8,128)(2,1)} %pad_maximum_fusion, ...), custom_call_target="tpu_custom_call" | custom-call | tf_op jit(solution)/shard_map/front/pallas_call | solution.py:575
  228.8 6.2 %fusion.11 = f32[704,1024]{1,0:T(8,128)S(1)} fusion(bf16[704,2048]{1,0:T(8,128)(2,1)} %get-tuple-element.36, bf16[1024,2048]{1,0:T(8,128)(2,1)} %get-tuple-element.37.n2), kind=kOutput, calls=%fused_computation.61 | convolution fusion | flops 2952790016 | bytes 9961472 | tf_op jit(solution)/shard_map/dot_general | solution.py:44
  235.1 3.3 fusion.12
  238.4 4.2 multiply_convert_fusion
  242.7 3.5 fusion.13
  246.2 5.1 %convolution_convert_fusion.p_block = bf16[1024,2048]{1,0:T(8,128)(2,1)} fusion(bf16[704,1024]{1,0:T(8,128)(2,1)S(1)} %get-tuple-element.61.h_d, bf16[704,2048]{1,0:T(8,128)(2,1)S(1)} %copy-done.17), kind=kOutput, calls=%fused_computation.1 | convolution fusion | flops 2954887168 | bytes 8519680 | tf_op jit(solution)/shard_map/dot_general | solution.py:38
  251.9 5.3 %add_convert_fusion.p_two = bf16[1024,2048]{1,0:T(8,128)(2,1)} fusion(f32[1024,2048]{1,0:T(8,128)S(1)} %fusion.13, bf16[704,1024]{1,0:T(8,128)(2,1)S(1)} %get-tuple-element.59.h_u, bf16[704,2048]{1,0:T(8,128)(2,1)S(1)} %copy-done.16), kind=kOutput, calls=%fused_computation | convolution fusion | flops 2956984320 | bytes 16908288 | tf_op jit(solution)/shard_map/dot_general | solution.py:38
  257.3 219.2 %back.1 = (bf16[4,704,128]{2,1,0:T(8,128)(2,1)}, bf16[4,704,128]{2,1,0:T(8,128)(2,1)}, bf16[4,704,128]{2,1,0:T(8,128)(2,1)}, bf16[4,768,128]{2,1,0:T(8,128)(2,1)...) custom-call(bf16[704,1024]{1,0:T(8,128)(2,1)} %copy-done.7, ...), custom_call_target="tpu_custom_call" | custom-call | tf_op jit(solution)/shard_map/back/pallas_call | solution.py:1072
  485.0 1.5 copy.71
  486.5 1.5 copy.72
  488.0 2.3 bitcast_convert_fusion
  493.0 2.0 copy.68
  495.0 1.8 squeeze.48
  497.6 1.8 squeeze.49
  500.2 1.8 squeeze.50
  502.9 3.1 copy.85
  (85 shorter events, 28.0 us)
Async XLA Ops:
  0.6 17.6 %copy-start = (f32[2048]{0:T(1024)S(1)}, f32[2048]{0:T(1024)}, u32[]{:S(2)}) copy-start(f32[2048]{0:T(1024)} %param.24) | copy-start | bytes 24580
  0.7 3.7 copy-start.11
  8.7 9.2 %copy-start.15 = (s32[2]{0:T(128)S(1)}, s32[2]{0:T(128)}, u32[]{:S(2)}) copy-start(s32[2]{0:T(128)} %param.27) | copy-start | bytes 28
  10.9 12.3 %copy-start.2 = (bf16[256,2048]{1,0:T(8,128)(2,1)S(1)}, bf16[256,2048]{1,0:T(8,128)(2,1)}, u32[]{:S(2)}) copy-start(bf16[256,2048]{1,0:T(8,128)(2,1)} %param.15) | copy-start | bytes 3145732
  10.9 12.4 %copy-start.13 = (f32[2048]{0:T(1024)S(1)}, f32[2048]{0:T(1024)}, u32[]{:S(2)}) copy-start(f32[2048]{0:T(1024)} %param.23) | copy-start | bytes 24580
  13.2 12.9 %copy-start.8 = (bf16[4,128,256]{2,1,0:T(8,128)(2,1)S(1)}, bf16[4,128,256]{2,1,0:T(8,128)(2,1)}, u32[]{:S(2)}) copy-start(bf16[4,128,256]{2,1,0:T(8,128)(2,1)} %reshape.195) | copy-start | bytes 786436
  228.8 6.2 %copy-start.4 = (bf16[1024,2048]{1,0:T(8,128)(2,1)S(1)}, bf16[1024,2048]{1,0:T(8,128)(2,1)}, u32[]{:S(2)}) copy-start(bf16[1024,2048]{1,0:T(8,128)(2,1)} %get-tuple-element.37.n2) | copy-start | bytes 12582916
  228.8 6.2 %copy-start.16 = (bf16[704,2048]{1,0:T(8,128)(2,1)S(1)}, bf16[704,2048]{1,0:T(8,128)(2,1)}, u32[]{:S(2)}) copy-start(bf16[704,2048]{1,0:T(8,128)(2,1)} %get-tuple-element.38) | copy-start | bytes 8650756
  235.1 3.3 copy-start.3
  235.1 3.3 copy-start.17
  238.4 4.3 copy-start.18
  242.6 3.6 copy-start.6
  242.6 3.6 copy-start.7
  242.6 9.3 %copy-start.5 = (bf16[704,1024]{1,0:T(8,128)(2,1)}, bf16[704,1024]{1,0:T(8,128)(2,1)S(1)}, u32[]{:S(2)}) copy-start(bf16[704,1024]{1,0:T(8,128)(2,1)S(1)} %get-tuple-element.59.h_u) | copy-start | bytes 4325380
  246.2 5.1 %copy-start.14 = (f32[2048]{0:T(1024)S(1)}, f32[2048]{0:T(1024)}, u32[]{:S(2)}) copy-start(f32[2048]{0:T(1024)} %param.25) | copy-start | bytes 24580
  476.5 7.4 %copy-start.10 = (bf16[128,2048]{1,0:T(8,128)(2,1)S(1)}, bf16[128,2048]{1,0:T(8,128)(2,1)}, u32[]{:S(2)}) copy-start(bf16[128,2048]{1,0:T(8,128)(2,1)} %get-tuple-element.54) | copy-start | bytes 1572868
  476.5 13.9 %collective-permute-start = (bf16[4,768,128]{2,1,0:T(8,128)(2,1)}, bf16[4,768,128]{2,1,0:T(8,128)(2,1)}, u32[]{:S(2)}, u32[]{:S(2)}) collective-permute-start(bf16[4,768,128]{2,1,0:T(8,128)(2,1)} %get-tuple-element.53), channel_id=1, source_target_pairs={{0,1},{1,0},{2,3},{3,2},{4,5},{5,4},{6,7},{7,6},{8,9},{9,8},{10,11... | collective-permute-start | bytes 2359304 | tf_op jit(solution)/shard_map/ppermute | solution.py:1129
  486.5 3.8 copy-start.9
  499.4 2.6 copy-start.12
  500.2 5.8 %copy-start.1 = (f32[2048]{0:T(1024)S(1)}, f32[2048]{0:T(1024)}, u32[]{:S(2)}) copy-start(f32[2048]{0:T(1024)} %param.24) | copy-start | bytes 24580

commit v5 on v4

--- a/solution.py
+++ b/solution.py
@@ -286,18 +286,20 @@
 
 
 def front_kernel(
-    s_mix, s_out, s_g, s_u, s_d, n1_own, go_own, aux_own, par, inp, gain2,
-    o_mix, o_out, o_g, o_u, o_d, o_n1, o_go, o_n2, o_pre, o_state, o_raw, o_res, o_mo, o_sc, o_aux,
-    w_mix, w_out, n1, aux, pre, state, raw, part, core_in, half, peer_in,
+    s_in, s_fg, s_og, s_out, w_g, w_u, s_d, cot, tok, gains, table, sizes,
+    o_mix, o_out, o_g, o_u, o_d, o_n1, o_go, o_n2, o_pre, o_state, o_raw, o_res, o_mo, o_sc, o_aux, o_par,
+    w_mix, w_out, n1, aux, pre, state, raw, part, core_in, half, peer_in, par, wide_g, wide_u, s_g, s_u, go_own, bound_row,
     sq, sq_core, sq_half, sq_peer, res, mo, sc, n2, decay, add,
     send, recv, local, core_send, core_recv, sqc_send, sqc_recv, out_send, out_recv,
 ):
     me, t, (zf, zn, y, x), q, group, far, side, core = position()
-    share, width = inp.shape
-    rows = 2 * share
+    rows, width = tok.shape
+    share = rows // 2
     block = s_out.shape[0]
     feat = par.shape[1]
+    hid = s_d.shape[0] // 4
     link = Copies(send, recv, local)
+    get_g, get_u, get_cot = link.here(w_g, wide_g), link.here(w_u, wide_u), link.here(cot, go_own)
     meet(group[1:] + [far, side, core])
 
     def at(start, size, unit):
@@ -311,8 +313,17 @@
     def row(r, tt):
         return at(r * rows + tt * share, share, share)
 
-    mix_in = [link.remote(s_mix.at[q[r]], w_mix.at[mine], group[r]) for r in (1, 2, 3)]
-    mix_own = link.here(s_mix.at[q[0]], w_mix.at[mine])
+    def columns(r, fz):
+        fx = x if r in (0, 2) else 1 - x
+        fzn = zn if r in (0, 1) else 1 - zn
+        return at((fz * 8 + fzn * 4 + t * 2 + fx) * block, block, block)
+
+    mix_in, mix_own = [], []
+    for k, s in enumerate((s_in, s_fg, s_og)):
+        for fz in (0, 1):
+            to = w_mix.at[mine, pl.ds(k * feat + fz * block, block)]
+            mix_in += [link.remote(s.at[:, columns(r, fz)], to, group[r]) for r in (1, 2, 3)]
+            mix_own.append(link.here(s.at[:, columns(0, fz)], to))
     out_rows = [at(z * block, block, block) for z in (zf, 1 - zf)]
 
     def out_copy(k, src, dst, device):
@@ -336,11 +347,39 @@
         out_side.start()
         out_here.start()
 
-    aux_in = [link.remote(aux_own, aux.at[r], group[r]) for r in (1, 2, 3)]
-    aux_mine = link.here(aux_own, aux.at[0])
-    n1_in = [link.remote(n1_own.at[at(t * share, share, share)], n1.at[row(r, t)], group[r]) for r in (1, 2)]
-    n1_mine = link.here(n1_own, n1.at[pl.ds(0, rows)])
-    mix_own.wait()
+    norm_row = gains[0:1, :]
+
+    def norm_rows(first):
+        def some(j, carry):
+            to = at(first + j * 16, 16, 16)
+            value = tok[to, :].astype(f32)
+            s = lax.rsqrt(jnp.mean(value * value, axis=1, keepdims=True) + epsilon)
+            n1[to, :] = (value * s * norm_row).astype(bf16)
+            return carry
+
+        lax.fori_loop(0, share // 16, some, 0)
+
+    norm_rows(t * share)
+    n1_in = [link.remote(n1.at[row(0, t)], n1.at[row(r, t)], group[r]) for r in (1, 2)]
+
+    count = sizes.shape[0] - 1
+    slot_len = lax.shift_right_logical(jnp.int32(rows), sizes[count])
+    position_row = lax.broadcasted_iota(jnp.int32, (1, rows), 1)
+    slot = jnp.zeros((1, rows), jnp.int32)
+    for j in range(1, count):
+        slot = slot + (position_row >= j * slot_len).astype(jnp.int32)
+    limit = jnp.zeros((1, rows), jnp.int32)
+    for j in range(count):
+        limit = limit + jnp.where(slot == j, sizes[j], 0)
+    offset = position_row - slot * slot_len
+    aux[0] = jnp.zeros(aux.shape[1:], f32)
+    aux[0, 0:1, :] = (offset < limit).astype(f32)
+    aux[0, 1:2, :] = (offset > 0).astype(f32)
+    aux_in = [link.remote(aux.at[0], aux.at[r], group[r]) for r in (1, 2, 3)]
+
+    norm_rows((1 - t) * share)
+    for c in mix_own:
+        c.wait()
     for c in mix_in:
         c.wait_recv()
     far_mix = [link.remote(w_mix.at[pair(zf, c, y)], w_mix.at[pair(zf, c, y)], far) for c in (0, 1)]
@@ -352,9 +391,43 @@
     n1_core.append(link.remote(n1.at[row(1, t)], n1.at[row(1, t)], core))
     shards = ((s_g, o_g), (s_u, o_u), (s_d, o_d))
     ffn_in, ffn_own = [], []
-    for s, o in shards:
-        ffn_in += [link.remote(s.at[q[r]], o.at[:, mine], group[r]) for r in (1, 2, 3)]
-        ffn_own.append(link.here(s.at[q[0]], o.at[:, mine]))
+
+    def turn_round(wide, tall):
+        size = min(128, wide.shape[1])
+
+        def some(j, carry):
+            to = at(j * size, size, size)
+            tall[to, :] = wide[:, to].astype(f32).T.astype(bf16)
+            return carry
+
+        lax.fori_loop(0, wide.shape[1] // size, some, 0)
+
+    def leave(s, o):
+        units = [at(q[r] * hid, hid, 16) for r in range(4)]
+        ffn_in.extend(link.remote(s.at[units[r]], o.at[:, mine], group[r]) for r in (1, 2, 3))
+        ffn_own.append(link.here(s.at[units[0]], o.at[:, mine]))
+
+    get_g.wait()
+    turn_round(wide_g, s_g)
+    leave(s_g, o_g)
+    get_u.wait()
+    turn_round(wide_u, s_u)
+    leave(s_u, o_u)
+    leave(s_d, o_d)
+
+    logits = table[...]
+    powers = jnp.exp(logits - jnp.max(logits, axis=0, keepdims=True))
+    layer_ids = lax.broadcasted_iota(jnp.int32, logits.shape, 0)
+    picked = jnp.where((layer_ids >= 1) & (layer_ids <= LAYER), powers, 0.0)
+    bound_row[0:1, :] = jnp.sum(picked, axis=0, keepdims=True) / jnp.sum(powers, axis=0, keepdims=True)
+    for fz in (0, 1):
+        par[0:1, fz * block : (fz + 1) * block] = bound_row[0:1, columns(0, fz)]
+        par[1:2, fz * block : (fz + 1) * block] = gains[1:2, columns(0, fz)]
+    get_cot.wait()
+    valid_rows = aux[0].T[:, 0:1]
+    first_half = lax.broadcasted_iota(jnp.int32, (share, 1), 0) * 0 + t
+    valid_half = jnp.where(first_half == 0, valid_rows[:share], valid_rows[share:])
+    go_own[...] = (go_own[...].astype(f32) * valid_half).astype(bf16)
     n1_in[2].wait_recv()
     n1_core.append(link.remote(n1.at[row(3, t)], n1.at[row(3, t)], core))
     for c in (0, 1):
@@ -396,8 +469,6 @@
     go_core = [link.remote(go_own, o_go.at[row(0, t)], core)]
     link.here(go_own, o_go.at[row(0, t)], keep=True)
 
-    n1_mine.wait()
-    aux_mine.wait()
     for c in side_mix + n1_core + aux_in:
         c.wait_recv()
 
@@ -454,6 +525,7 @@
     link.here(state, o_state, keep=True)
     link.here(raw, o_raw, keep=True)
     link.here(aux, o_aux, keep=True)
+    link.here(par, o_par, keep=True)
 
     def spread(o, incoming, cores):
         incoming[1].wait_recv()
@@ -495,11 +567,11 @@
         for r in (1, 2, 3):
             total = total + peer_in[at(r * share + i * chunk, chunk, chunk), :].astype(f32)
         mixed = total * sc[to, 0:1]
-        value = inp[to, :] + mixed
+        value = tok[at(t * share + i * chunk, chunk, chunk), :].astype(f32) + mixed
         mo[to, :] = mixed
         res[to, :] = value
         scale_two = lax.rsqrt(jnp.mean(value * value, axis=1, keepdims=True) + epsilon)
-        n2[to, :] = (value * scale_two * gain2[...]).astype(bf16)
+        n2[to, :] = (value * scale_two * gains[2:3, :]).astype(bf16)
         return carry
 
     lax.fori_loop(0, share // chunk, finish, 0)
@@ -520,11 +592,11 @@
     link.close()
 
 
-def front(s_mix, s_out, s_g, s_u, s_d, n1_own, go_own, aux_own, par, inp, gain2):
-    share, width = inp.shape
-    rows, group_rows = 2 * share, 8 * share
-    feat, hid = par.shape[1], s_g.shape[1]
+def front(s_in, s_fg, s_og, s_out, w_g, w_u, s_d, cot, tok, gains, table, sizes):
+    rows, width = tok.shape
+    share, group_rows = rows // 2, 4 * rows
     block = s_out.shape[0]
+    feat, hid = 2 * block, s_d.shape[0] // 4
     lanes = 128 if feat % 128 == 0 else feat
     any_spec = pl.BlockSpec(memory_space=pl.ANY)
     vmem_spec = pl.BlockSpec(memory_space=pltpu.VMEM)
@@ -544,13 +616,14 @@
         made((share, width), f32),
         made((share, width), f32),
         made((share, 128), f32),
-        made((4,) + aux_own.shape, f32),
+        made((4, 8, rows), f32),
+        made((2, feat), f32),
     ]
     scratch = [
         pltpu.VMEM((width, 3 * feat), bf16),
         pltpu.VMEM((feat, width), bf16),
         pltpu.VMEM((group_rows, width), bf16),
-        pltpu.VMEM((4,) + aux_own.shape, f32),
+        pltpu.VMEM((4, 8, rows), f32),
         pltpu.VMEM((group_rows, 3 * feat), f32),
         pltpu.VMEM((group_rows, feat), f32),
         pltpu.VMEM((group_rows, feat), bf16),
@@ -558,6 +631,13 @@
         pltpu.VMEM((4 * share, width), bf16),
         pltpu.VMEM((4 * share, width), bf16),
         pltpu.VMEM((4 * share, width), bf16),
+        pltpu.VMEM((2, feat), f32),
+        pltpu.VMEM(w_g.shape, bf16),
+        pltpu.VMEM(w_u.shape, bf16),
+        pltpu.VMEM((4 * hid, block), bf16),
+        pltpu.VMEM((4 * hid, block), bf16),
+        pltpu.VMEM((share, width), bf16),
+        pltpu.VMEM((8, width), f32),
         pltpu.VMEM((group_rows, lanes), f32),
         pltpu.VMEM((4 * share, lanes), f32),
         pltpu.VMEM((4 * share, lanes), f32),
@@ -568,13 +648,13 @@
         pltpu.VMEM((share, width), bf16),
         pltpu.VMEM((rows, feat), f32),
         pltpu.VMEM((rows, feat), f32),
-        pltpu.SemaphoreType.DMA((68,)),
-        pltpu.SemaphoreType.DMA((68,)),
-        pltpu.SemaphoreType.DMA((24,)),
+        pltpu.SemaphoreType.DMA((88,)),
+        pltpu.SemaphoreType.DMA((88,)),
+        pltpu.SemaphoreType.DMA((32,)),
     ] + [pltpu.SemaphoreType.DMA((4,))] * 6
     return pl.pallas_call(
         front_kernel,
-        in_specs=[any_spec] * 7 + [any_spec] + [vmem_spec] * 3,
+        in_specs=[any_spec] * 8 + [vmem_spec] * 3 + [pl.BlockSpec(memory_space=pltpu.SMEM)],
         out_specs=[any_spec] * len(outs),
         out_shape=outs,
         scratch_shapes=scratch,
@@ -582,22 +662,22 @@
             collective_id=1, has_side_effects=True, vmem_limit_bytes=56 << 20
         ),
         name="front",
-    )(s_mix, s_out, s_g, s_u, s_d, n1_own, go_own, aux_own, par, inp, gain2)
+    )(s_in, s_fg, s_og, s_out, w_g, w_u, s_d, cot, tok, gains, table, sizes)
 
 
 def back_kernel(
     h_d, h_g, h_u, n2, go, p_two, p_block, n1, w_mix_in, w_out_in, pre, state, raw, aux_in,
-    par, inp, res, mo, sc, go_own, gains,
+    par, tok, res, mo, sc, gains,
     o_g, o_u, o_d, o_mix, o_out, o_tok, o_blk, o_vec,
     left, right, gmix, dw_d, dw_g, dw_u, dw_mix, yr_d, yr_g, yr_u, yr_mix, zr_d, zr_g, zr_u, zr_mix,
     own, half, core_in, core_blk, peer_in, peer_blk, w_mix, w_out, aux, pre_b, state_b, raw_b,
     grads, grads_t, decay, add, hold, yr_out, zr_out, hid_a, hid_b,
-    gres, gm_own, scalars, scal_all, sums, vec, vec_in,
+    gres, gm_own, go_own, scalars, scal_all, sums, vec, vec_in,
     send, recv, local, core_send, core_recv, out_send, out_recv, piece_sem,
 ):
     me, t, (zf, zn, y, x), q, group, far, side, core = position()
-    share, width = inp.shape
-    rows = 2 * share
+    rows, width = tok.shape
+    share = rows // 2
     block = width // 16
     feat = par.shape[1]
     link = Copies(send, recv, local)
@@ -619,6 +699,7 @@
     two_own = [link.here(p_two.at[row(r, t)], own.at[rel(r)]) for r in (3, 2, 1, 0)]
     get_d = [link.here(h_d, hid_a), link.here(go, left)]
     get_g = [link.here(h_g, hid_b), link.here(n2, right)]
+    get_go = link.here(go.at[row(0, t)], go_own)
     get_aux = [link.here(aux_in, aux), link.here(w_out_in, w_out), link.here(w_mix_in, w_mix)]
 
     def over_cores(arrived, mine, source, peers):
@@ -651,30 +732,44 @@
 
         def columns(i, carry):
             to = at(((1 - zf) * 2 + i - (i // 2) * 4 * (1 - zf)) * wide, wide, wide)
-            dw[:, to] = jnp.dot(hid[...], other[:, to], preferred_element_type=f32).astype(bf16)
+            made = jnp.dot(hid[...], other[:, to], preferred_element_type=f32).astype(bf16)
+            if len(dw.shape) == 2:
+                dw[:, to] = made
+            else:
+                dw[:, :, :, to] = made.reshape(dw.shape[:3] + (wide,))
             return carry
 
         lax.fori_loop(first, first + count, columns, 0)
+
+    def cut(ref, cols):
+        return ref.at[:, cols] if len(ref.shape) == 2 else ref.at[:, :, :, cols]
 
     def side_send(dw, yr, slot):
         fz = 1 - zf if slot == 0 else zf
         return [
-            link.remote(dw.at[:, pair(fz, c, 1 - y)], yr.at[:, pl.ds((slot * 2 + c) * 2 * block, 2 * block)], side)
+            link.remote(cut(dw, pair(fz, c, 1 - y)), cut(yr, pl.ds((slot * 2 + c) * 2 * block, 2 * block)), side)
             for c in (0, 1)
         ]
 
     def add_columns(dw, to, others):
-        size = 64 if dw.shape[0] % 64 == 0 else dw.shape[0]
+        if len(dw.shape) == 2:
+            size = 64 if dw.shape[0] % 64 == 0 else dw.shape[0]
+            steps = dw.shape[0] // size
+        else:
+            steps = dw.shape[0] * dw.shape[1]
 
         def some(j, carry):
-            at_rows = at(j * size, size, size)
-            total = dw[at_rows, to].astype(f32)
+            if len(dw.shape) == 2:
+                lead = (at(j * size, size, size),)
+            else:
+                lead = (j // dw.shape[1], j % dw.shape[1], slice(None))
+            total = dw[lead + (to,)].astype(f32)
             for ref, cols in others:
-                total = total + ref[at_rows, cols].astype(f32)
-            dw[at_rows, to] = total.astype(bf16)
+                total = total + ref[lead + (cols,)].astype(f32)
+            dw[lead + (to,)] = total.astype(bf16)
             return carry
 
-        lax.fori_loop(0, dw.shape[0] // size, some, 0)
+        lax.fori_loop(0, steps, some, 0)
 
     def part_of(i):
         return pl.ds(i * 2 * block, 2 * block)
@@ -684,7 +779,7 @@
         for c in (0, 1):
             hop[c].wait_recv()
             add_columns(dw, pair(1 - zf, c, y), [(yr, part_of(c))])
-            sent.append(link.remote(dw.at[:, pair(1 - zf, c, y)], zr.at[:, part_of(c)], far))
+            sent.append(link.remote(cut(dw, pair(1 - zf, c, y)), cut(zr, part_of(c)), far))
         return sent
 
     def last_hop(near, sent, dw, yr, zr, out):
@@ -698,8 +793,15 @@
             fzn = zn if r in (0, 1) else 1 - zn
             return at((zf * 8 + fzn * 4 + y * 2 + fx) * block, block, block)
 
-        link.here(dw.at[:, owner(0)], out.at[q[0]], keep=True)
-        return [link.remote(dw.at[:, owner(r)], out.at[q[0]], group[r]) for r in (1, 2, 3)]
+        if len(dw.shape) == 2:
+            place = out.at[q[0]]
+            link.here(dw.at[:, owner(0)], place, keep=True)
+            return [link.remote(dw.at[:, owner(r)], place, group[r]) for r in (1, 2, 3)]
+        place = out.at[:, :, zn, t, x]
+        kept = link.here(cut(dw, owner(0)), place)
+        sent = [link.remote(cut(dw, owner(r)), place, group[r]) for r in (1, 2, 3)]
+        kept.wait()
+        return sent
 
     for c in get_d:
         c.wait()
@@ -720,7 +822,8 @@
 
     for c in two_peer:
         c.wait_recv()
-    gain_two = gains[1:2, :]
+    get_go.wait()
+    gain_two = gains[2:3, :]
     sums[...] = jnp.zeros_like(sums)
     step = 16
 
@@ -922,7 +1025,7 @@
         total = one_rows(0, j) + core_in[to, :].astype(f32)
         for r in (0, 1, 2):
             total = total + peer_in[at(r * share + j * step, step, step), :].astype(f32)
-        value = inp[to, :]
+        value = tok[at(t * share + j * step, step, step), :].astype(f32)
         s = lax.rsqrt(jnp.mean(value * value, axis=1, keepdims=True) + epsilon)
         weighted = total * gain_one
         gres[to, :] = (
@@ -1006,15 +1109,18 @@
         out_side.wait_send()
         out_core.wait_recv()
 
-    for c in back_d + back_g + back_u + back_mix + [tok_core]:
+    for c in back_mix:
+        c.wait_recv()
+    mix_core = link.remote(o_mix.at[:, :, :, t], o_mix.at[:, :, :, t], core)
+    for c in back_d + back_g + back_u + [mix_core, tok_core]:
         c.wait_recv()
     link.close()
 
 
 def back(*arrays):
-    par, inp = arrays[14], arrays[15]
-    share, width = inp.shape
-    rows, group_rows = 2 * share, 8 * share
+    par, tok = arrays[14], arrays[15]
+    rows, width = tok.shape
+    share, group_rows = rows // 2, 4 * rows
     feat, hid, block = par.shape[1], arrays[0].shape[0], width // 16
     made = jax.ShapeDtypeStruct
     vm = pltpu.VMEM
@@ -1022,7 +1128,7 @@
         made((4, hid, block), bf16),
         made((4, hid, block), bf16),
         made((4, hid, block), bf16),
-        made((4, 3 * feat, block), bf16),
+        made((3, 2, 2, 2, 2, block, block), bf16),
         made((block, width), bf16),
         made((rows, width), f32),
         made((share, width), bf16),
@@ -1031,11 +1137,11 @@
     scratch = (
         [vm((group_rows, width), bf16)] * 3
         + [vm((hid, width), bf16)] * 3
-        + [vm((3 * feat, width), bf16)]
+        + [vm((3, 2, block, width), bf16)]
         + [vm((hid, width // 2), bf16)] * 3
-        + [vm((3 * feat, width // 2), bf16)]
+        + [vm((3, 2, block, width // 2), bf16)]
         + [vm((hid, width // 4), bf16)] * 3
-        + [vm((3 * feat, width // 4), bf16)]
+        + [vm((3, 2, block, width // 4), bf16)]
         + [vm((4 * share, width), bf16)] * 4
         + [vm((3 * share, width), bf16)] * 2
         + [
@@ -1056,6 +1162,7 @@
             vm((hid, group_rows), bf16),
             vm((share, width), f32),
             vm((share, width), bf16),
+            vm((share, width), bf16),
             vm((8, share), f32),
             vm((8, 8, share), f32),
             vm((4, width), f32),
@@ -1071,7 +1178,7 @@
     vmem_spec = pl.BlockSpec(memory_space=pltpu.VMEM)
     return pl.pallas_call(
         back_kernel,
-        in_specs=[any_spec] * 14 + [vmem_spec] * 7,
+        in_specs=[any_spec] * 14 + [vmem_spec] * 6,
         out_specs=[any_spec] * len(outs),
         out_shape=outs,
         scratch_shapes=scratch,
@@ -1210,34 +1317,32 @@
     def my_half(values):
         return lax.dynamic_slice_in_dim(values, t * share, share, 0)
 
-    inputs = tokens_in.astype(f32)
-    scale_one = rms_scale(inputs)
-    normed_mine = (inputs * scale_one * norm_gain).astype(bf16)
-    inputs_half = my_half(inputs)
-    scale_one_half = my_half(scale_one)
-    mix_shards = jnp.concatenate(
-        [my_columns(w) for w in (input_proj, forget_proj, outgate_proj)], axis=-1
-    )
     hid = glu_gate.shape[1] // n_tp
-    gate_shards = glu_gate.T.reshape(n_tp, hid, block)
-    up_shards = glu_up.T.reshape(n_tp, hid, block)
-    down_shards = glu_down.reshape(n_tp, hid, block)
-    my_table = pick(my_columns(bound_table), q, 0)
-    par = jnp.stack([bound_parts(my_table)[2], pick(my_columns(mixer_gain), q, 0)])
-    valid_own, keep_own = layout(lengths, bucket, rows)
-    grad_out_rows = (cotangent.astype(f32) * my_half(valid_own)).astype(bf16)
     if n_dp == 16 and n_t == 2:
-        aux_own = jnp.concatenate([valid_own.T, keep_own.T, jnp.zeros((6, rows), f32)])
+        gains = jnp.stack([norm_gain, mixer_gain, ffn_gain])
         (
             mix_full, out_full, gate_full, up_full, down_full, normed_one, grad_out_all, normed_two,
-            pre, state, mix_raw, residual, mixed_out, scale_lanes, aux_rows,
+            pre, state, mix_raw, residual, mixed_out, scale_lanes, aux_rows, par,
         ) = front(
-            mix_shards, output_proj, gate_shards, up_shards, down_shards, normed_mine, grad_out_rows,
-            aux_own, par, inputs_half, ffn_gain[None, :],
+            input_proj, forget_proj, outgate_proj, output_proj, glu_gate, glu_up, glu_down, cotangent,
+            tokens_in, gains, bound_table, jnp.concatenate([lengths, bucket]),
         )
-        scale_state = scale_lanes[:, :1]
-        aux = aux_rows[:, :2].transpose(0, 2, 1).reshape(n_tp * rows, 2)
     else:
+        inputs = tokens_in.astype(f32)
+        scale_one = rms_scale(inputs)
+        normed_mine = (inputs * scale_one * norm_gain).astype(bf16)
+        inputs_half = my_half(inputs)
+        scale_one_half = my_half(scale_one)
+        mix_shards = jnp.concatenate(
+            [my_columns(w) for w in (input_proj, forget_proj, outgate_proj)], axis=-1
+        )
+        gate_shards = glu_gate.T.reshape(n_tp, hid, block)
+        up_shards = glu_up.T.reshape(n_tp, hid, block)
+        down_shards = glu_down.reshape(n_tp, hid, block)
+        my_table = pick(my_columns(bound_table), q, 0)
+        par = jnp.stack([bound_parts(my_table)[2], pick(my_columns(mixer_gain), q, 0)])
+        valid_own, keep_own = layout(lengths, bucket, rows)
+        grad_out_rows = (cotangent.astype(f32) * my_half(valid_own)).astype(bf16)
         normed_half = my_half(normed_mine)
         normed_parts = [normed_mine] + [
             t_gather(swap(normed_half, tp_mask[r])).reshape(rows, width) for r in range(1, n_tp)
@@ -1282,11 +1387,10 @@
         block_parts = cross_rows(hidden, down_full).astype(bf16)
         grad_g, grad_u, grad_d, grad_mix_w, grad_out_w, grad_tokens, block_out, vec = back(
             hidden, grad_gate, grad_up, normed_two, grad_out_all, two_parts, block_parts, normed_one,
-            mix_full, out_full, pre, state, mix_raw, aux_rows, par, inputs_half, residual, mixed_out,
-            scale_lanes, grad_out_rows, jnp.stack([norm_gain, ffn_gain]),
+            mix_full, out_full, pre, state, mix_raw, aux_rows, par, tokens_in, residual, mixed_out,
+            scale_lanes, gains,
         )
-        mix_all = t_gather(grad_mix_w).reshape((2, 2, 2, 3, 2, block, block))
-        mix_all = mix_all.transpose((3, 6, 4, 1, 0, 2, 5)).reshape(3, block, width).astype(f32)
+        mix_all = grad_mix_w.reshape(3, width, block)
         mine = lambda k: lax.dynamic_slice_in_dim(vec, k * n_dp + me, 1, 0)
         shares, picked, lower = bound_parts(
             lax.dynamic_slice_in_dim(bound_table, me * block, block, 1)
@@ -1294,9 +1398,9 @@
         return (
             block_out,
             grad_tokens,
-            mix_all[0],
-            mix_all[1],
-            mix_all[2],
+            mix_all[0].T.astype(f32),
+            mix_all[1].T.astype(f32),
+            mix_all[2].T.astype(f32),
             grad_out_w.astype(f32),
             grad_g.reshape(n_tp * hid, block).T.astype(f32),
             grad_u.reshape(n_tp * hid, block).T.astype(f32),

time: 515 us -> 474 us (0.920); the launches traced: 506 us -> 473 us
  local copies, waits for them, and re-layouts: 35.4 us -> 12.9 us
  other arithmetic: 24.2 us -> 11.4 us
    reshape x8 -> x0, local copies, waits for them, and re-layouts: 9.08 us -> none  [the longest x4 5.75 us: my_columns(): values = values.reshape(lead + (2,) * depth + (block,))]
    convert_element_type x7 -> x2, other arithmetic: 6.75 us -> 0.31 us  [the longest x1 0.2 us: body(): mix_all[2].T.astype(f32)]
    squeeze x3 -> x0, local copies, waits for them, and re-layouts: 5.43 us -> none  [the longest x1 1.81 us: body(): mix_all[0]]
  transfers between devices with their start and end apart: 1 -> 0, of which waited for: 0 -> 0; matrix products, arithmetic and copies ran while one was open for 3% -> 0% of each run, Pallas kernels for 0% -> 0%
where the time goes in v5:
time: 474 us; the launch traced here: 473 us
  Pallas kernels  420 us (89%)
  matrix products  27.2 us (6%)
  local copies, waits for them, and re-layouts  12.9 us (3%)
  other arithmetic  11.4 us (2%)
    pallas_call x1, Pallas kernels, back(): pl.pallas_call(back_kernel, in_specs=[any_spec] * 14 + [vmem_spec] * 6, o...  223 us
    pallas_call x1, Pallas kernels, front(): pl.pallas_call(front_kernel, in_specs=[any_spec] * 8 + [vmem_spec] * 3 +...  197 us
    dot_general x3, matrix products, cross_rows(): lax.dot_general(first_op, second_op, (((0,), (0,)), ((), ())), preferred_...  13.6 us
    dot_general x3, matrix products, cross_cols(): lax.dot_general(first_op, second_op, (((1,), (1,)), ((), ())), preferred_...  13.6 us

profile of v5, /device:TPU:0, one launch (start us, length us, event | category | flops | bytes accessed | tf_op | source)
XLA Modules:
  0.0 472.9 jit_solution(5981700603221598073)
XLA Ops:
  0.6 1.4 pad_maximum_fusion.gains
  2.7 1.2 pad_add_fusion.sizes
  3.9 196.9 %front.1 = (bf16[2048,768]{1,0:T(8,128)(2,1)}, bf16[256,2048]{1,0:T(8,128)(2,1)}, bf16[704,2048]{1,0:T(8,128)(2,1)}, bf16[704,2048]{1,0:T(8,128)(2,1)}, bf16[704...) custom-call(bf16[128,2048]{1,0:T(8,128)(2,1)} %s_in.1, ...), custom_call_target="tpu_custom_call" | custom-call | tf_op jit(solution)/shard_map/front/pallas_call | solution.py:655
  200.9 6.2 %fusion.8 = f32[704,1024]{1,0:T(8,128)S(1)} fusion(bf16[704,2048]{1,0:T(8,128)(2,1)} %get-tuple-element.37, bf16[1024,2048]{1,0:T(8,128)(2,1)} %get-tuple-element.38.n2), kind=kOutput, calls=%fused_computation.31 | convolution fusion | flops 2952790016 | bytes 9961472 | tf_op jit(solution)/shard_map/dot_general | solution.py:44
  207.1 3.3 fusion.9
  210.4 4.1 multiply_convert_fusion
  214.6 3.5 fusion.10
  218.1 5.1 %add_convert_fusion.p_two = bf16[1024,2048]{1,0:T(8,128)(2,1)} fusion(f32[1024,2048]{1,0:T(8,128)S(1)} %fusion.10, bf16[704,1024]{1,0:T(8,128)(2,1)S(1)} %get-tuple-element.61.h_u, bf16[704,2048]{1,0:T(8,128)(2,1)S(1)} %copy-done.8), kind=kOutput, calls=%fused_computation | convolution fusion | flops 2956984320 | bytes 16908288 | tf_op jit(solution)/shard_map/dot_general | solution.py:38
  223.2 5.0 %convolution_convert_fusion.p_block = bf16[1024,2048]{1,0:T(8,128)(2,1)} fusion(bf16[704,1024]{1,0:T(8,128)(2,1)S(1)} %get-tuple-element.63.h_d, bf16[704,2048]{1,0:T(8,128)(2,1)S(1)} %copy-done.7), kind=kOutput, calls=%fused_computation.1 | convolution fusion | flops 2954887168 | bytes 8519680 | tf_op jit(solution)/shard_map/dot_general | solution.py:38
  228.3 222.9 %back.1 = (bf16[4,704,128]{2,1,0:T(8,128)(2,1)}, bf16[4,704,128]{2,1,0:T(8,128)(2,1)}, bf16[4,704,128]{2,1,0:T(8,128)(2,1)}, bf16[3,2,2,2,2,128,128]{6,5,4,3,2,1...) custom-call(bf16[704,1024]{1,0:T(8,128)(2,1)} %copy-done.5, ...), custom_call_target="tpu_custom_call" | custom-call | tf_op jit(solution)/shard_map/back/pallas_call | solution.py:1179
  451.1 1.5 fusion.7
  452.7 1.3 copy.28
  454.2 1.3 copy.29
  455.6 1.3 copy.30
  456.9 2.1 convert_element_type.93
  459.1 1.5 copy.31
  460.7 2.6 bitcast_convert_fusion
  463.3 1.5 copy.32
  464.8 1.2 fusion.6
  466.8 0.7 fusion.2
  467.5 0.8 multiply_reduce_fusion
  468.3 1.4 multiply_multiply_fusion
  469.7 1.9 copy.36
  471.5 1.3 copy.37
  (25 shorter events, 1.2 us)
Async XLA Ops:
  200.9 6.2 %copy-start.1 = (bf16[1024,2048]{1,0:T(8,128)(2,1)S(1)}, bf16[1024,2048]{1,0:T(8,128)(2,1)}, u32[]{:S(2)}) copy-start(bf16[1024,2048]{1,0:T(8,128)(2,1)} %get-tuple-element.38.n2) | copy-start | bytes 12582916
  200.9 6.2 %copy-start.8 = (bf16[704,2048]{1,0:T(8,128)(2,1)S(1)}, bf16[704,2048]{1,0:T(8,128)(2,1)}, u32[]{:S(2)}) copy-start(bf16[704,2048]{1,0:T(8,128)(2,1)} %get-tuple-element.39) | copy-start | bytes 8650756
  207.1 3.3 copy-start
  207.1 3.3 copy-start.7
  210.4 4.2 copy-start.9
  214.6 3.5 copy-start.3
  214.6 3.5 copy-start.4
  214.6 8.6 %copy-start.5 = (bf16[704,1024]{1,0:T(8,128)(2,1)}, bf16[704,1024]{1,0:T(8,128)(2,1)S(1)}, u32[]{:S(2)}) copy-start(bf16[704,1024]{1,0:T(8,128)(2,1)S(1)} %get-tuple-element.63.h_d) | copy-start | bytes 4325380
  455.6 3.4 copy-start.6
  463.3 8.3 %copy-start.2 = (f32[256,2048]{1,0:T(8,128)S(1)}, f32[256,2048]{1,0:T(8,128)}, u32[]{:S(2)}) copy-start(f32[256,2048]{1,0:T(8,128)} %get-tuple-element.89) | copy-start | bytes 6291460

commit v6 on v5

--- a/solution.py
+++ b/solution.py
@@ -290,7 +290,7 @@
     o_mix, o_out, o_g, o_u, o_d, o_n1, o_go, o_n2, o_pre, o_state, o_raw, o_res, o_mo, o_sc, o_aux, o_par,
     w_mix, w_out, n1, aux, pre, state, raw, part, core_in, half, peer_in, par, wide_g, wide_u, s_g, s_u, go_own, bound_row,
     sq, sq_core, sq_half, sq_peer, res, mo, sc, n2, decay, add,
-    send, recv, local, core_send, core_recv, sqc_send, sqc_recv, out_send, out_recv,
+    send, recv, local, core_send, core_recv, sqc_send, sqc_recv, out_send, out_recv, x_send, x_recv,
 ):
     me, t, (zf, zn, y, x), q, group, far, side, core = position()
     rows, width = tok.shape
@@ -495,13 +495,40 @@
     bound = par[0:1, :]
     gain = par[1:2, :]
 
+    def to_x(slot, r):
+        from_rows, to_rows = at(r * share, share, share), at(slot * share, share, share)
+        return [
+            pltpu.make_async_remote_copy(
+                src_ref=a.at[from_rows],
+                dst_ref=b.at[to_rows],
+                send_sem=x_send.at[i * 2 + slot],
+                recv_sem=x_recv.at[i * 2 + slot],
+                device_id=group[1],
+                device_id_type=MESH,
+            )
+            for i, (a, b) in enumerate(((half, peer_in), (sq_half, sq_peer)))
+        ]
+
+    def hand_over(r):
+        core_copy(r).wait()
+        sq_copy(r).wait()
+
+        def some(j, carry):
+            to = at(r * share + j * 16, 16, 16)
+            mine_rows = at(r * rows + t * share + j * 16, 16, 16)
+            half[to, :] = (part[mine_rows, :].astype(f32) + core_in[to, :].astype(f32)).astype(bf16)
+            sq_half[to, :] = sq[mine_rows, :] + sq_core[to, :]
+            return carry
+
+        lax.fori_loop(0, share // 16, some, 0)
+
     def piece(i, carry):
-        r = 3 - i
+        r = 3 - 2 * i + 3 * (i // 2)
         here = at(r * rows, rows, rows)
         pre[here, :] = jnp.dot(n1[here, :], w_mix[...], preferred_element_type=f32)
-        columns = aux[r].T
-        valid = columns[:, 0:1]
-        keep = columns[:, 1:2]
+        masks = aux[r].T
+        valid = masks[:, 0:1]
+        keep = masks[:, 1:2]
         forget = bound + (1.0 - bound) * jax.nn.sigmoid(pre[here, feat : 2 * feat])
         input_pre = pre[here, 0:feat]
         add[...] = input_pre * jax.nn.sigmoid(input_pre) * (1.0 - forget) * valid
@@ -514,9 +541,21 @@
         part[here, :] = jnp.dot(raw[here, :], w_out[...], preferred_element_type=f32).astype(bf16)
         core_copy(r).start()
         sq_copy(r).start()
+
+        @pl.when(i > 0)
+        def _():
+            before = 5 - 2 * i + 3 * ((i - 1) // 2)
+            hand_over(before)
+
+            @pl.when(i < 3)
+            def _():
+                for c in to_x(i - 1, before):
+                    c.start()
+
         return carry
 
     lax.fori_loop(0, 4, piece, 0)
+    start_ffn(1)
 
     link.here(w_mix, o_mix, keep=True)
     link.here(w_out, o_out, keep=True)
@@ -538,25 +577,29 @@
         incoming[2].wait_recv()
         cores.append(link.remote(o.at[row(3, t)], o.at[row(3, t)], core))
 
-    out_in, sq_in = [], []
-    for r in (3, 2, 1):
-        core_copy(r).wait()
-        sq_copy(r).wait()
-        to = at(r * share, share, share)
-        half[to, :] = (part[row(r, t), :].astype(f32) + core_in[to, :].astype(f32)).astype(bf16)
-        sq_half[to, :] = sq[row(r, t), :] + sq_core[to, :]
-        out_in.append(link.remote(half.at[to], peer_in.at[to], group[r]))
-        sq_in.append(link.remote(sq_half.at[to], sq_peer.at[to], group[r]))
-    core_copy(0).wait()
-    sq_copy(0).wait()
-    start_ffn(1)
+    hand_over(0)
+    for c in to_x(0, 3):
+        c.wait()
+
+    def pass_on(j, carry):
+        two = at(2 * share + j * 16, 16, 16)
+        half[two, :] = (half[two, :].astype(f32) + peer_in[at(j * 16, 16, 16), :].astype(f32)).astype(bf16)
+        sq_half[two, :] = sq_half[two, :] + sq_peer[at(j * 16, 16, 16), :]
+        return carry
+
+    lax.fori_loop(0, share // 16, pass_on, 0)
+    third = pl.ds(2 * share, share)
+    to_z = [
+        link.remote(half.at[third], peer_in.at[third], group[2]),
+        link.remote(sq_half.at[third], sq_peer.at[third], group[2]),
+    ]
     spread(o_go, go_in, go_core)
     forward_ffn(0)
-    for c in out_in + sq_in:
+    for c in to_x(1, 1):
+        c.wait()
+    for c in to_z:
         c.wait_recv()
-    total_sq = sq[row(0, t), :] + sq_core[0:share, :]
-    for r in (1, 2, 3):
-        total_sq = total_sq + sq_peer[r * share : (r + 1) * share, :]
+    total_sq = sq_half[0:share, :] + sq_peer[share : 2 * share, :] + sq_peer[2 * share : 3 * share, :]
     scale = lax.rsqrt(jnp.sum(total_sq, axis=1, keepdims=True) / width + epsilon)
     sc[...] = jnp.broadcast_to(scale, sc.shape)
     chunk = min(share, 16)
@@ -564,7 +607,7 @@
     def finish(i, carry):
         to = at(i * chunk, chunk, chunk)
         total = part[at(t * share + i * chunk, chunk, chunk), :].astype(f32) + core_in[to, :].astype(f32)
-        for r in (1, 2, 3):
+        for r in (1, 2):
             total = total + peer_in[at(r * share + i * chunk, chunk, chunk), :].astype(f32)
         mixed = total * sc[to, 0:1]
         value = tok[at(t * share + i * chunk, chunk, chunk), :].astype(f32) + mixed
@@ -651,7 +694,7 @@
         pltpu.SemaphoreType.DMA((88,)),
         pltpu.SemaphoreType.DMA((88,)),
         pltpu.SemaphoreType.DMA((32,)),
-    ] + [pltpu.SemaphoreType.DMA((4,))] * 6
+    ] + [pltpu.SemaphoreType.DMA((4,))] * 8
     return pl.pallas_call(
         front_kernel,
         in_specs=[any_spec] * 8 + [vmem_spec] * 3 + [pl.BlockSpec(memory_space=pltpu.SMEM)],
@@ -671,8 +714,8 @@
     o_g, o_u, o_d, o_mix, o_out, o_tok, o_blk, o_vec,
     left, right, gmix, dw_d, dw_g, dw_u, dw_mix, yr_d, yr_g, yr_u, yr_mix, zr_d, zr_g, zr_u, zr_mix,
     own, half, core_in, core_blk, peer_in, peer_blk, w_mix, w_out, aux, pre_b, state_b, raw_b,
-    grads, grads_t, decay, add, hold, yr_out, zr_out, hid_a, hid_b,
-    gres, gm_own, go_own, scalars, scal_all, sums, vec, vec_in,
+    grads, grads_t, decay, add, yr_out, zr_out, hid_a, hid_b,
+    gres, gm_own, scalars, scal_all, sums, vec, vec_in,
     send, recv, local, core_send, core_recv, out_send, out_recv, piece_sem,
 ):
     me, t, (zf, zn, y, x), q, group, far, side, core = position()
@@ -695,37 +738,50 @@
     def rel(r):
         return pl.ds(r * share, share)
 
-    two_core = [link.remote(p_two.at[row(r, 1 - t)], core_in.at[rel(r)], core) for r in (3, 2, 1, 0)]
-    two_own = [link.here(p_two.at[row(r, t)], own.at[rel(r)]) for r in (3, 2, 1, 0)]
+    two_core = [link.remote(p_two.at[row(r, 1 - t)], core_in.at[rel(r)], core) for r in (3, 1, 2, 0)]
+    two_own = [link.here(p_two.at[row(r, t)], own.at[rel(r)]) for r in (3, 1, 2, 0)]
     get_d = [link.here(h_d, hid_a), link.here(go, left)]
     get_g = [link.here(h_g, hid_b), link.here(n2, right)]
-    get_go = link.here(go.at[row(0, t)], go_own)
+    get_go = link.here(go.at[row(0, t)], gm_own)
     get_aux = [link.here(aux_in, aux), link.here(w_out_in, w_out), link.here(w_mix_in, w_mix)]
-
-    def over_cores(arrived, mine, source, peers):
-        sent = []
-        for i, r in enumerate((3, 2, 1)):
-            for c in mine[i]:
-                c.wait()
-            arrived[i].wait_recv()
-
-            def add_rows(j, carry):
-                to = at(r * share + j * 16, 16, 16)
-                half[to, :] = (source(r, j) + core_in_now[to, :].astype(f32)).astype(bf16)
-                return carry
-
-            lax.fori_loop(0, share // 16, add_rows, 0)
-            sent.append(link.remote(half.at[rel(r)], peers.at[rel(r - 1)], group[r]))
-        for c in mine[3]:
-            c.wait()
-        arrived[3].wait_recv()
-        return sent
 
     def own_rows(r, j):
         return own[at(r * share + j * 16, 16, 16), :].astype(f32)
 
-    core_in_now = core_in
-    two_peer = over_cores(two_core, [[c] for c in two_own], own_rows, peer_in)
+    def add_half(r, source, incoming):
+        def some(j, carry):
+            to = at(r * share + j * 16, 16, 16)
+            half[to, :] = (source(r, j) + incoming[to, :].astype(f32)).astype(bf16)
+            return carry
+
+        lax.fori_loop(0, share // 16, some, 0)
+
+    def over_cores(arrived, mine, source, incoming, peers):
+        sent = []
+        for r in (3, 1, 2, 0):
+            mine[r].wait()
+            arrived[r].wait_recv()
+            if r:
+                add_half(r, source, incoming)
+            if r % 2:
+                sent.append(link.remote(half.at[rel(r)], peers.at[rel(len(sent))], group[1]))
+        return sent
+
+    def pass_on(sent, peers):
+        sent[0].wait_recv()
+
+        def some(j, carry):
+            two = at(2 * share + j * 16, 16, 16)
+            half[two, :] = (half[two, :].astype(f32) + peers[at(j * 16, 16, 16), :].astype(f32)).astype(bf16)
+            return carry
+
+        lax.fori_loop(0, share // 16, some, 0)
+        sent.append(link.remote(half.at[rel(2)], peers.at[rel(2)], group[2]))
+
+    def by_piece(copies):
+        return dict(zip((3, 1, 2, 0), copies))
+
+    two_peer = over_cores(by_piece(two_core), by_piece(two_own), own_rows, core_in, peer_in)
 
     def weight_grad(hid, other, dw, first, count):
         wide = 4 * block
@@ -815,12 +871,13 @@
     weight_grad(hid_b, right, dw_g, 0, 2)
     hop_g = side_send(dw_g, yr_g, 0)
     weight_grad(hid_b, right, dw_g, 2, 2)
+    pass_on(two_peer, peer_in)
     get_u.wait()
     weight_grad(hid_a, right, dw_u, 0, 4)
     far_d = second_hop(hop_d, dw_d, yr_d, zr_d)
     hop_u = side_send(dw_u, yr_u, 0)
 
-    for c in two_peer:
+    for c in two_peer[1:]:
         c.wait_recv()
     get_go.wait()
     gain_two = gains[2:3, :]
@@ -830,13 +887,13 @@
     def residual_rows(j, carry):
         to = at(j * step, step, step)
         total = own[to, :].astype(f32) + core_in[to, :].astype(f32)
-        for r in (0, 1, 2):
+        for r in (1, 2):
             total = total + peer_in[at(r * share + j * step, step, step), :].astype(f32)
         value = res[to, :]
         s = lax.rsqrt(jnp.mean(value * value, axis=1, keepdims=True) + epsilon)
         weighted = total * gain_two
         grad = (
-            go_own[to, :].astype(f32)
+            gm_own[to, :].astype(f32)
             + s * weighted
             - value * (s * s * s) * jnp.mean(weighted * value, axis=1, keepdims=True)
         )
@@ -859,7 +916,7 @@
     sc_in = [link.remote(scalars, scal(r, t), group[r]) for r in (1, 2, 3)]
     gm_core = [link.remote(gm_own, gmix.at[row(0, t)], core), link.remote(scalars, scal(0, t), core)]
     gm_here = [link.here(gm_own, gmix.at[row(0, t)]), link.here(scalars, scal(0, t))]
-    blk_core = [link.remote(p_block.at[row(r, 1 - t)], core_blk.at[rel(r)], core) for r in (3, 2, 1, 0)]
+    blk_core = [link.remote(p_block.at[row(r, 1 - t)], core_blk.at[rel(r)], core) for r in (3, 1, 2, 0)]
 
     far_g = second_hop(hop_g, dw_g, yr_g, zr_g)
     near_d = side_send(dw_d, yr_d, 1)
@@ -878,7 +935,7 @@
     near_u = side_send(dw_u, yr_u, 1)
 
     link.sent(two_peer)
-    blk_own = [link.here(p_block.at[row(r, t)], own.at[rel(r)]) for r in (3, 2, 1, 0)]
+    blk_own = [link.here(p_block.at[row(r, t)], own.at[rel(r)]) for r in (3, 1, 2, 0)]
     for c in get_aux + [get_n1] + gm_here:
         c.wait()
     for c in gm_core:
@@ -908,8 +965,25 @@
     mixed_t = hid_b.at[0:feat]
     dw_out = w_out
 
+    def one_rows(r, j):
+        return right[at(r * rows + t * share + j * 16, 16, 16), :].astype(f32)
+
+    def one_x(slot, r):
+        return pltpu.make_async_remote_copy(
+            src_ref=half.at[at(r * share, share, share)],
+            dst_ref=peer_in.at[at(slot * share, share, share)],
+            send_sem=core_send.at[4 + slot],
+            recv_sem=core_recv.at[4 + slot],
+            device_id=group[1],
+            device_id_type=MESH,
+        )
+
+    def hand_over(r):
+        one_core(r).wait()
+        add_half(r, one_rows, core_in)
+
     def piece(i, carry):
-        r = 3 - i
+        r = 3 - 2 * i + 3 * (i // 2)
         here = at(r * rows, rows, rows)
         copies = fetch(r)
         for c in copies:
@@ -938,8 +1012,8 @@
         sig_forget = jax.nn.sigmoid(pre_b[:, feat : 2 * feat])
         forget = bound + (1.0 - bound) * sig_forget
         decay[...] = jnp.where(at_row < rows - 1, pltpu.roll(forget * keep, rows - 1, 0), 0.0)
-        scan_rows(decay, add, hold, True)
-        grad_state = hold[...]
+        scan_rows(decay, add, add, True)
+        grad_state = add[...]
         before = jnp.where(at_row > 0, pltpu.roll(held, 1, 0), 0.0)
         sig_in = jax.nn.sigmoid(input_pre)
         grad_forget = grad_state * (before * keep - input_pre * sig_in * valid)
@@ -955,23 +1029,21 @@
         one_core(r).start()
         grads_t[:, here] = grads[...].T.astype(bf16)
         mixed_t[:, here] = (raw_b[...].astype(f32) * scale).T.astype(bf16)
+
+        @pl.when(i > 0)
+        def _():
+            before_r = 5 - 2 * i + 3 * ((i - 1) // 2)
+            hand_over(before_r)
+
+            @pl.when(i < 3)
+            def _():
+                one_x(i - 1, before_r).start()
+
         return carry
 
     lax.fori_loop(0, 4, piece, 0)
 
-    core_in_now = core_in
-
-    class Arrival:
-        def __init__(self, copy):
-            self.wait_recv = copy.wait_recv
-
-    def one_rows(r, j):
-        return right[at(r * rows + t * share + j * 16, 16, 16), :].astype(f32)
-
-    one_arrived = [Arrival(one_core(r)) for r in (3, 2, 1, 0)]
-    one_peer = over_cores(one_arrived, [[], [], [], []], one_rows, peer_in)
-    for r in (3, 2, 1, 0):
-        one_core(r).wait_send()
+    one_core(0).wait()
 
     weight_grad(grads_t, left, dw_mix, 0, 2)
     hop_mix = side_send(dw_mix, yr_mix, 0)
@@ -1005,6 +1077,15 @@
     def _():
         out_side.start()
 
+    one_x(0, 3).wait()
+
+    def one_on(j, carry):
+        two = at(2 * share + j * 16, 16, 16)
+        half[two, :] = (half[two, :].astype(f32) + peer_in[at(j * 16, 16, 16), :].astype(f32)).astype(bf16)
+        return carry
+
+    lax.fori_loop(0, share // 16, one_on, 0)
+    one_z = link.remote(half.at[rel(2)], peer_in.at[rel(2)], group[2])
     near_mix = side_send(dw_mix, yr_mix, 1)
     back_d = last_hop(near_d, far_d, dw_d, yr_d, zr_d, o_d)
     back_g = last_hop(near_g, far_g, dw_g, yr_g, zr_g, o_g)
@@ -1016,14 +1097,14 @@
         add_columns(dw_out, pl.ds(0, width), [(yr_out, pl.ds(0, width))])
         out_far.start()
 
-    for c in one_peer:
-        c.wait_recv()
+    one_x(1, 1).wait()
+    one_z.wait_recv()
     gain_one = gains[0:1, :]
 
     def token_rows(j, carry):
         to = at(j * step, step, step)
         total = one_rows(0, j) + core_in[to, :].astype(f32)
-        for r in (0, 1, 2):
+        for r in (1, 2):
             total = total + peer_in[at(r * share + j * step, step, step), :].astype(f32)
         value = tok[at(t * share + j * step, step, step), :].astype(f32)
         s = lax.rsqrt(jnp.mean(value * value, axis=1, keepdims=True) + epsilon)
@@ -1060,20 +1141,20 @@
         if k < len(partners):
             turn.append(link.remote(vec.at[k], vec_in.at[k], partners[k]))
 
-    link.sent(one_peer)
-    core_in_now = core_blk
-    blk_peer = over_cores(blk_core, [[c] for c in blk_own], own_rows, peer_blk)
+    link.sent([one_z])
+    blk_peer = over_cores(by_piece(blk_core), by_piece(blk_own), own_rows, core_blk, peer_blk)
     next_turn()
     back_u = last_hop(near_u, far_u, dw_u, yr_u, zr_u, o_u)
+    pass_on(blk_peer, peer_blk)
     next_turn()
     next_turn()
-    for c in blk_peer:
+    for c in blk_peer[1:]:
         c.wait_recv()
 
     def block_rows(j, carry):
         to = at(j * step, step, step)
         total = own_rows(0, j) + core_blk[to, :].astype(f32)
-        for r in (0, 1, 2):
+        for r in (1, 2):
             total = total + peer_blk[at(r * share + j * step, step, step), :].astype(f32)
         gm_own[to, :] = (res[to, :] + total).astype(bf16)
         return carry
@@ -1155,13 +1236,11 @@
             vm((3 * feat, group_rows), bf16),
             vm((rows, feat), f32),
             vm((rows, feat), f32),
-            vm((rows, feat), f32),
             vm((feat, width), bf16),
             vm((block, width), bf16),
             vm((hid, group_rows), bf16),
             vm((hid, group_rows), bf16),
             vm((share, width), f32),
-            vm((share, width), bf16),
             vm((share, width), bf16),
             vm((8, share), f32),
             vm((8, 8, share), f32),
@@ -1172,7 +1251,7 @@
             pltpu.SemaphoreType.DMA((96,)),
             pltpu.SemaphoreType.DMA((32,)),
         ]
-        + [pltpu.SemaphoreType.DMA((4,))] * 5
+        + [pltpu.SemaphoreType.DMA((6,))] * 5
     )
     any_spec = pl.BlockSpec(memory_space=pl.ANY)
     vmem_spec = pl.BlockSpec(memory_space=pltpu.VMEM)
@@ -1183,7 +1262,7 @@
         out_shape=outs,
         scratch_shapes=scratch,
         compiler_params=pltpu.CompilerParams(
-            collective_id=2, has_side_effects=True, vmem_limit_bytes=62 << 20
+            collective_id=2, has_side_effects=True, vmem_limit_bytes=63 << 20
         ),
         name="back",
     )(*arrays)

time: 474 us -> 450 us (0.949)
  Pallas kernels: 420 us -> 393 us
    pallas_call x1, Pallas kernels: 197 us -> 182 us  [front(): pl.pallas_call(front_kernel, in_specs=[any_spec] * 8 + [vmem_spec] * 3 +...]
    pallas_call x1, Pallas kernels: 223 us -> 212 us  [back(): pl.pallas_call(back_kernel, in_specs=[any_spec] * 14 + [vmem_spec] * 6, o...]
where the time goes in v6:
time: 450 us; the launch traced here: 446 us
  Pallas kernels  393 us (87%)
  matrix products  27.2 us (6%)
  local copies, waits for them, and re-layouts  12.9 us (3%)
  other arithmetic  11.4 us (3%)
    pallas_call x1, Pallas kernels, back(): pl.pallas_call(back_kernel, in_specs=[any_spec] * 14 + [vmem_spec] * 6, o...  212 us
    pallas_call x1, Pallas kernels, front(): pl.pallas_call(front_kernel, in_specs=[any_spec] * 8 + [vmem_spec] * 3 +...  182 us
    dot_general x3, matrix products, cross_rows(): lax.dot_general(first_op, second_op, (((0,), (0,)), ((), ())), preferred_...  13.6 us
    dot_general x3, matrix products, cross_cols(): lax.dot_general(first_op, second_op, (((1,), (1,)), ((), ())), preferred_...  13.6 us

profile of v6, /device:TPU:0, one launch (start us, length us, event | category | flops | bytes accessed | tf_op | source)
XLA Modules:
  0.0 446.1 jit_solution(11612308590424108134)
XLA Ops:
  0.6 1.4 pad_maximum_fusion.gains
  2.7 1.2 pad_add_fusion.sizes
  3.9 181.5 %front.1 = (bf16[2048,768]{1,0:T(8,128)(2,1)}, bf16[256,2048]{1,0:T(8,128)(2,1)}, bf16[704,2048]{1,0:T(8,128)(2,1)}, bf16[704,2048]{1,0:T(8,128)(2,1)}, bf16[704...) custom-call(bf16[128,2048]{1,0:T(8,128)(2,1)} %s_in.1, ...), custom_call_target="tpu_custom_call" | custom-call | tf_op jit(solution)/shard_map/front/pallas_call | solution.py:698
  185.5 6.2 %fusion.8 = f32[704,1024]{1,0:T(8,128)S(1)} fusion(bf16[704,2048]{1,0:T(8,128)(2,1)} %get-tuple-element.37, bf16[1024,2048]{1,0:T(8,128)(2,1)} %get-tuple-element.38.n2), kind=kOutput, calls=%fused_computation.31 | convolution fusion | flops 2952790016 | bytes 9961472 | tf_op jit(solution)/shard_map/dot_general | solution.py:44
  191.7 3.3 fusion.9
  195.0 4.1 multiply_convert_fusion
  199.2 3.5 fusion.10
  202.7 5.1 %add_convert_fusion.p_two = bf16[1024,2048]{1,0:T(8,128)(2,1)} fusion(f32[1024,2048]{1,0:T(8,128)S(1)} %fusion.10, bf16[704,1024]{1,0:T(8,128)(2,1)S(1)} %get-tuple-element.61.h_u, bf16[704,2048]{1,0:T(8,128)(2,1)S(1)} %copy-done.8), kind=kOutput, calls=%fused_computation | convolution fusion | flops 2956984320 | bytes 16908288 | tf_op jit(solution)/shard_map/dot_general | solution.py:38
  207.8 5.0 %convolution_convert_fusion.p_block = bf16[1024,2048]{1,0:T(8,128)(2,1)} fusion(bf16[704,1024]{1,0:T(8,128)(2,1)S(1)} %get-tuple-element.63.h_d, bf16[704,2048]{1,0:T(8,128)(2,1)S(1)} %copy-done.7), kind=kOutput, calls=%fused_computation.1 | convolution fusion | flops 2954887168 | bytes 8519680 | tf_op jit(solution)/shard_map/dot_general | solution.py:38
  212.8 211.5 %back.1 = (bf16[4,704,128]{2,1,0:T(8,128)(2,1)}, bf16[4,704,128]{2,1,0:T(8,128)(2,1)}, bf16[4,704,128]{2,1,0:T(8,128)(2,1)}, bf16[3,2,2,2,2,128,128]{6,5,4,3,2,1...) custom-call(bf16[704,1024]{1,0:T(8,128)(2,1)} %copy-done.5, ...), custom_call_target="tpu_custom_call" | custom-call | tf_op jit(solution)/shard_map/back/pallas_call | solution.py:1258
  424.4 1.5 fusion.7
  426.0 1.3 copy.28
  427.5 1.3 copy.29
  428.8 1.3 copy.30
  430.1 2.1 convert_element_type.93
  432.4 1.5 copy.31
  433.9 2.6 bitcast_convert_fusion
  436.5 1.5 copy.32
  438.0 1.2 fusion.6
  440.0 0.7 fusion.2
  440.7 0.8 multiply_reduce_fusion
  441.5 1.4 multiply_multiply_fusion
  442.9 1.9 copy.36
  444.8 1.3 copy.37
  (25 shorter events, 1.2 us)
Async XLA Ops:
  185.4 6.2 %copy-start.1 = (bf16[1024,2048]{1,0:T(8,128)(2,1)S(1)}, bf16[1024,2048]{1,0:T(8,128)(2,1)}, u32[]{:S(2)}) copy-start(bf16[1024,2048]{1,0:T(8,128)(2,1)} %get-tuple-element.38.n2) | copy-start | bytes 12582916
  185.5 6.2 %copy-start.8 = (bf16[704,2048]{1,0:T(8,128)(2,1)S(1)}, bf16[704,2048]{1,0:T(8,128)(2,1)}, u32[]{:S(2)}) copy-start(bf16[704,2048]{1,0:T(8,128)(2,1)} %get-tuple-element.39) | copy-start | bytes 8650756
  191.7 3.3 copy-start
  191.7 3.3 copy-start.7
  195.0 4.2 copy-start.9
  199.1 3.5 copy-start.3
  199.2 3.5 copy-start.4
  199.2 8.6 %copy-start.5 = (bf16[704,1024]{1,0:T(8,128)(2,1)}, bf16[704,1024]{1,0:T(8,128)(2,1)S(1)}, u32[]{:S(2)}) copy-start(bf16[704,1024]{1,0:T(8,128)(2,1)S(1)} %get-tuple-element.63.h_d) | copy-start | bytes 4325380
  428.8 3.4 copy-start.6
  436.5 8.3 %copy-start.2 = (f32[256,2048]{1,0:T(8,128)S(1)}, f32[256,2048]{1,0:T(8,128)}, u32[]{:S(2)}) copy-start(f32[256,2048]{1,0:T(8,128)} %get-tuple-element.89) | copy-start | bytes 6291460

commit v7 on v6

--- a/solution.py
+++ b/solution.py
@@ -287,8 +287,8 @@
 
 def front_kernel(
     s_in, s_fg, s_og, s_out, w_g, w_u, s_d, cot, tok, gains, table, sizes,
-    o_mix, o_out, o_g, o_u, o_d, o_n1, o_go, o_n2, o_pre, o_state, o_raw, o_res, o_mo, o_sc, o_aux, o_par,
-    w_mix, w_out, n1, aux, pre, state, raw, part, core_in, half, peer_in, par, wide_g, wide_u, s_g, s_u, go_own, bound_row,
+    o_mix, o_out, o_g, o_u, o_d, o_n1, o_go, o_n2, o_pre, o_state, o_raw, o_res, o_mo, o_sc, o_aux, o_par, o_gate, o_up, o_coef,
+    w_mix, w_out, n1, aux, pre, state, raw, part, core_in, half, peer_in, par, wide_g, wide_u, s_g, s_u, go_own, bound_row, full_g, full_u, gate, up, all_powers, coef,
     sq, sq_core, sq_half, sq_peer, res, mo, sc, n2, decay, add,
     send, recv, local, core_send, core_recv, sqc_send, sqc_recv, out_send, out_recv, x_send, x_recv,
 ):
@@ -420,6 +420,13 @@
     layer_ids = lax.broadcasted_iota(jnp.int32, logits.shape, 0)
     picked = jnp.where((layer_ids >= 1) & (layer_ids <= LAYER), powers, 0.0)
     bound_row[0:1, :] = jnp.sum(picked, axis=0, keepdims=True) / jnp.sum(powers, axis=0, keepdims=True)
+    all_powers[...] = powers
+    mine_powers = all_powers[:, mine]
+    mine_shares = mine_powers / jnp.sum(mine_powers, axis=0, keepdims=True)
+    ids = lax.broadcasted_iota(jnp.int32, mine_shares.shape, 0)
+    mine_picked = ((ids >= 1) & (ids <= LAYER)).astype(f32)
+    coef[...] = mine_shares * (mine_picked - jnp.sum(mine_shares * mine_picked, axis=0, keepdims=True))
+    link.here(coef, o_coef, keep=True)
     for fz in (0, 1):
         par[0:1, fz * block : (fz + 1) * block] = bound_row[0:1, columns(0, fz)]
         par[1:2, fz * block : (fz + 1) * block] = gains[1:2, columns(0, fz)]
@@ -448,7 +455,7 @@
         out_side.wait_recv()
         out_next.wait_recv()
 
-    far_ffn, side_ffn = [], []
+    far_ffn, side_ffn = [], ([], [], [])
 
     def start_ffn(i):
         o = shards[i][1]
@@ -456,13 +463,13 @@
         for c in ffn_in[3 * i : 3 * i + 3]:
             c.wait_recv()
         far_ffn.append([link.remote(o.at[:, pair(zf, c, y)], o.at[:, pair(zf, c, y)], far) for c in (0, 1)])
-        side_ffn.extend(link.remote(o.at[:, pair(zf, c, y)], o.at[:, pair(zf, c, y)], side) for c in (0, 1))
+        side_ffn[i].extend(link.remote(o.at[:, pair(zf, c, y)], o.at[:, pair(zf, c, y)], side) for c in (0, 1))
 
     def forward_ffn(i):
         o = shards[i][1]
         for c in (0, 1):
             far_ffn[i][c].wait_recv()
-            side_ffn.append(link.remote(o.at[:, pair(1 - zf, c, y)], o.at[:, pair(1 - zf, c, y)], side))
+            side_ffn[i].append(link.remote(o.at[:, pair(1 - zf, c, y)], o.at[:, pair(1 - zf, c, y)], side))
 
     start_ffn(0)
     go_in = [link.remote(go_own, o_go.at[row(r, t)], group[r]) for r in (1, 2)]
@@ -620,7 +627,7 @@
     lax.fori_loop(0, share // chunk, finish, 0)
     n2_in = [link.remote(n2, o_n2.at[row(r, t)], group[r]) for r in (1, 2)]
     n2_core = [link.remote(n2, o_n2.at[row(0, t)], core)]
-    link.here(n2, o_n2.at[row(0, t)], keep=True)
+    n2_here = link.here(n2, o_n2.at[row(0, t)])
     link.here(res, o_res, keep=True)
     link.here(mo, o_mo, keep=True)
     link.here(sc, o_sc, keep=True)
@@ -629,8 +636,38 @@
     forward_ffn(1)
     spread(o_n2, n2_in, n2_core)
     spread_last(o_n2, n2_in, n2_core)
+
     forward_ffn(2)
-    for c in side_ffn + go_core + n2_core:
+
+    for c in side_ffn[0]:
+        c.wait_recv()
+    get_full = link.here(o_g, full_g)
+    for c in n2_core:
+        c.wait_recv()
+    n2_here.wait()
+    get_rows = link.here(o_n2, part)
+    get_full.wait()
+    get_rows.wait()
+
+    def product(full, made):
+        def some(j, carry):
+            to = at(j * rows, rows, rows)
+            made[:, to] = lax.dot_general(
+                full[...], part[to, :], (((1,), (1,)), ((), ())), preferred_element_type=f32
+            )
+            return carry
+
+        lax.fori_loop(0, 4, some, 0)
+
+    product(full_g, gate)
+    link.here(gate, o_gate, keep=True)
+    for c in side_ffn[1]:
+        c.wait_recv()
+    get_full = link.here(o_u, full_u)
+    get_full.wait()
+    product(full_u, up)
+    link.here(up, o_up, keep=True)
+    for c in side_ffn[2] + go_core:
         c.wait_recv()
     link.close()
 
@@ -661,6 +698,9 @@
         made((share, 128), f32),
         made((4, 8, rows), f32),
         made((2, feat), f32),
+        made((hid, group_rows), f32),
+        made((hid, group_rows), f32),
+        made((table.shape[0], block), f32),
     ]
     scratch = [
         pltpu.VMEM((width, 3 * feat), bf16),
@@ -681,6 +721,12 @@
         pltpu.VMEM((4 * hid, block), bf16),
         pltpu.VMEM((share, width), bf16),
         pltpu.VMEM((8, width), f32),
+        pltpu.VMEM((hid, width), bf16),
+        pltpu.VMEM((hid, width), bf16),
+        pltpu.VMEM((hid, group_rows), f32),
+        pltpu.VMEM((hid, group_rows), f32),
+        pltpu.VMEM(table.shape, f32),
+        pltpu.VMEM((table.shape[0], block), f32),
         pltpu.VMEM((group_rows, lanes), f32),
         pltpu.VMEM((4 * share, lanes), f32),
         pltpu.VMEM((4 * share, lanes), f32),
@@ -709,7 +755,7 @@
 
 
 def back_kernel(
-    h_d, h_g, h_u, n2, go, p_two, p_block, n1, w_mix_in, w_out_in, pre, state, raw, aux_in,
+    h_d, h_g, h_u, n2, go, w_g, w_u, w_d, n1, w_mix_in, w_out_in, pre, state, raw, aux_in,
     par, tok, res, mo, sc, gains,
     o_g, o_u, o_d, o_mix, o_out, o_tok, o_blk, o_vec,
     left, right, gmix, dw_d, dw_g, dw_u, dw_mix, yr_d, yr_g, yr_u, yr_mix, zr_d, zr_g, zr_u, zr_mix,
@@ -738,50 +784,100 @@
     def rel(r):
         return pl.ds(r * share, share)
 
-    two_core = [link.remote(p_two.at[row(r, 1 - t)], core_in.at[rel(r)], core) for r in (3, 1, 2, 0)]
-    two_own = [link.here(p_two.at[row(r, t)], own.at[rel(r)]) for r in (3, 1, 2, 0)]
-    get_d = [link.here(h_d, hid_a), link.here(go, left)]
-    get_g = [link.here(h_g, hid_b), link.here(n2, right)]
-    get_go = link.here(go.at[row(0, t)], gm_own)
-    get_aux = [link.here(aux_in, aux), link.here(w_out_in, w_out), link.here(w_mix_in, w_mix)]
+    hid_rows = pl.ds(0, w_g.shape[0])
+    full_g, full_u = left.at[hid_rows], gmix.at[hid_rows]
+    get_g = [link.here(h_g, hid_a), link.here(n2, right)]
+    get_u = link.here(h_u, hid_b)
+    get_two = [link.here(w_g, full_g), link.here(w_u, full_u)]
+    get_go = [link.here(go.at[row(0, t)], gm_own)]
+    get_w_d = link.here(w_d, dw_d)
+    get_aux = [link.here(aux_in, aux), link.here(w_mix_in, w_mix)]
+    order = (3, 1, 2, 0)
+
+    def stage(r):
+        i = order.index(r)
+        return w_out if i == 3 else dw_mix.at[i]
+
+    def staged(r, tt):
+        return w_out.at[at(tt * share, share, share)] if r == 0 else stage(r).at[tt]
+
+    def products(terms):
+        wide = 4 * block
+
+        def at_piece(r, store):
+            here = at(r * rows, rows, rows)
+
+            def some(j, carry):
+                to = at(j * wide, wide, wide)
+                total = None
+                for hid, weight in terms:
+                    one = lax.dot_general(
+                        hid[:, here], weight[:, to], (((0,), (0,)), ((), ())), preferred_element_type=f32
+                    )
+                    total = one if total is None else total + one
+                store(to, total.astype(bf16))
+                return carry
+
+            lax.fori_loop(0, width // wide, some, 0)
+
+        return at_piece
+
+    def all_pieces(terms, incoming):
+        at_piece = products(terms)
+        copies = {}
+        for i, r in enumerate(order):
+            if r:
+
+                def store(to, value):
+                    dw_mix[i, 0, :, to] = value[:share]
+                    dw_mix[i, 1, :, to] = value[share:]
+
+            else:
+
+                def store(to, value):
+                    w_out[:, to] = value
+
+            at_piece(r, store)
+            copies[r] = link.remote(staged(r, 1 - t), incoming.at[rel(r)], core)
+        return copies
+
+    def two_rows(r, j):
+        if r == 0:
+            return w_out[at(t * share + j * 16, 16, 16), :].astype(f32)
+        return dw_mix[order.index(r), t, at(j * 16, 16, 16), :].astype(f32)
 
     def own_rows(r, j):
         return own[at(r * share + j * 16, 16, 16), :].astype(f32)
 
-    def add_half(r, source, incoming):
+    def add_half(r, source, incoming, held):
         def some(j, carry):
             to = at(r * share + j * 16, 16, 16)
-            half[to, :] = (source(r, j) + incoming[to, :].astype(f32)).astype(bf16)
+            held[to, :] = (source(r, j) + incoming[to, :].astype(f32)).astype(bf16)
             return carry
 
         lax.fori_loop(0, share // 16, some, 0)
 
-    def over_cores(arrived, mine, source, incoming, peers):
+    def over_cores(arrived, source, incoming, held, peers):
         sent = []
         for r in (3, 1, 2, 0):
-            mine[r].wait()
             arrived[r].wait_recv()
             if r:
-                add_half(r, source, incoming)
+                add_half(r, source, incoming, held)
             if r % 2:
-                sent.append(link.remote(half.at[rel(r)], peers.at[rel(len(sent))], group[1]))
+                sent.append(link.remote(held.at[rel(r)], peers.at[rel(len(sent))], group[1]))
         return sent
 
-    def pass_on(sent, peers):
+    def pass_on(sent, held, peers):
         sent[0].wait_recv()
 
         def some(j, carry):
             two = at(2 * share + j * 16, 16, 16)
-            half[two, :] = (half[two, :].astype(f32) + peers[at(j * 16, 16, 16), :].astype(f32)).astype(bf16)
+            held[two, :] = (held[two, :].astype(f32) + peers[at(j * 16, 16, 16), :].astype(f32)).astype(bf16)
             return carry
 
         lax.fori_loop(0, share // 16, some, 0)
-        sent.append(link.remote(half.at[rel(2)], peers.at[rel(2)], group[2]))
-
-    def by_piece(copies):
-        return dict(zip((3, 1, 2, 0), copies))
-
-    two_peer = over_cores(by_piece(two_core), by_piece(two_own), own_rows, core_in, peer_in)
+        sent.append(link.remote(held.at[rel(2)], peers.at[rel(2)], group[2]))
+
 
     def weight_grad(hid, other, dw, first, count):
         wide = 4 * block
@@ -859,34 +955,36 @@
         kept.wait()
         return sent
 
-    for c in get_d:
-        c.wait()
-    weight_grad(hid_a, left, dw_d, 0, 2)
-    hop_d = side_send(dw_d, yr_d, 0)
-    weight_grad(hid_a, left, dw_d, 2, 2)
-    get_u = link.here(h_u, hid_a)
-    get_n1 = link.here(n1, left)
     for c in get_g:
         c.wait()
-    weight_grad(hid_b, right, dw_g, 0, 2)
+    weight_grad(hid_a, right, dw_g, 0, 2)
     hop_g = side_send(dw_g, yr_g, 0)
-    weight_grad(hid_b, right, dw_g, 2, 2)
-    pass_on(two_peer, peer_in)
     get_u.wait()
-    weight_grad(hid_a, right, dw_u, 0, 4)
-    far_d = second_hop(hop_d, dw_d, yr_d, zr_d)
+    for c in get_two:
+        c.wait()
+    two_core = all_pieces([(hid_a, full_g), (hid_b, full_u)], core_in)
+
+    two_peer = over_cores(two_core, two_rows, core_in, half, peer_in)
+    weight_grad(hid_b, right, dw_u, 0, 2)
+    get_left = link.here(go, left)
+    weight_grad(hid_a, right, dw_g, 2, 2)
+    get_d = link.here(h_d, hid_a)
+    far_g = second_hop(hop_g, dw_g, yr_g, zr_g)
     hop_u = side_send(dw_u, yr_u, 0)
+    pass_on(two_peer, half, peer_in)
+    weight_grad(hid_b, right, dw_u, 2, 2)
 
     for c in two_peer[1:]:
         c.wait_recv()
-    get_go.wait()
+    for c in get_go:
+        c.wait()
     gain_two = gains[2:3, :]
     sums[...] = jnp.zeros_like(sums)
     step = 16
 
     def residual_rows(j, carry):
         to = at(j * step, step, step)
-        total = own[to, :].astype(f32) + core_in[to, :].astype(f32)
+        total = two_rows(0, j) + core_in[to, :].astype(f32)
         for r in (1, 2):
             total = total + peer_in[at(r * share + j * step, step, step), :].astype(f32)
         value = res[to, :]
@@ -916,10 +1014,15 @@
     sc_in = [link.remote(scalars, scal(r, t), group[r]) for r in (1, 2, 3)]
     gm_core = [link.remote(gm_own, gmix.at[row(0, t)], core), link.remote(scalars, scal(0, t), core)]
     gm_here = [link.here(gm_own, gmix.at[row(0, t)]), link.here(scalars, scal(0, t))]
-    blk_core = [link.remote(p_block.at[row(r, 1 - t)], core_blk.at[rel(r)], core) for r in (3, 1, 2, 0)]
-
-    far_g = second_hop(hop_g, dw_g, yr_g, zr_g)
-    near_d = side_send(dw_d, yr_d, 1)
+    for c in (get_d, get_w_d, get_left):
+        c.wait()
+    link.sent(two_core.values())
+    blk_core = all_pieces([(hid_a, dw_d)], core_blk)
+    blk_own = [link.here(staged(r, t), own.at[rel(r)]) for r in order]
+    weight_grad(hid_a, left, dw_d, 0, 2)
+    hop_d = side_send(dw_d, yr_d, 0)
+    far_u = second_hop(hop_u, dw_u, yr_u, zr_u)
+    near_g = side_send(dw_g, yr_g, 1)
     gm_in[1].wait_recv()
     gm_in.append(link.remote(gmix.at[row(2, t)], gmix.at[row(3, t)], group[1]))
     gm_core.append(link.remote(gmix.at[row(2, t)], gmix.at[row(2, t)], core))
@@ -928,14 +1031,19 @@
     for i, r in enumerate((1, 2, 3)):
         sc_in[i].wait_recv()
         gm_core.append(link.remote(scal(r, t), scal(r, t), core))
-    near_g = side_send(dw_g, yr_g, 1)
-    far_u = second_hop(hop_u, dw_u, yr_u, zr_u)
+    weight_grad(hid_a, left, dw_d, 2, 2)
+    get_n1 = link.here(n1, left)
+    near_u = side_send(dw_u, yr_u, 1)
+    for c in blk_own:
+        c.wait()
     gm_in[2].wait_recv()
     gm_core.append(link.remote(gmix.at[row(3, t)], gmix.at[row(3, t)], core))
-    near_u = side_send(dw_u, yr_u, 1)
-
+    far_d = second_hop(hop_d, dw_d, yr_d, zr_d)
+    near_d = side_send(dw_d, yr_d, 1)
+    blk_peer = over_cores(blk_core, own_rows, core_blk, own, peer_blk)
+    link.sent(blk_core.values())
     link.sent(two_peer)
-    blk_own = [link.here(p_block.at[row(r, t)], own.at[rel(r)]) for r in (3, 1, 2, 0)]
+    get_aux.append(link.here(w_out_in, w_out))
     for c in get_aux + [get_n1] + gm_here:
         c.wait()
     for c in gm_core:
@@ -980,7 +1088,7 @@
 
     def hand_over(r):
         one_core(r).wait()
-        add_half(r, one_rows, core_in)
+        add_half(r, one_rows, core_in, half)
 
     def piece(i, carry):
         r = 3 - 2 * i + 3 * (i // 2)
@@ -1044,6 +1152,7 @@
     lax.fori_loop(0, 4, piece, 0)
 
     one_core(0).wait()
+    pass_on(blk_peer, own, peer_blk)
 
     weight_grad(grads_t, left, dw_mix, 0, 2)
     hop_mix = side_send(dw_mix, yr_mix, 0)
@@ -1087,8 +1196,8 @@
     lax.fori_loop(0, share // 16, one_on, 0)
     one_z = link.remote(half.at[rel(2)], peer_in.at[rel(2)], group[2])
     near_mix = side_send(dw_mix, yr_mix, 1)
-    back_d = last_hop(near_d, far_d, dw_d, yr_d, zr_d, o_d)
     back_g = last_hop(near_g, far_g, dw_g, yr_g, zr_g, o_g)
+    back_u = last_hop(near_u, far_u, dw_u, yr_u, zr_u, o_u)
     far_mix = second_hop(hop_mix, dw_mix, yr_mix, zr_mix)
 
     @pl.when(t == y)
@@ -1141,11 +1250,8 @@
         if k < len(partners):
             turn.append(link.remote(vec.at[k], vec_in.at[k], partners[k]))
 
-    link.sent([one_z])
-    blk_peer = over_cores(by_piece(blk_core), by_piece(blk_own), own_rows, core_blk, peer_blk)
     next_turn()
-    back_u = last_hop(near_u, far_u, dw_u, yr_u, zr_u, o_u)
-    pass_on(blk_peer, peer_blk)
+    back_d = last_hop(near_d, far_d, dw_d, yr_d, zr_d, o_d)
     next_turn()
     next_turn()
     for c in blk_peer[1:]:
@@ -1199,7 +1305,7 @@
 
 
 def back(*arrays):
-    par, tok = arrays[14], arrays[15]
+    par, tok = arrays[15], arrays[16]
     rows, width = tok.shape
     share, group_rows = rows // 2, 4 * rows
     feat, hid, block = par.shape[1], arrays[0].shape[0], width // 16
@@ -1228,7 +1334,7 @@
         + [
             vm((width, 3 * feat), bf16),
             vm((feat, width), bf16),
-            vm(arrays[13].shape, f32),
+            vm(arrays[14].shape, f32),
             vm((rows, 3 * feat), f32),
             vm((rows, feat), f32),
             vm((rows, feat), bf16),
@@ -1257,7 +1363,7 @@
     vmem_spec = pl.BlockSpec(memory_space=pltpu.VMEM)
     return pl.pallas_call(
         back_kernel,
-        in_specs=[any_spec] * 14 + [vmem_spec] * 6,
+        in_specs=[any_spec] * 15 + [vmem_spec] * 6,
         out_specs=[any_spec] * len(outs),
         out_shape=outs,
         scratch_shapes=scratch,
@@ -1401,7 +1507,8 @@
         gains = jnp.stack([norm_gain, mixer_gain, ffn_gain])
         (
             mix_full, out_full, gate_full, up_full, down_full, normed_one, grad_out_all, normed_two,
-            pre, state, mix_raw, residual, mixed_out, scale_lanes, aux_rows, par,
+            pre, state, mix_raw, residual, mixed_out, scale_lanes, aux_rows, par, gate_pre, up_pre,
+            coef,
         ) = front(
             input_proj, forget_proj, outgate_proj, output_proj, glu_gate, glu_up, glu_down, cotangent,
             tokens_in, gains, bound_table, jnp.concatenate([lengths, bucket]),
@@ -1455,25 +1562,18 @@
         normed_two = jnp.stack(tp_gather(normed_two_half)).reshape(n_tp * rows, width)
 
     if n_dp == 16 and n_t == 2:
-        gate_pre = cross_cols(gate_full, normed_two)
-        up_pre = cross_cols(up_full, normed_two)
         grad_hidden = cross_cols(down_full, grad_out_all)
         gate_act = jax.nn.silu(gate_pre)
         hidden = (gate_act * up_pre).astype(bf16)
         grad_up = (grad_hidden * gate_act).astype(bf16)
         grad_gate = (grad_hidden * up_pre * silu_slope(gate_pre)).astype(bf16)
-        two_parts = (cross_rows(grad_gate, gate_full) + cross_rows(grad_up, up_full)).astype(bf16)
-        block_parts = cross_rows(hidden, down_full).astype(bf16)
         grad_g, grad_u, grad_d, grad_mix_w, grad_out_w, grad_tokens, block_out, vec = back(
-            hidden, grad_gate, grad_up, normed_two, grad_out_all, two_parts, block_parts, normed_one,
-            mix_full, out_full, pre, state, mix_raw, aux_rows, par, tokens_in, residual, mixed_out,
+            hidden, grad_gate, grad_up, normed_two, grad_out_all, gate_full, up_full, down_full,
+            normed_one, mix_full, out_full, pre, state, mix_raw, aux_rows, par, tokens_in, residual, mixed_out,
             scale_lanes, gains,
         )
         mix_all = grad_mix_w.reshape(3, width, block)
         mine = lambda k: lax.dynamic_slice_in_dim(vec, k * n_dp + me, 1, 0)
-        shares, picked, lower = bound_parts(
-            lax.dynamic_slice_in_dim(bound_table, me * block, block, 1)
-        )
         return (
             block_out,
             grad_tokens,
@@ -1487,7 +1587,7 @@
             mine(0)[0],
             mine(2)[0],
             mine(1)[0],
-            shares * (picked - lower[None, :]) * mine(3),
+            coef * mine(3),
         )
 
     scale_two = rms_scale(residual)

time: 450 us -> 436 us (0.969)
  matrix products: 27.2 us -> 11 us
  Pallas kernels: 393 us -> 400 us
    dot_general x3 -> x0, matrix products: 13.6 us -> none  [cross_rows(): lax.dot_general(first_op, second_op, (((0,), (0,)), ((), ())), preferred_...]
    dot_general x3 -> x1, matrix products: 13.6 us -> 11 us  [cross_cols(): lax.dot_general(first_op, second_op, (((1,), (1,)), ((), ())), preferred_...]
where the time goes in v7:
time: 436 us; the launch traced here: 433 us
  Pallas kernels  400 us (92%)
  local copies, waits for them, and re-layouts  11.6 us (3%)
  matrix products  11 us (3%)
  other arithmetic  9.57 us (2%)
    pallas_call x1, Pallas kernels, back(): pl.pallas_call(back_kernel, in_specs=[any_spec] * 15 + [vmem_spec] * 6, o...  216 us
    pallas_call x1, Pallas kernels, front(): pl.pallas_call(front_kernel, in_specs=[any_spec] * 8 + [vmem_spec] * 3 +...  184 us
    dot_general x1, matrix products, cross_cols(): lax.dot_general(first_op, second_op, (((1,), (1,)), ((), ())), preferred_...  11 us

profile of v7, /device:TPU:0, one launch (start us, length us, event | category | flops | bytes accessed | tf_op | source)
XLA Modules:
  0.0 433.1 jit_solution(17219038835101402988)
XLA Ops:
  0.6 1.4 pad_maximum_fusion.gains
  2.7 1.2 pad_add_fusion.sizes
  3.9 183.9 %front.1 = (bf16[2048,768]{1,0:T(8,128)(2,1)}, bf16[256,2048]{1,0:T(8,128)(2,1)}, bf16[704,2048]{1,0:T(8,128)(2,1)}, bf16[704,2048]{1,0:T(8,128)(2,1)}, bf16[704...) custom-call(bf16[128,2048]{1,0:T(8,128)(2,1)} %s_in.1, ...), custom_call_target="tpu_custom_call" | custom-call | tf_op jit(solution)/shard_map/front/pallas_call | solution.py:744
  187.8 11.0 %multiply_convert_fusion = (bf16[704,1024]{1,0:T(8,128)(2,1)}, bf16[704,1024]{1,0:T(8,128)(2,1)}, bf16[704,1024]{1,0:T(8,128)(2,1)}) fusion(f32[704,1024]{1,0:T(8,128)} %get-tuple-element.40, f32[704,1024]{1,0:T(8,128)} %get-tuple-element.41, bf16[704,2048]{1,0:T(8,128)(2,1)} %get-tuple-element.42.w_d, bf16[1024,2048]{1,0:T(8,128)(2,1)} %get-tuple-element.43.go), kind=kOutput, calls=%fused_computation | convolution fusion | flops 2963603456 | bytes 17170432 | tf_op jit(solution)/shard_map/dot_general | solution.py:44
  198.9 215.6 %back.1 = (bf16[4,704,128]{2,1,0:T(8,128)(2,1)}, bf16[4,704,128]{2,1,0:T(8,128)(2,1)}, bf16[4,704,128]{2,1,0:T(8,128)(2,1)}, bf16[3,2,2,2,2,128,128]{6,5,4,3,2,1...) custom-call(bf16[704,1024]{1,0:T(8,128)(2,1)} %get-tuple-element.69., ...), custom_call_target="tpu_custom_call" | custom-call | tf_op jit(solution)/shard_map/back/pallas_call | solution.py:1364
  414.5 1.2 fusion.4
  415.7 0.0 copy-done.2
  415.7 0.6 broadcast_multiply_fusion
  416.3 2.7 bitcast_convert_fusion
  419.1 1.5 copy.32
  420.6 0.0 copy-done.1
  420.6 0.1 fusion.5
  420.7 0.2 bitcast_convert_fusion.3
  421.0 1.3 copy.29
  422.3 1.3 copy.30
  423.6 0.1 bitcast_convert_fusion.5
  423.7 1.3 copy.28
  425.0 1.2 bitcast_convert_fusion.2
  426.2 0.0 copy-start
  426.2 1.5 copy.31
  427.7 2.1 convert_element_type.75
  429.9 1.9 copy.36
  431.7 0.0 copy-done
  431.7 1.3 copy.37
  (2 shorter events, 0.0 us)
Async XLA Ops:
  198.9 216.9 %copy-start.2 = (f32[24,128]{1,0:T(8,128)S(1)}, f32[24,128]{1,0:T(8,128)}, u32[]{:S(2)}) copy-start(f32[24,128]{1,0:T(8,128)} %get-tuple-element.66) | copy-start | bytes 36868
  416.3 4.3 copy-start.1
  426.2 5.5 %copy-start = (f32[256,2048]{1,0:T(8,128)S(1)}, f32[256,2048]{1,0:T(8,128)}, u32[]{:S(2)}) copy-start(f32[256,2048]{1,0:T(8,128)} %get-tuple-element.95) | copy-start | bytes 6291460

commit v8 on v7

--- a/solution.py
+++ b/solution.py
@@ -286,9 +286,9 @@
 
 
 def front_kernel(
-    s_in, s_fg, s_og, s_out, w_g, w_u, s_d, cot, tok, gains, table, sizes,
-    o_mix, o_out, o_g, o_u, o_d, o_n1, o_go, o_n2, o_pre, o_state, o_raw, o_res, o_mo, o_sc, o_aux, o_par, o_gate, o_up, o_coef,
-    w_mix, w_out, n1, aux, pre, state, raw, part, core_in, half, peer_in, par, wide_g, wide_u, s_g, s_u, go_own, bound_row, full_g, full_u, gate, up, all_powers, coef,
+    s_in, s_fg, s_og, s_out, w_g, w_u, s_d, cot, tok, gain_one, gain_mix, gain_two, table, lengths, bucket,
+    o_mix, o_out, o_g, o_u, o_d, o_n1, o_go, o_n2, o_pre, o_state, o_raw, o_res, o_mo, o_sc, o_aux, o_par, o_hid, o_hg, o_hu, o_coef,
+    w_mix, w_out, n1, aux, pre, state, raw, part, core_in, half, peer_in, par, wide_g, wide_u, s_g, s_u, go_own, bound_row, full_g, full_u, gate, up, hid_v, hid_g, hid_u, all_powers, coef,
     sq, sq_core, sq_half, sq_peer, res, mo, sc, n2, decay, add,
     send, recv, local, core_send, core_recv, sqc_send, sqc_recv, out_send, out_recv, x_send, x_recv,
 ):
@@ -347,7 +347,7 @@
         out_side.start()
         out_here.start()
 
-    norm_row = gains[0:1, :]
+    norm_row = gain_one[...]
 
     def norm_rows(first):
         def some(j, carry):
@@ -362,15 +362,15 @@
     norm_rows(t * share)
     n1_in = [link.remote(n1.at[row(0, t)], n1.at[row(r, t)], group[r]) for r in (1, 2)]
 
-    count = sizes.shape[0] - 1
-    slot_len = lax.shift_right_logical(jnp.int32(rows), sizes[count])
+    count = lengths.shape[0]
+    slot_len = lax.shift_right_logical(jnp.int32(rows), bucket[0])
     position_row = lax.broadcasted_iota(jnp.int32, (1, rows), 1)
     slot = jnp.zeros((1, rows), jnp.int32)
     for j in range(1, count):
         slot = slot + (position_row >= j * slot_len).astype(jnp.int32)
     limit = jnp.zeros((1, rows), jnp.int32)
     for j in range(count):
-        limit = limit + jnp.where(slot == j, sizes[j], 0)
+        limit = limit + jnp.where(slot == j, lengths[j], 0)
     offset = position_row - slot * slot_len
     aux[0] = jnp.zeros(aux.shape[1:], f32)
     aux[0, 0:1, :] = (offset < limit).astype(f32)
@@ -429,7 +429,7 @@
     link.here(coef, o_coef, keep=True)
     for fz in (0, 1):
         par[0:1, fz * block : (fz + 1) * block] = bound_row[0:1, columns(0, fz)]
-        par[1:2, fz * block : (fz + 1) * block] = gains[1:2, columns(0, fz)]
+        par[1:2, fz * block : (fz + 1) * block] = gain_mix[0:1, columns(0, fz)]
     get_cot.wait()
     valid_rows = aux[0].T[:, 0:1]
     first_half = lax.broadcasted_iota(jnp.int32, (share, 1), 0) * 0 + t
@@ -474,7 +474,7 @@
     start_ffn(0)
     go_in = [link.remote(go_own, o_go.at[row(r, t)], group[r]) for r in (1, 2)]
     go_core = [link.remote(go_own, o_go.at[row(0, t)], core)]
-    link.here(go_own, o_go.at[row(0, t)], keep=True)
+    go_here = link.here(go_own, o_go.at[row(0, t)])
 
     for c in side_mix + n1_core + aux_in:
         c.wait_recv()
@@ -566,7 +566,7 @@
 
     link.here(w_mix, o_mix, keep=True)
     link.here(w_out, o_out, keep=True)
-    link.here(n1, o_n1, keep=True)
+    n1_out = link.here(n1, o_n1)
     link.here(pre, o_pre, keep=True)
     link.here(state, o_state, keep=True)
     link.here(raw, o_raw, keep=True)
@@ -621,7 +621,7 @@
         mo[to, :] = mixed
         res[to, :] = value
         scale_two = lax.rsqrt(jnp.mean(value * value, axis=1, keepdims=True) + epsilon)
-        n2[to, :] = (value * scale_two * gains[2:3, :]).astype(bf16)
+        n2[to, :] = (value * scale_two * gain_two[...]).astype(bf16)
         return carry
 
     lax.fori_loop(0, share // chunk, finish, 0)
@@ -660,19 +660,43 @@
         lax.fori_loop(0, 4, some, 0)
 
     product(full_g, gate)
-    link.here(gate, o_gate, keep=True)
     for c in side_ffn[1]:
         c.wait_recv()
     get_full = link.here(o_u, full_u)
     get_full.wait()
+    for c in go_core:
+        c.wait_recv()
+    go_here.wait()
+    n1_out.wait()
+    link.sent(n1_in + n1_core)
+    get_rows = link.here(o_go, n1)
     product(full_u, up)
-    link.here(up, o_up, keep=True)
-    for c in side_ffn[2] + go_core:
+    for c in side_ffn[2]:
         c.wait_recv()
+    get_full = link.here(o_d, full_g)
+    get_full.wait()
+    get_rows.wait()
+
+    def hidden_rows(j, carry):
+        to = at(j * rows, rows, rows)
+        grad = lax.dot_general(
+            full_g[...], n1[to, :], (((1,), (1,)), ((), ())), preferred_element_type=f32
+        )
+        value, other = gate[:, to], up[:, to]
+        sig = jax.nn.sigmoid(value)
+        act = value * sig
+        hid_v[:, to] = (act * other).astype(bf16)
+        hid_u[:, to] = (grad * act).astype(bf16)
+        hid_g[:, to] = (grad * other * (sig * (1.0 + value * (1.0 - sig)))).astype(bf16)
+        return carry
+
+    lax.fori_loop(0, 4, hidden_rows, 0)
+    for made, out in ((hid_v, o_hid), (hid_g, o_hg), (hid_u, o_hu)):
+        link.here(made, out, keep=True)
     link.close()
 
 
-def front(s_in, s_fg, s_og, s_out, w_g, w_u, s_d, cot, tok, gains, table, sizes):
+def front(s_in, s_fg, s_og, s_out, w_g, w_u, s_d, cot, tok, gain_one, gain_mix, gain_two, table, lengths, bucket):
     rows, width = tok.shape
     share, group_rows = rows // 2, 4 * rows
     block = s_out.shape[0]
@@ -698,8 +722,9 @@
         made((share, 128), f32),
         made((4, 8, rows), f32),
         made((2, feat), f32),
-        made((hid, group_rows), f32),
-        made((hid, group_rows), f32),
+        made((hid, group_rows), bf16),
+        made((hid, group_rows), bf16),
+        made((hid, group_rows), bf16),
         made((table.shape[0], block), f32),
     ]
     scratch = [
@@ -725,6 +750,9 @@
         pltpu.VMEM((hid, width), bf16),
         pltpu.VMEM((hid, group_rows), f32),
         pltpu.VMEM((hid, group_rows), f32),
+        pltpu.VMEM((hid, group_rows), bf16),
+        pltpu.VMEM((hid, group_rows), bf16),
+        pltpu.VMEM((hid, group_rows), bf16),
         pltpu.VMEM(table.shape, f32),
         pltpu.VMEM((table.shape[0], block), f32),
         pltpu.VMEM((group_rows, lanes), f32),
@@ -739,11 +767,11 @@
         pltpu.VMEM((rows, feat), f32),
         pltpu.SemaphoreType.DMA((88,)),
         pltpu.SemaphoreType.DMA((88,)),
-        pltpu.SemaphoreType.DMA((32,)),
+        pltpu.SemaphoreType.DMA((40,)),
     ] + [pltpu.SemaphoreType.DMA((4,))] * 8
     return pl.pallas_call(
         front_kernel,
-        in_specs=[any_spec] * 8 + [vmem_spec] * 3 + [pl.BlockSpec(memory_space=pltpu.SMEM)],
+        in_specs=[any_spec] * 8 + [vmem_spec] * 5 + [pl.BlockSpec(memory_space=pltpu.SMEM)] * 2,
         out_specs=[any_spec] * len(outs),
         out_shape=outs,
         scratch_shapes=scratch,
@@ -751,12 +779,12 @@
             collective_id=1, has_side_effects=True, vmem_limit_bytes=56 << 20
         ),
         name="front",
-    )(s_in, s_fg, s_og, s_out, w_g, w_u, s_d, cot, tok, gains, table, sizes)
+    )(s_in, s_fg, s_og, s_out, w_g, w_u, s_d, cot, tok, gain_one, gain_mix, gain_two, table, lengths, bucket)
 
 
 def back_kernel(
     h_d, h_g, h_u, n2, go, w_g, w_u, w_d, n1, w_mix_in, w_out_in, pre, state, raw, aux_in,
-    par, tok, res, mo, sc, gains,
+    par, tok, res, mo, sc, first_gain, second_gain,
     o_g, o_u, o_d, o_mix, o_out, o_tok, o_blk, o_vec,
     left, right, gmix, dw_d, dw_g, dw_u, dw_mix, yr_d, yr_g, yr_u, yr_mix, zr_d, zr_g, zr_u, zr_mix,
     own, half, core_in, core_blk, peer_in, peer_blk, w_mix, w_out, aux, pre_b, state_b, raw_b,
@@ -978,7 +1006,7 @@
         c.wait_recv()
     for c in get_go:
         c.wait()
-    gain_two = gains[2:3, :]
+    gain_two = second_gain[...]
     sums[...] = jnp.zeros_like(sums)
     step = 16
 
@@ -1208,7 +1236,7 @@
 
     one_x(1, 1).wait()
     one_z.wait_recv()
-    gain_one = gains[0:1, :]
+    gain_one = first_gain[...]
 
     def token_rows(j, carry):
         to = at(j * step, step, step)
@@ -1363,7 +1391,7 @@
     vmem_spec = pl.BlockSpec(memory_space=pltpu.VMEM)
     return pl.pallas_call(
         back_kernel,
-        in_specs=[any_spec] * 15 + [vmem_spec] * 6,
+        in_specs=[any_spec] * 15 + [vmem_spec] * 7,
         out_specs=[any_spec] * len(outs),
         out_shape=outs,
         scratch_shapes=scratch,
@@ -1504,14 +1532,13 @@
 
     hid = glu_gate.shape[1] // n_tp
     if n_dp == 16 and n_t == 2:
-        gains = jnp.stack([norm_gain, mixer_gain, ffn_gain])
         (
             mix_full, out_full, gate_full, up_full, down_full, normed_one, grad_out_all, normed_two,
-            pre, state, mix_raw, residual, mixed_out, scale_lanes, aux_rows, par, gate_pre, up_pre,
-            coef,
+            pre, state, mix_raw, residual, mixed_out, scale_lanes, aux_rows, par, hidden, grad_gate,
+            grad_up, coef,
         ) = front(
             input_proj, forget_proj, outgate_proj, output_proj, glu_gate, glu_up, glu_down, cotangent,
-            tokens_in, gains, bound_table, jnp.concatenate([lengths, bucket]),
+            tokens_in, norm_gain[None, :], mixer_gain[None, :], ffn_gain[None, :], bound_table, lengths, bucket,
         )
     else:
         inputs = tokens_in.astype(f32)
@@ -1562,15 +1589,10 @@
         normed_two = jnp.stack(tp_gather(normed_two_half)).reshape(n_tp * rows, width)
 
     if n_dp == 16 and n_t == 2:
-        grad_hidden = cross_cols(down_full, grad_out_all)
-        gate_act = jax.nn.silu(gate_pre)
-        hidden = (gate_act * up_pre).astype(bf16)
-        grad_up = (grad_hidden * gate_act).astype(bf16)
-        grad_gate = (grad_hidden * up_pre * silu_slope(gate_pre)).astype(bf16)
         grad_g, grad_u, grad_d, grad_mix_w, grad_out_w, grad_tokens, block_out, vec = back(
             hidden, grad_gate, grad_up, normed_two, grad_out_all, gate_full, up_full, down_full,
             normed_one, mix_full, out_full, pre, state, mix_raw, aux_rows, par, tokens_in, residual, mixed_out,
-            scale_lanes, gains,
+            scale_lanes, norm_gain[None, :], ffn_gain[None, :],
         )
         mix_all = grad_mix_w.reshape(3, width, block)
         mine = lambda k: lax.dynamic_slice_in_dim(vec, k * n_dp + me, 1, 0)

time: 436 us -> 428 us (0.982)
  matrix products: 11 us -> 0 us
  Pallas kernels: 400 us -> 407 us
  other arithmetic: 9.57 us -> 4.73 us
    dot_general x1 -> x0, matrix products: 11 us -> none  [cross_cols(): lax.dot_general(first_op, second_op, (((1,), (1,)), ((), ())), preferred_...]
    pallas_call x2, Pallas kernels: 400 us -> 407 us  [the longest x1 217 us: back(): pl.pallas_call(back_kernel, in_specs=[any_spec] * 15 + [vmem_spec] * 7, o...]
where the time goes in v8:
time: 428 us; the launch traced here: 424 us
  Pallas kernels  407 us (95%)
  local copies, waits for them, and re-layouts  10.6 us (2%)
  other arithmetic  4.73 us (1%)
    pallas_call x1, Pallas kernels, back(): pl.pallas_call(back_kernel, in_specs=[any_spec] * 15 + [vmem_spec] * 7, o...  217 us
    pallas_call x1, Pallas kernels, front(): pl.pallas_call(front_kernel, in_specs=[any_spec] * 8 + [vmem_spec] * 5 +...  190 us

profile of v8, /device:TPU:0, one launch (start us, length us, event | category | flops | bytes accessed | tf_op | source)
XLA Modules:
  0.0 423.9 jit_solution(13824437989782480652)
XLA Ops:
  1.3 189.8 %front.1 = (bf16[2048,768]{1,0:T(8,128)(2,1)}, bf16[256,2048]{1,0:T(8,128)(2,1)}, bf16[704,2048]{1,0:T(8,128)(2,1)}, bf16[704,2048]{1,0:T(8,128)(2,1)}, bf16[704...) custom-call(bf16[128,2048]{1,0:T(8,128)(2,1)} %s_in.1, ...), custom_call_target="tpu_custom_call" | custom-call | tf_op jit(solution)/shard_map/front/pallas_call | solution.py:772
  191.1 0.0 copy-start.5
  191.1 217.5 %back.1 = (bf16[4,704,128]{2,1,0:T(8,128)(2,1)}, bf16[4,704,128]{2,1,0:T(8,128)(2,1)}, bf16[4,704,128]{2,1,0:T(8,128)(2,1)}, bf16[3,2,2,2,2,128,128]{6,5,4,3,2,1...) custom-call(bf16[704,1024]{1,0:T(8,128)(2,1)} %get-tuple-element.41., ...), custom_call_target="tpu_custom_call" | custom-call | tf_op jit(solution)/shard_map/back/pallas_call | solution.py:1392
  408.6 1.2 fusion.3
  409.8 0.0 copy-done.5
  409.8 0.6 broadcast_multiply_fusion
  410.4 2.6 bitcast_convert_fusion
  413.0 1.5 copy.32
  414.6 0.0 copy-done.1
  414.6 0.1 fusion.4
  414.7 0.2 bitcast_convert_fusion.3
  414.9 1.3 copy.29
  416.2 1.3 copy.30
  417.5 0.1 bitcast_convert_fusion.5
  417.6 1.3 copy.28
  418.9 0.0 copy-done.2
  418.9 0.1 bitcast_convert_fusion.2
  419.1 0.0 copy-start.3
  419.1 0.0 copy-start.4
  419.1 1.5 copy.31
  420.6 1.1 convert_element_type.63
  421.7 0.8 copy.36
  422.5 0.1 copy-done
  422.6 1.3 copy.37
  (5 shorter events, 0.0 us)
Async XLA Ops:
  191.1 218.7 %copy-start.5 = (f32[24,128]{1,0:T(8,128)S(1)}, f32[24,128]{1,0:T(8,128)}, u32[]{:S(2)}) copy-start(f32[24,128]{1,0:T(8,128)} %get-tuple-element.68) | copy-start | bytes 36868
  413.0 1.5 copy-start.1
  417.5 1.4 copy-start.2
  419.1 1.6 copy-start.3
  419.1 2.6 copy-start.4
  420.6 2.0 copy-start

commit v9 on v8

--- a/solution.py
+++ b/solution.py
@@ -288,7 +288,7 @@
 def front_kernel(
     s_in, s_fg, s_og, s_out, w_g, w_u, s_d, cot, tok, gain_one, gain_mix, gain_two, table, lengths, bucket,
     o_mix, o_out, o_g, o_u, o_d, o_n1, o_go, o_n2, o_pre, o_state, o_raw, o_res, o_mo, o_sc, o_aux, o_par, o_hid, o_hg, o_hu, o_coef,
-    w_mix, w_out, n1, aux, pre, state, raw, part, core_in, half, peer_in, par, wide_g, wide_u, s_g, s_u, go_own, bound_row, full_g, full_u, gate, up, hid_v, hid_g, hid_u, all_powers, coef,
+    w_mix, w_out, n1, aux, pre, state, raw, part, core_in, half, peer_in, par, wide_g, wide_u, s_g, s_u, go_own, bound_row, full_g, full_u, gate, up, into, hid_v, hid_g, hid_u, all_powers, coef,
     sq, sq_core, sq_half, sq_peer, res, mo, sc, n2, decay, add,
     send, recv, local, core_send, core_recv, sqc_send, sqc_recv, out_send, out_recv, x_send, x_recv,
 ):
@@ -670,18 +670,39 @@
     n1_out.wait()
     link.sent(n1_in + n1_core)
     get_rows = link.here(o_go, n1)
+    for c in side_ffn[2][:2]:
+        c.wait_recv()
+    early = [pair(fz, c, fy) for fz, fy in ((zf, y), (zf, 1 - y), (1 - zf, y)) for c in (0, 1)]
+    get_early = [link.here(o_d.at[:, cols], full_g.at[:, cols]) for cols in early]
     product(full_u, up)
-    for c in side_ffn[2]:
+    for c in get_early + [get_rows]:
+        c.wait()
+
+    def contribution(cols, to):
+        return lax.dot_general(
+            full_g[:, cols], n1[to, cols], (((1,), (1,)), ((), ())), preferred_element_type=f32
+        )
+
+    def early_rows(j, carry):
+        to = at(j * rows, rows, rows)
+        total = contribution(early[0], to)
+        for cols in early[1:]:
+            total = total + contribution(cols, to)
+        into[:, to] = total
+        return carry
+
+    lax.fori_loop(0, 4, early_rows, 0)
+    late = [pair(1 - zf, c, 1 - y) for c in (0, 1)]
+    get_late = []
+    for c, cols in zip(side_ffn[2][2:], late):
         c.wait_recv()
-    get_full = link.here(o_d, full_g)
-    get_full.wait()
-    get_rows.wait()
+        get_late.append(link.here(o_d.at[:, cols], full_g.at[:, cols]))
+    for c in get_late:
+        c.wait()
 
     def hidden_rows(j, carry):
         to = at(j * rows, rows, rows)
-        grad = lax.dot_general(
-            full_g[...], n1[to, :], (((1,), (1,)), ((), ())), preferred_element_type=f32
-        )
+        grad = into[:, to] + contribution(late[0], to) + contribution(late[1], to)
         value, other = gate[:, to], up[:, to]
         sig = jax.nn.sigmoid(value)
         act = value * sig
@@ -750,6 +771,7 @@
         pltpu.VMEM((hid, width), bf16),
         pltpu.VMEM((hid, group_rows), f32),
         pltpu.VMEM((hid, group_rows), f32),
+        pltpu.VMEM((hid, group_rows), f32),
         pltpu.VMEM((hid, group_rows), bf16),
         pltpu.VMEM((hid, group_rows), bf16),
         pltpu.VMEM((hid, group_rows), bf16),
@@ -767,7 +789,7 @@
         pltpu.VMEM((rows, feat), f32),
         pltpu.SemaphoreType.DMA((88,)),
         pltpu.SemaphoreType.DMA((88,)),
-        pltpu.SemaphoreType.DMA((40,)),
+        pltpu.SemaphoreType.DMA((48,)),
     ] + [pltpu.SemaphoreType.DMA((4,))] * 8
     return pl.pallas_call(
         front_kernel,
@@ -776,7 +798,7 @@
         out_shape=outs,
         scratch_shapes=scratch,
         compiler_params=pltpu.CompilerParams(
-            collective_id=1, has_side_effects=True, vmem_limit_bytes=56 << 20
+            collective_id=1, has_side_effects=True, vmem_limit_bytes=60 << 20
         ),
         name="front",
     )(s_in, s_fg, s_og, s_out, w_g, w_u, s_d, cot, tok, gain_one, gain_mix, gain_two, table, lengths, bucket)

time: 428 us -> 426 us (level)
  no operation moved by 1% of the time
where the time goes in v9:
time: 426 us; the launch traced here: 425 us
  Pallas kernels  408 us (96%)
  local copies, waits for them, and re-layouts  10.6 us (2%)
  other arithmetic  4.73 us (1%)
    pallas_call x1, Pallas kernels, back(): pl.pallas_call(back_kernel, in_specs=[any_spec] * 15 + [vmem_spec] * 7, o...  218 us
    pallas_call x1, Pallas kernels, front(): pl.pallas_call(front_kernel, in_specs=[any_spec] * 8 + [vmem_spec] * 5 +...  190 us

profile of v9, /device:TPU:0, one launch (start us, length us, event | category | flops | bytes accessed | tf_op | source)
XLA Modules:
  0.0 424.7 jit_solution(8322136972317279375)
XLA Ops:
  1.3 190.0 %front.1 = (bf16[2048,768]{1,0:T(8,128)(2,1)}, bf16[256,2048]{1,0:T(8,128)(2,1)}, bf16[704,2048]{1,0:T(8,128)(2,1)}, bf16[704,2048]{1,0:T(8,128)(2,1)}, bf16[704...) custom-call(bf16[128,2048]{1,0:T(8,128)(2,1)} %s_in.1, ...), custom_call_target="tpu_custom_call" | custom-call | tf_op jit(solution)/shard_map/front/pallas_call | solution.py:794
  191.3 0.0 copy-start.5
  191.3 218.0 %back.1 = (bf16[4,704,128]{2,1,0:T(8,128)(2,1)}, bf16[4,704,128]{2,1,0:T(8,128)(2,1)}, bf16[4,704,128]{2,1,0:T(8,128)(2,1)}, bf16[3,2,2,2,2,128,128]{6,5,4,3,2,1...) custom-call(bf16[704,1024]{1,0:T(8,128)(2,1)} %get-tuple-element.41., ...), custom_call_target="tpu_custom_call" | custom-call | tf_op jit(solution)/shard_map/back/pallas_call | solution.py:1414
  409.3 1.2 fusion.3
  410.5 0.0 copy-done.5
  410.5 0.6 broadcast_multiply_fusion
  411.1 2.6 bitcast_convert_fusion
  413.8 1.5 copy.32
  415.3 0.0 copy-done.1
  415.3 0.1 fusion.4
  415.4 0.2 bitcast_convert_fusion.3
  415.6 1.3 copy.29
  416.9 1.3 copy.30
  418.3 0.1 bitcast_convert_fusion.5
  418.4 1.3 copy.28
  419.7 0.0 copy-done.2
  419.7 0.1 bitcast_convert_fusion.2
  419.8 0.0 copy-start.3
  419.8 0.0 copy-start.4
  419.8 1.5 copy.31
  421.4 1.1 convert_element_type.63
  422.5 0.8 copy.36
  423.2 0.1 copy-done
  423.3 1.3 copy.37
  (5 shorter events, 0.0 us)
Async XLA Ops:
  191.3 219.2 %copy-start.5 = (f32[24,128]{1,0:T(8,128)S(1)}, f32[24,128]{1,0:T(8,128)}, u32[]{:S(2)}) copy-start(f32[24,128]{1,0:T(8,128)} %get-tuple-element.68) | copy-start | bytes 36868
  413.8 1.5 copy-start.1
  418.3 1.4 copy-start.2
  419.8 1.6 copy-start.3
  419.8 2.6 copy-start.4
  421.4 2.0 copy-start

commit v10 on v9

--- a/solution.py
+++ b/solution.py
@@ -946,12 +946,20 @@
     def cut(ref, cols):
         return ref.at[:, cols] if len(ref.shape) == 2 else ref.at[:, :, :, cols]
 
+    def side_part(dw, yr, slot, c):
+        fz = 1 - zf if slot == 0 else zf
+        to = cut(yr, pl.ds((slot * 2 + c) * 2 * block, 2 * block))
+        return link.remote(cut(dw, pair(fz, c, 1 - y)), to, side)
+
     def side_send(dw, yr, slot):
-        fz = 1 - zf if slot == 0 else zf
-        return [
-            link.remote(cut(dw, pair(fz, c, 1 - y)), cut(yr, pl.ds((slot * 2 + c) * 2 * block, 2 * block)), side)
-            for c in (0, 1)
-        ]
+        return [side_part(dw, yr, slot, c) for c in (0, 1)]
+
+    def far_half(hid, other, dw, yr):
+        sent = []
+        for c in (0, 1):
+            weight_grad(hid, other, dw, c, 1)
+            sent.append(side_part(dw, yr, 0, c))
+        return sent
 
     def add_columns(dw, to, others):
         if len(dw.shape) == 2:
@@ -1007,8 +1015,7 @@
 
     for c in get_g:
         c.wait()
-    weight_grad(hid_a, right, dw_g, 0, 2)
-    hop_g = side_send(dw_g, yr_g, 0)
+    hop_g = far_half(hid_a, right, dw_g, yr_g)
     get_u.wait()
     for c in get_two:
         c.wait()
@@ -1204,8 +1211,7 @@
     one_core(0).wait()
     pass_on(blk_peer, own, peer_blk)
 
-    weight_grad(grads_t, left, dw_mix, 0, 2)
-    hop_mix = side_send(dw_mix, yr_mix, 0)
+    hop_mix = far_half(grads_t, left, dw_mix, yr_mix)
     weight_grad(grads_t, left, dw_mix, 2, 2)
 
     def out_columns(i, carry):
@@ -1418,7 +1424,7 @@
         out_shape=outs,
         scratch_shapes=scratch,
         compiler_params=pltpu.CompilerParams(
-            collective_id=2, has_side_effects=True, vmem_limit_bytes=63 << 20
+            collective_id=2, has_side_effects=True, vmem_limit_bytes=127 << 19
         ),
         name="back",
     )(*arrays)

time: 426 us -> 426 us (level)
  no operation moved by 1% of the time
where the time goes in v10:
time: 426 us; the launch traced here: 424 us
  Pallas kernels  408 us (96%)
  local copies, waits for them, and re-layouts  10.6 us (2%)
  other arithmetic  4.73 us (1%)
    pallas_call x1, Pallas kernels, back(): pl.pallas_call(back_kernel, in_specs=[any_spec] * 15 + [vmem_spec] * 7, o...  218 us
    pallas_call x1, Pallas kernels, front(): pl.pallas_call(front_kernel, in_specs=[any_spec] * 8 + [vmem_spec] * 5 +...  190 us

profile of v10, /device:TPU:0, one launch (start us, length us, event | category | flops | bytes accessed | tf_op | source)
XLA Modules:
  0.0 424.4 jit_solution(3537207283519777019)
XLA Ops:
  1.3 190.0 %front.1 = (bf16[2048,768]{1,0:T(8,128)(2,1)}, bf16[256,2048]{1,0:T(8,128)(2,1)}, bf16[704,2048]{1,0:T(8,128)(2,1)}, bf16[704,2048]{1,0:T(8,128)(2,1)}, bf16[704...) custom-call(bf16[128,2048]{1,0:T(8,128)(2,1)} %s_in.1, ...), custom_call_target="tpu_custom_call" | custom-call | tf_op jit(solution)/shard_map/front/pallas_call | solution.py:794
  191.3 0.0 copy-start.5
  191.3 217.7 %back.1 = (bf16[4,704,128]{2,1,0:T(8,128)(2,1)}, bf16[4,704,128]{2,1,0:T(8,128)(2,1)}, bf16[4,704,128]{2,1,0:T(8,128)(2,1)}, bf16[3,2,2,2,2,128,128]{6,5,4,3,2,1...) custom-call(bf16[704,1024]{1,0:T(8,128)(2,1)} %get-tuple-element.41., ...), custom_call_target="tpu_custom_call" | custom-call | tf_op jit(solution)/shard_map/back/pallas_call | solution.py:1420
  409.0 1.2 fusion.3
  410.2 0.0 copy-done.5
  410.2 0.6 broadcast_multiply_fusion
  410.8 2.6 bitcast_convert_fusion
  413.4 1.5 copy.32
  415.0 0.0 copy-done.1
  415.0 0.1 fusion.4
  415.1 0.2 bitcast_convert_fusion.3
  415.3 1.3 copy.29
  416.6 1.3 copy.30
  417.9 0.1 bitcast_convert_fusion.5
  418.0 1.3 copy.28
  419.4 0.0 copy-done.2
  419.4 0.1 bitcast_convert_fusion.2
  419.5 0.0 copy-start.3
  419.5 1.5 copy.31
  421.1 0.0 copy-done.3
  421.1 1.1 convert_element_type.63
  422.1 0.8 copy.36
  422.9 0.1 copy-done
  423.0 1.3 copy.37
  (5 shorter events, 0.0 us)
Async XLA Ops:
  191.3 218.9 %copy-start.5 = (f32[24,128]{1,0:T(8,128)S(1)}, f32[24,128]{1,0:T(8,128)}, u32[]{:S(2)}) copy-start(f32[24,128]{1,0:T(8,128)} %get-tuple-element.68) | copy-start | bytes 36868
  413.4 1.5 copy-start.1
  417.9 1.4 copy-start.2
  419.5 1.6 copy-start.3
  419.5 2.6 copy-start.4
  421.1 2.0 copy-start
